TPU v7x, 32 devices: a whole 2x2x4 slice. The times are simulated.
32 devices in a mesh: rad: 4 (over y, x), azi: 8 (over z, core).
Axes of the slice: x: 2, y: 2, z: 4, core: 2. Of those that a mesh axis runs over, the one named last changes fastest.
Arguments:
- blocks: float32 [512, 8, 4096], P(('rad', 'azi')), may hold values from -8 to 8
- assignment: int32 [512], replicated, may hold values from 0 to 511, as said below
- levels: int32 [512], P(('rad', 'azi')), may hold values from 0 to 2
- coupling: float32 [3, 8, 8], replicated, may hold values from -2 to 2
- damping: float32 [8], replicated, may hold values from 0.5 to 5
Outputs:
- new_blocks: float32 [512, 8, 4096], P(('rad', 'azi'))
- tendency: float32 [512, 8, 4096], P(('rad', 'azi'))
Inputs may be any that keep to these rules, and one draw needn't show every extreme that they name: A permutation. The slot assignment[i] lies on a device (slot // 16, devices ordered rad then azi) with the same rad index as the device that holds block i now. From one device to one device (itself included) go at most 2 blocks, and every device sends exactly 2 blocks to some one device.
All inputs are finite; a program needn't handle non-finite values.
Results may differ from a plain program's by a relative error of at most 0.0003.
Values sent between devices are 32-bit elements; how exact they have to be, the bound alone decides.
No kernel may reach another device: no remote copies, remote signals or barrier semaphores. Data moves between devices by JAX's collectives and lax.ppermute only.
A program may use at most 128 MiB of HBM per device.

v0:
```python
import jax
import jax.numpy as jnp
from jax import lax
from jax.sharding import PartitionSpec as P

EDGE = 16
CHANNELS = 8


time_step = 0.02
signal_speed = 2.0
shear_rate = -1.5


def extended(cells, sides, width, closed):
    for axis, dim in sides:
        count = lax.axis_size(axis)
        ends = count if closed else count - 1
        head = lax.slice_in_dim(cells, 0, width, axis=dim)
        tail = lax.slice_in_dim(cells, cells.shape[dim] - width, cells.shape[dim], axis=dim)
        cells = jnp.concatenate(
            [
                lax.ppermute(tail, axis, [(i, (i + 1) % count) for i in range(ends)]),
                cells,
                lax.ppermute(head, axis, [((i + 1) % count, i) for i in range(ends)]),
            ],
            axis=dim,
        )
    return cells


def limited(lower, upper):
    return jnp.where(
        lower * upper > 0.0, jnp.sign(lower) * jnp.minimum(jnp.abs(lower), jnp.abs(upper)), 0.0
    )


def window(array, offset, length, along):
    return lax.slice_in_dim(array, offset, offset + length, axis=along)


def flux_change(padded, along, velocity, signal, matrix):
    inner = padded.shape[along] - 4
    differences = window(padded, 1, inner + 3, along) - window(padded, 0, inner + 3, along)
    slopes = limited(
        window(differences, 0, inner + 2, along), window(differences, 1, inner + 2, along)
    )
    left_state = window(padded, 1, inner + 1, along) + 0.5 * window(slopes, 0, inner + 1, along)
    right_state = window(padded, 2, inner + 1, along) - 0.5 * window(slopes, 1, inner + 1, along)
    summed = left_state + right_state
    mixed_flux = jnp.einsum("ce,e...->c...", matrix, summed, precision=lax.Precision.HIGHEST)
    face_values = 0.5 * mixed_flux - 0.5 * signal * (right_state - left_state)
    if velocity is not None:
        face_values = face_values + 0.5 * velocity * summed
    return window(face_values, 1, inner, along) - window(face_values, 0, inner, along)


def increment(
    state_field, padded_rad, padded_azi, column_mean, step_ratio, shear_speed, coupling, damping
):
    padded_vert = jnp.concatenate(
        [state_field[..., -2:], state_field, state_field[..., :2]], axis=3
    )
    velocity = (shear_speed[:, None] + column_mean[2])[:, None, :]
    signal = jnp.abs(velocity) + signal_speed
    total_change = flux_change(padded_rad, 1, None, signal_speed, coupling[0])
    total_change = total_change + flux_change(padded_azi, 2, velocity, signal, coupling[1])
    total_change = total_change + flux_change(padded_vert, 3, None, signal_speed, coupling[2])
    relax = time_step * damping[:, None, None, None] * (state_field - column_mean[:, :, None, :])
    return -step_ratio * total_change - relax


def on_device(blocks, assignment, levels, coupling, damping):
    azi_count = lax.axis_size("azi")
    rad_count = lax.axis_size("rad")
    azi_index = lax.axis_index("azi")
    rad_index = lax.axis_index("rad")
    block_count = blocks.shape[0]
    row_start = rad_index * (azi_count * block_count)
    own_device = rad_index * azi_count + azi_index
    arrived = lax.all_gather(blocks, "azi", axis=0, tiled=True)
    slots_here = lax.dynamic_slice_in_dim(assignment, row_start, arrived.shape[0])
    owned_here = slots_here // block_count == own_device
    target = jnp.where(owned_here, slots_here % block_count, block_count)
    state_blocks = jnp.zeros_like(blocks).at[target].set(arrived, mode="drop")
    start_field = state_blocks.reshape(block_count, CHANNELS, EDGE, EDGE, EDGE)
    start_field = start_field.transpose(1, 2, 3, 0, 4).reshape(
        CHANNELS, EDGE, EDGE, block_count * EDGE
    )
    factor = (
        jnp.where(levels == 0, 1.0, jnp.where(levels == 1, 2.0, 4.0)).astype(jnp.float32)
        * time_step
    )
    step_ratio = jnp.repeat(factor, EDGE)
    global_rad = (rad_index * EDGE + jnp.arange(EDGE)).astype(jnp.float32)
    shear_speed = shear_rate * ((global_rad + 0.5) * (2.0 / (EDGE * rad_count)) - 1.0)
    azi_cells = EDGE * azi_count

    def sum_columns(state_field):
        return lax.psum(jnp.sum(state_field, axis=2), "azi") / azi_cells

    def advance(state_field, column_mean):
        padded_rad = extended(state_field, (("rad", 1),), 2, False)
        padded_azi = extended(state_field, (("azi", 2),), 2, True)
        return increment(
            state_field,
            padded_rad,
            padded_azi,
            column_mean,
            step_ratio,
            shear_speed,
            coupling,
            damping,
        )

    first_mean = sum_columns(start_field)
    first_state = start_field + advance(start_field, first_mean)
    final_state = 0.5 * start_field + 0.5 * (
        first_state + advance(first_state, sum_columns(first_state))
    )
    tendency_field = (final_state - start_field) / time_step

    def to_blocks(state_field):
        split_field = state_field.reshape(CHANNELS, EDGE, EDGE, block_count, EDGE)
        return split_field.transpose(3, 0, 1, 2, 4).reshape(
            block_count, CHANNELS, EDGE * EDGE * EDGE
        )

    return (to_blocks(final_state), to_blocks(tendency_field))


def solution(mesh):
    in_specs = (P(("rad", "azi"), None, None), P(), P(("rad", "azi")), P(), P())
    out_specs = (P(("rad", "azi"), None, None), P(("rad", "azi"), None, None))
    return jax.shard_map(
        on_device, mesh=mesh, in_specs=in_specs, out_specs=out_specs, check_vma=False
    )
```

profile of v0, /device:TPU:0, one launch (start us, length us, event | category | flops | bytes accessed | tf_op | source)
XLA Modules:
  0.0 481.5 jit_solution(11758504771758727994)
XLA Ops:
  10.2 153.2 %all-gather.2.cloned.1.call-done = f32[128,8,4096]{2,1,0:T(8,128)} async-done(((f32[16,8,4096]{2,1,0:T(8,128)}), f32[128,8,4096]{2,1,0:T(8,128)}) %all-gather.2.cloned.1.call-update) | async-done | bytes 16777232 | tf_op jit(solution)/shard_map/all_gather | solution.py:81
  163.6 17.3 %scatter_fusion = f32[16,8,4096]{2,1,0:T(8,128)S(1)} fusion(f32[16,8,4096]{2,1,0:T(8,128)S(1)} %broadcast_in_dim.29, s32[128]{0:T(128)S(1)} %compare_select_fusion, f32[128,8,4096]{2,1,0:T(8,128)} %all-gather.2.cloned.1.call-done), kind=kCustom, calls=%fused_computation | custom fusion | bytes 50332160 | tf_op jit(solution)/shard_map/scatter | solution.py:85
  181.0 9.0 %reshape.127 = f32[16,8,16,16,16]{4,3,2,1,0:T(8,128)} reshape(f32[16,8,4096]{2,1,0:T(8,128)S(1)} %scatter_fusion) | data formatting | bytes 4194304 | tf_op jit(solution)/shard_map/reshape | solution.py:86
  190.0 10.4 %bitcast_reduce_fusion = f32[8,16,16,16]{3,1,0,2:T(8,128)S(1)} fusion(f32[16,8,16,16,16]{4,3,2,1,0:T(8,128)} %reshape.127), kind=kLoop, calls=%fused_computation.148 | loop fusion | flops 491520 | bytes 2228224 | tf_op jit(solution)/shard_map/reduce_sum | solution.py:100
  200.4 17.7 %copy.21 = f32[8,16,16,16,16]{4,3,0,2,1:T(8,128)} copy(f32[8,16,16,16,16]{4,2,1,0,3:T(8,128)} %bitcast.80) | data formatting | bytes 4194304 | tf_op jit(solution)/shard_map/transpose | solution.py:87
  218.1 23.6 %reshape.128 = f32[8,16,16,256]{3,0,2,1:T(8,128)S(1)} reshape(f32[8,16,16,16,16]{4,3,0,2,1:T(8,128)} %copy.21) | data formatting | bytes 4194304 | tf_op jit(solution)/shard_map/reshape | solution.py:87
  250.7 4.6 collective-permute-start
  260.5 7.4 %bitcast_subtract_fusion.1 = f32[8,16,16,257]{3,0,2,1:T(8,128)} fusion(f32[8,16,16,258]{3,0,2,1:T(8,128)S(1)} %multiply_select_fusion.1, f32[8,16,16,256]{3,0,2,1:T(8,128)S(1)} %reshape.128, f32[8,16,16,2]{3,0,2,1:T(8,128)S(1)} %copy-done.6, f32[8,16,16,2]{3,0,2,1:T(8,128)S(1)} %copy-done.7, f32[3,8,8]{2,1,0:T(8,128)S(1)} %copy-done.9), kind=kOutput, calls=%fused_computation.18 | convolution fusion | flops 58949632 | bytes 23080960 | tf_op jit(solution)/shard_map/ce,e...->c.../dot_general | solution.py:51
  267.8 33.7 %all-reduce.3.cloned.1.call-done = f32[8,16,256]{2,1,0:T(8,128)} async-done(((f32[8,16,256]{2,1,0:T(8,128)}), f32[8,16,256]{2,1,0:T(8,128)}) %all-reduce.3.cloned.1.call-update) | async-done | bytes 131088 | tf_op jit(solution)/shard_map/psum | solution.py:100
  305.7 3.3 bitcast_subtract_fusion.5
  309.0 3.5 fusion.25
  317.6 3.5 collective-permute-start.7
  321.2 4.1 collective-permute-start.4
  326.5 3.1 pad_maximum_fusion.5
  332.3 7.8 %bitcast_subtract_fusion = f32[8,16,16,257]{3,0,2,1:T(8,128)} fusion(f32[8,16,16,258]{3,0,2,1:T(8,128)S(1)} %multiply_select_fusion, f32[8,16,16,256]{3,0,2,1:T(8,128)S(1)} %copy-done.1, f32[8,16,16,2]{3,0,2,1:T(8,128)S(1)} %get-tuple-element.10, f32[8,16,16,2]{3,0,2,1:T(8,128)S(1)} %copy-done.8, f32[3,8,8]{2,1,0:T(8,128)S(1)} %copy-done.9), kind=kOutput, calls=%fused_computation.17 | convolution fusion | flops 58949632 | bytes 23080960 | tf_op jit(solution)/shard_map/ce,e...->c.../dot_general | solution.py:51
  340.2 30.9 %all-reduce.5.cloned.1.call-done = f32[8,16,256]{2,0,1:T(8,128)} async-done(((f32[8,16,256]{2,0,1:T(8,128)}), f32[8,16,256]{2,0,1:T(8,128)}) %all-reduce.5.cloned.1.call-update) | async-done | bytes 131088 | tf_op jit(solution)/shard_map/psum | solution.py:100
  378.3 3.9 bitcast_subtract_fusion.3
  382.2 4.1 fusion.24
  389.3 10.5 %reshape.131 = f32[8,16,16,16,16]{4,3,0,2,1:T(8,128)} reshape(f32[8,16,16,256]{3,0,2,1:T(8,128)} %get-tuple-element.2) | data formatting | bytes 4194304 | tf_op jit(solution)/shard_map/reshape | solution.py:124
  399.8 18.0 %copy.26 = f32[16,8,16,16,16]{4,3,2,1,0:T(8,128)} copy(f32[16,8,16,16,16]{4,0,1,3,2:T(8,128)} %bitcast.81) | data formatting | bytes 4194304 | tf_op jit(solution)/shard_map/transpose | solution.py:125
  417.8 15.4 %reshape.132 = f32[16,8,4096]{2,1,0:T(8,128)} reshape(f32[16,8,16,16,16]{4,3,2,1,0:T(8,128)} %copy.26) | data formatting | bytes 4194304 | tf_op jit(solution)/shard_map/reshape | solution.py:125
  433.2 8.6 %reshape.129 = f32[8,16,16,16,16]{4,3,0,2,1:T(8,128)} reshape(f32[8,16,16,256]{3,0,2,1:T(8,128)S(1)} %copy-done.3) | data formatting | bytes 4194304 | tf_op jit(solution)/shard_map/reshape | solution.py:124
  441.8 17.8 %copy.25 = f32[16,8,16,16,16]{4,3,2,1,0:T(8,128)} copy(f32[16,8,16,16,16]{4,0,1,3,2:T(8,128)} %bitcast.82) | data formatting | bytes 4194304 | tf_op jit(solution)/shard_map/transpose | solution.py:125
  459.6 15.2 %reshape.130 = f32[16,8,4096]{2,1,0:T(8,128)} reshape(f32[16,8,16,16,16]{4,3,2,1,0:T(8,128)} %copy.25) | data formatting | bytes 4194304 | tf_op jit(solution)/shard_map/reshape | solution.py:125
  (82 shorter events, 40.6 us)
Async XLA Ops:
  7.2 156.3 %all-gather.2.cloned.1.call-start = ((), (), s32[]{:S(2)}) async-start(), calls=%async_computation | async-start | bytes 18874368 | tf_op jit(solution)/shard_map/all_gather | solution.py:81
  7.9 293.6 %all-reduce.3.cloned.1.call-start = ((), (), s32[]{:S(2)}) async-start(), calls=%async_computation.1 | async-start | bytes 262144 | tf_op jit(solution)/shard_map/psum | solution.py:100
  248.8 122.3 %all-reduce.5.cloned.1.call-start = ((), (), s32[]{:S(2)}) async-start(), calls=%async_computation.2 | async-start | bytes 262144 | tf_op jit(solution)/shard_map/psum | solution.py:100
  248.9 55.6 %collective-permute-start.3 = (f32[8,16,2,256]{3,0,2,1:T(8,128)S(1)}, f32[8,16,2,256]{3,0,2,1:T(8,128)S(1)}, u32[]{:S(2)}, u32[]{:S(2)}) collective-permute-start(f32[8,16,2,256]{3,0,2,1:T(8,128)S(1)} %get-tuple-element.16), channel_id=1, source_target_pairs={{1,0},{2,1},{3,2},{4,3},{5,4},{6,5},{7,6},{0,7},{9,8},{10,9},{11,1... | collective-permute-start | bytes 786440 | tf_op jit(solution)/shard_map/ppermute | solution.py:25
  249.1 53.6 %collective-permute-start.2 = (f32[8,16,2,256]{3,0,2,1:T(8,128)}, f32[8,16,2,256]{3,0,2,1:T(8,128)S(1)}, u32[]{:S(2)}, u32[]{:S(2)}) collective-permute-start(f32[8,16,2,256]{3,0,2,1:T(8,128)} %get-tuple-element.17), channel_id=1, source_target_pairs={{0,1},{1,2},{2,3},{3,4},{4,5},{5,6},{6,7},{7,0},{8,9},{9,10},{10,1... | collective-permute-start | bytes 786440 | tf_op jit(solution)/shard_map/ppermute | solution.py:23
  249.4 53.7 %collective-permute-start.1 = (f32[8,2,16,256]{3,0,2,1:T(8,128)}, f32[8,2,16,256]{3,0,2,1:T(8,128)S(1)}, u32[]{:S(2)}, u32[]{:S(2)}) collective-permute-start(f32[8,2,16,256]{3,0,2,1:T(8,128)} %get-tuple-element.12), channel_id=1, source_target_pairs={{8,0},{16,8},{24,16},{9,1},{17,9},{25,17},{10,2},{18,10},{26,18},{... | collective-permute-start | bytes 786440 | tf_op jit(solution)/shard_map/ppermute | solution.py:25
  250.7 51.9 %collective-permute-start = (f32[8,2,16,256]{3,0,2,1:T(8,128)}, f32[8,2,16,256]{3,0,2,1:T(8,128)S(1)}, u32[]{:S(2)}, u32[]{:S(2)}) collective-permute-start(f32[8,2,16,256]{3,0,2,1:T(8,128)} %get-tuple-element.13), channel_id=1, source_target_pairs={{0,8},{8,16},{16,24},{1,9},{9,17},{17,25},{2,10},{10,18},{18,26},{... | collective-permute-start | bytes 786440 | tf_op jit(solution)/shard_map/ppermute | solution.py:23
  258.9 1.6 copy-start.6
  258.9 1.6 copy-start.7
  258.9 1.6 copy-start.9
  309.0 3.5 copy-start.4
  314.5 3.1 copy-start
  317.6 57.7 %collective-permute-start.6 = (f32[8,16,2,256]{3,0,2,1:T(8,128)}, f32[8,16,2,256]{3,0,2,1:T(8,128)S(1)}, u32[]{:S(2)}, u32[]{:S(2)}) collective-permute-start(f32[8,16,2,256]{3,0,2,1:T(8,128)} %get-tuple-element.8), channel_id=1, source_target_pairs={{0,1},{1,2},{2,3},{3,4},{4,5},{5,6},{6,7},{7,0},{8,9},{9,10},{10,1... | collective-permute-start | bytes 786440 | tf_op jit(solution)/shard_map/ppermute | solution.py:23
  317.6 57.6 %collective-permute-start.7 = (f32[8,16,2,256]{3,0,2,1:T(8,128)}, f32[8,16,2,256]{3,0,2,1:T(8,128)}, u32[]{:S(2)}, u32[]{:S(2)}) collective-permute-start(f32[8,16,2,256]{3,0,2,1:T(8,128)} %get-tuple-element.9), channel_id=1, source_target_pairs={{1,0},{2,1},{3,2},{4,3},{5,4},{6,5},{7,6},{0,7},{9,8},{10,9},{11,1... | collective-permute-start | bytes 786440 | tf_op jit(solution)/shard_map/ppermute | solution.py:25
  321.2 51.0 %collective-permute-start.4 = (f32[8,2,16,256]{3,0,2,1:T(8,128)}, f32[8,2,16,256]{3,0,2,1:T(8,128)}, u32[]{:S(2)}, u32[]{:S(2)}) collective-permute-start(f32[8,2,16,256]{3,0,2,1:T(8,128)} %get-tuple-element.6), channel_id=1, source_target_pairs={{0,8},{8,16},{16,24},{1,9},{9,17},{17,25},{2,10},{10,18},{18,26},{... | collective-permute-start | bytes 786440 | tf_op jit(solution)/shard_map/ppermute | solution.py:23
  325.2 46.9 %collective-permute-start.5 = (f32[8,2,16,256]{3,0,2,1:T(8,128)}, f32[8,2,16,256]{3,0,2,1:T(8,128)}, u32[]{:S(2)}, u32[]{:S(2)}) collective-permute-start(f32[8,2,16,256]{3,0,2,1:T(8,128)} %get-tuple-element.7), channel_id=1, source_target_pairs={{8,0},{16,8},{24,16},{9,1},{17,9},{25,17},{10,2},{18,10},{26,18},{... | collective-permute-start | bytes 786440 | tf_op jit(solution)/shard_map/ppermute | solution.py:25
  330.5 1.6 copy-start.1
  330.5 1.9 copy-start.8
  374.2 1.6 copy-start.2
  382.2 4.1 copy-start.5
  417.8 15.4 %copy-start.3 = (f32[8,16,16,256]{3,0,2,1:T(8,128)S(1)}, f32[8,16,16,256]{3,0,2,1:T(8,128)}, u32[]{:S(2)}) copy-start(f32[8,16,16,256]{3,0,2,1:T(8,128)} %get-tuple-element.3) | copy-start | bytes 6291460
Sparse Core Ops, SparseCore 0:
  9.6 153.7 all-gather.1
  248.9 52.5 all-reduce.2
  317.7 53.3 all-reduce.4
where the time goes:
time: 485 us; the launch traced here: 482 us
  waiting for transfers between devices  219 us (45%)
  local copies, waits for them, and re-layouts  165 us (34%)
  other arithmetic  37.9 us (8%)
  matrix products  30 us (6%)
  starting transfers between devices  15.5 us (3%)
  between operations  14.4 us (3%)
    all_gather x1, waiting for transfers between devices, on_device(): arrived = lax.all_gather(blocks, 'azi', axis=0, tiled=True)  153 us
    psum x2, waiting for transfers between devices, sum_columns(): return lax.psum(jnp.sum(state_field, axis=2), 'azi') / azi_cells  64.6 us
    transpose x2, local copies, waits for them, and re-layouts, to_blocks(): split_field.transpose(3, 0, 1, 2, 4)  35.8 us
    reshape x2, local copies, waits for them, and re-layouts, to_blocks(): split_field.transpose(3, 0, 1, 2, 4)  30.6 us
    dot_general x6, matrix products, flux_change(): jnp.einsum('ce,e...->c...', matrix, summed, precision=lax.Precision.HIGHEST)  30 us
    reshape x1, local copies, waits for them, and re-layouts, on_device(): start_field.transpose(1, 2, 3, 0, 4)  23.6 us
    reshape x2, local copies, waits for them, and re-layouts, to_blocks(): split_field = state_field.reshape(CHANNELS, EDGE, EDGE, block_count, EDGE)  19.1 us
    transpose x1, local copies, waits for them, and re-layouts, on_device(): start_field.transpose(1, 2, 3, 0, 4)  17.7 us
  transfers between devices with their start and end apart: 11, of which 3 were waited for; matrix products, arithmetic and copies ran while one was open for 7% of the time, Pallas kernels for 0%

commit v1 on v0

v1 whole, which is shorter than its diff:
```python
import functools

import jax
import jax.numpy as jnp
from jax import lax
from jax.experimental import pallas as pl
from jax.experimental.pallas import tpu as pltpu
from jax.sharding import PartitionSpec as P

EDGE = 16
CHANNELS = 8
CAPACITY = 2
LANES = 128

time_step = 0.02
signal_speed = 2.0
shear_rate = -1.5

ANY = pl.BlockSpec(memory_space=pl.ANY)
SMEM = pl.BlockSpec(memory_space=pltpu.SMEM)
VMEM = pl.BlockSpec(memory_space=pltpu.VMEM)
F32 = jnp.float32


def minmod(a, b):
    return jnp.maximum(jnp.minimum(a, b), jnp.minimum(jnp.maximum(a, b), 0.0))


def lane_group():
    return lax.broadcasted_iota(jnp.int32, (CHANNELS, LANES), 1) // EDGE


def swap_groups(rows, group):
    rows = list(rows)
    for bit in (1, 2, 4):
        low = (group & bit) == 0
        shift = EDGE * bit
        for i in range(8):
            if i & bit:
                continue
            a, b = rows[i], rows[i + bit]
            rows[i] = jnp.where(low, a, pltpu.roll(b, shift, 1))
            rows[i + bit] = jnp.where(low, pltpu.roll(a, LANES - shift, 1), b)
    return rows


def pack_kernel(azi_count, block_count, place, assignment, blocks, *refs):
    outs = refs[: azi_count - 1]
    table, fill, sems = refs[azi_count - 1 :]
    azi = place[0]
    first = place[1]
    for i in range(azi_count):
        fill[i] = 0
    for i in range(azi_count * CAPACITY):
        table[i] = 0

    def note(j, carry):
        device = lax.div(assignment[first + j], block_count)
        shift = lax.rem(lax.rem(device, azi_count) - azi + azi_count, azi_count)
        k = fill[shift]
        table[shift * CAPACITY + k] = j
        fill[shift] = k + 1
        return carry

    lax.fori_loop(0, block_count, note, 0)
    copies = []
    for shift in range(1, azi_count):
        for k in range(CAPACITY):
            spot = shift * CAPACITY + k
            copy = pltpu.make_async_copy(
                blocks.at[table[spot]], outs[shift - 1].at[k], sems.at[spot]
            )
            copy.start()
            copies.append(copy)
    for copy in copies:
        copy.wait()


def pack(place, assignment, blocks, azi_count):
    shape = (CAPACITY,) + blocks.shape[1:]
    spots = azi_count * CAPACITY
    return pl.pallas_call(
        functools.partial(pack_kernel, azi_count, blocks.shape[0]),
        out_shape=[jax.ShapeDtypeStruct(shape, F32)] * (azi_count - 1),
        in_specs=[SMEM, SMEM, ANY],
        out_specs=[ANY] * (azi_count - 1),
        scratch_shapes=[
            pltpu.SMEM((spots,), jnp.int32),
            pltpu.SMEM((azi_count,), jnp.int32),
            pltpu.SemaphoreType.DMA((spots,)),
        ],
        name="pack",
    )(place, assignment, blocks)


def column_kernel(azi_count, block_count, place, assignment, blocks, sums, table, fill):
    azi = place[0]
    first = place[1]
    row_first = place[2]
    own = place[3]
    group = lane_group()
    sums[...] = jnp.zeros(sums.shape, F32)

    def one(j, carry):
        slot = lax.rem(assignment[first + j], block_count)
        here = group == lax.rem(slot, 8)
        lanes = pl.ds(pl.multiple_of(lax.div(slot, 8) * LANES, LANES), LANES)
        for x in range(EDGE):
            base = x * EDGE * EDGE
            part = blocks[j, :, base : base + LANES] + blocks[j, :, base + LANES : base + 2 * LANES]
            for shift in (64, 32, 16):
                part = part + pltpu.roll(part, shift, 1)
            sums[x, :, lanes] = sums[x, :, lanes] + jnp.where(here, part, 0.0)
        return carry

    lax.fori_loop(0, block_count, one, 0)

    spots = azi_count * CAPACITY
    for i in range(spots):
        table[i] = -1
    for i in range(CAPACITY):
        table[spots + i] = 0

    def source(s, carry):
        shift = lax.rem(azi - s + azi_count, azi_count)
        fill[0] = 0

        def entry(j, inner):
            slot = assignment[row_first + s * block_count + j]

            @pl.when(lax.div(slot, block_count) == own)
            def _():
                k = fill[0]
                table[shift * CAPACITY + k] = lax.rem(slot, block_count)

                @pl.when(shift == 0)
                def _():
                    table[spots + k] = j

                fill[0] = k + 1

            return inner

        lax.fori_loop(0, block_count, entry, 0)
        return carry

    lax.fori_loop(0, azi_count, source, 0)


def column_sums(place, assignment, blocks, azi_count):
    block_count = blocks.shape[0]
    spots = azi_count * CAPACITY
    return pl.pallas_call(
        functools.partial(column_kernel, azi_count, block_count),
        out_shape=[
            jax.ShapeDtypeStruct((EDGE, CHANNELS, block_count * EDGE), F32),
            jax.ShapeDtypeStruct((spots + CAPACITY,), jnp.int32),
        ],
        in_specs=[SMEM, SMEM, VMEM],
        out_specs=[VMEM, SMEM],
        scratch_shapes=[pltpu.SMEM((1,), jnp.int32)],
        name="column_sums",
    )(place, assignment, blocks)


def unpack_kernel(azi_count, block_count, table, blocks, *refs):
    arrived = refs[: azi_count - 1]
    field, rad_head, rad_tail, azi_head, azi_tail, held, sems = refs[azi_count - 1 :]
    spots = azi_count * CAPACITY

    def copy_of(shift, k):
        spot = shift * CAPACITY + k
        if shift == 0:
            source = blocks.at[table[spots + k]]
        else:
            source = arrived[shift - 1].at[k]
        return pltpu.make_async_copy(source, held.at[jnp.maximum(table[spot], 0)], sems.at[spot])

    for shift in range(azi_count):
        for k in range(CAPACITY):

            @pl.when(table[shift * CAPACITY + k] >= 0)
            def _(shift=shift, k=k):
                copy_of(shift, k).start()

    for shift in range(azi_count):
        for k in range(CAPACITY):

            @pl.when(table[shift * CAPACITY + k] >= 0)
            def _(shift=shift, k=k):
                copy_of(shift, k).wait()

    group = lane_group()

    def row(x, carry):
        base = x * (EDGE * EDGE)
        for half in range(block_count // 8):
            lanes = slice(half * LANES, (half + 1) * LANES)
            for upper in range(2):
                at = pl.ds(pl.multiple_of(base + upper * LANES, LANES), LANES)
                tiles = swap_groups([held[half * 8 + i, :, at] for i in range(8)], group)
                for i in range(8):
                    field[x, upper * 8 + i, :, lanes] = tiles[i]
                for i in range(2):
                    if upper == 0:
                        azi_head[x, i, :, lanes] = tiles[i]
                    else:
                        azi_tail[x, i, :, lanes] = tiles[6 + i]
        return carry

    lax.fori_loop(0, EDGE, row, 0)
    rad_head[...] = field[0:2]
    rad_tail[...] = field[EDGE - 2 : EDGE]


def field_shapes(vertical):
    rad = jax.ShapeDtypeStruct((2, EDGE, CHANNELS, vertical), F32)
    azi = jax.ShapeDtypeStruct((EDGE, 2, CHANNELS, vertical), F32)
    return [jax.ShapeDtypeStruct((EDGE, EDGE, CHANNELS, vertical), F32), rad, rad, azi, azi]


def unpack(table, blocks, arrived, azi_count):
    block_count = blocks.shape[0]
    return pl.pallas_call(
        functools.partial(unpack_kernel, azi_count, block_count),
        out_shape=field_shapes(block_count * EDGE),
        in_specs=[SMEM] + [ANY] * azi_count,
        out_specs=[VMEM] * 5,
        scratch_shapes=[
            pltpu.VMEM(blocks.shape, F32),
            pltpu.SemaphoreType.DMA((azi_count * CAPACITY,)),
        ],
        name="unpack",
    )(table, blocks, *arrived)


def stage_row(x, padded, mixed, total, weights, mean, shear, finish):
    vertical = padded.shape[-1]
    velocity = jnp.broadcast_to(mean[x, 2:3, :], (CHANNELS, vertical)) + shear[x]
    half_velocity = 0.5 * velocity
    half_signal = 0.5 * jnp.abs(velocity) + 0.5 * signal_speed
    here = x + 2
    u = [padded[here, i] for i in range(4)]
    d = [u[i + 1] - u[i] for i in range(3)]
    s = [minmod(d[0], d[1]), minmod(d[1], d[2])]
    u1, u2, u3 = u[1:]
    d1, d2 = d[1:]
    s0, s1 = s
    for y in range(EDGE):
        u4 = padded[here, y + 4]
        d3 = u4 - u3
        s2 = minmod(d2, d3)
        sum_azi = (d1 + d2) + s1 - 0.5 * (s0 + s2)
        jump_azi = (d2 - d1) - 0.5 * (s2 - s0)
        cell = u2
        r0, r1, r3, r4 = (padded[here + k, y + 2] for k in (-2, -1, 1, 2))
        e0, e1, e2, e3 = r1 - r0, cell - r1, r3 - cell, r4 - r3
        t0, t1, t2 = minmod(e0, e1), minmod(e1, e2), minmod(e2, e3)
        sum_rad = (e1 + e2) + t1 - 0.5 * (t0 + t2)
        jump = (e2 - e1) - 0.5 * (t2 - t0)
        f1 = pltpu.roll(cell, vertical - 1, 1) - cell
        f0 = pltpu.roll(f1, 1, 1)
        g1 = minmod(f0, f1)
        g0 = pltpu.roll(g1, 1, 1)
        g2 = pltpu.roll(g1, vertical - 1, 1)
        sum_vert = (f0 + f1) + g1 - 0.5 * (g0 + g2)
        jump = jump + ((f1 - f0) - 0.5 * (g2 - g0))
        at = slice(y * vertical, (y + 1) * vertical)
        mixed[0:8, at] = sum_rad
        mixed[8:16, at] = sum_azi
        mixed[16:24, at] = sum_vert
        total[y] = half_velocity * sum_azi - half_signal * jump_azi - jump
        u1, u2, u3 = u2, u3, u4
        d1, d2 = d2, d3
        s0, s1 = s1, s2
    flux = lax.dot_general(
        weights[...],
        mixed[...],
        (((1,), (0,)), ((), ())),
        precision=lax.Precision.HIGHEST,
        preferred_element_type=F32,
    )
    for y in range(EDGE):
        finish(y, padded[here, y + 2], flux[:, y * vertical : (y + 1) * vertical] + total[y])


def load_padded(field, low_rad, high_rad, low_azi, high_azi, padded, sems):
    middle = pl.ds(2, EDGE)
    copies = [
        (field, padded.at[middle, middle]),
        (low_rad, padded.at[pl.ds(0, 2), middle]),
        (high_rad, padded.at[pl.ds(EDGE + 2, 2), middle]),
        (low_azi, padded.at[middle, pl.ds(0, 2)]),
        (high_azi, padded.at[middle, pl.ds(EDGE + 2, 2)]),
    ]
    copies = [pltpu.make_async_copy(a, b, sems.at[i]) for i, (a, b) in enumerate(copies)]
    for copy in copies:
        copy.start()
    for copy in copies:
        copy.wait()


def first_kernel(
    shear, field, low_rad, high_rad, low_azi, high_azi, mean, weights, ratio, relax,
    state, rad_head, rad_tail, azi_head, azi_tail, sums, padded, mixed, total, sems,
):
    load_padded(field, low_rad, high_rad, low_azi, high_azi, padded, sems)

    def row(x, carry):
        step = ratio[...]
        pull = relax[...]
        average = mean[x]
        column = []

        def finish(y, cell, change):
            value = cell - step * change - pull * (cell - average)
            state[x, y] = value
            if y < 2:
                azi_head[x, y] = value
            if y >= EDGE - 2:
                azi_tail[x, y - (EDGE - 2)] = value
            column.append(value if not column else column.pop() + value)

        stage_row(x, padded, mixed, total, weights, mean, shear, finish)
        sums[x] = column[0]
        return carry

    lax.fori_loop(0, EDGE, row, 0)
    rad_head[...] = state[0:2]
    rad_tail[...] = state[EDGE - 2 : EDGE]


def stage_scratch(vertical):
    return [
        pltpu.VMEM((EDGE + 4, EDGE + 4, CHANNELS, vertical), F32),
        pltpu.VMEM((3 * CHANNELS, EDGE * vertical), F32),
        pltpu.VMEM((EDGE, CHANNELS, vertical), F32),
        pltpu.SemaphoreType.DMA((6,)),
    ]


def first_stage(shear, field, halos, mean, weights, ratio, relax):
    vertical = field.shape[-1]
    return pl.pallas_call(
        first_kernel,
        out_shape=field_shapes(vertical) + [jax.ShapeDtypeStruct((EDGE, CHANNELS, vertical), F32)],
        in_specs=[SMEM] + [ANY] * 5 + [VMEM] * 4,
        out_specs=[VMEM] * 6,
        scratch_shapes=stage_scratch(vertical),
        name="first_stage",
    )(shear, field, *halos, mean, weights, ratio, relax)


def second_kernel(
    shear, start, field, low_rad, high_rad, low_azi, high_azi, mean, weights, ratio, relax,
    final, tendency, padded, mixed, total, sems, change_row, start_field,
):
    begin = pltpu.make_async_copy(start, start_field, sems.at[5])
    begin.start()
    load_padded(field, low_rad, high_rad, low_azi, high_azi, padded, sems)
    begin.wait()
    group = lane_group()
    halves = start.shape[-1] // LANES

    def row(x, carry):
        step = ratio[...]
        pull = relax[...]
        average = mean[x]

        def finish(y, cell, change):
            delta = (cell - start_field[x, y]) - step * change - pull * (cell - average)
            change_row[y] = 0.5 * delta

        stage_row(x, padded, mixed, total, weights, mean, shear, finish)
        base = x * (EDGE * EDGE)
        for half in range(halves):
            lanes = slice(half * LANES, (half + 1) * LANES)
            for upper in range(2):
                at = pl.ds(pl.multiple_of(base + upper * LANES, LANES), LANES)
                deltas = [change_row[upper * 8 + i, :, lanes] for i in range(8)]
                values = [start_field[x, upper * 8 + i, :, lanes] + deltas[i] for i in range(8)]
                for i, tile in enumerate(swap_groups(deltas, group)):
                    tendency[half * 8 + i, :, at] = tile * (1.0 / time_step)
                for i, tile in enumerate(swap_groups(values, group)):
                    final[half * 8 + i, :, at] = tile
        return carry

    lax.fori_loop(0, EDGE, row, 0)


def second_stage(shear, start, field, halos, mean, weights, ratio, relax, out_shape):
    vertical = field.shape[-1]
    return pl.pallas_call(
        second_kernel,
        out_shape=[jax.ShapeDtypeStruct(out_shape, F32)] * 2,
        in_specs=[SMEM] + [ANY] * 6 + [VMEM] * 4,
        out_specs=[VMEM] * 2,
        scratch_shapes=stage_scratch(vertical)
        + [
            pltpu.VMEM((EDGE, CHANNELS, vertical), F32),
            pltpu.VMEM((EDGE, EDGE, CHANNELS, vertical), F32),
        ],
        name="second_stage",
    )(shear, start, field, *halos, mean, weights, ratio, relax)


def sum_azi(values):
    count = lax.axis_size("azi")
    if count & (count - 1):
        return lax.psum(values, "azi")
    step = 1
    while step < count:
        values = values + lax.ppermute(values, "azi", [(i, i ^ step) for i in range(count)])
        step *= 2
    return values


def exchange(rad_head, rad_tail, azi_head, azi_tail):
    rad, azi = lax.axis_size("rad"), lax.axis_size("azi")
    return (
        lax.ppermute(rad_tail, "rad", [(i, i + 1) for i in range(rad - 1)]),
        lax.ppermute(rad_head, "rad", [(i + 1, i) for i in range(rad - 1)]),
        lax.ppermute(azi_tail, "azi", [(i, (i + 1) % azi) for i in range(azi)]),
        lax.ppermute(azi_head, "azi", [((i + 1) % azi, i) for i in range(azi)]),
    )


def on_device(blocks, assignment, levels, coupling, damping):
    azi_count = lax.axis_size("azi")
    rad_count = lax.axis_size("rad")
    azi_index = lax.axis_index("azi")
    rad_index = lax.axis_index("rad")
    block_count = blocks.shape[0]
    vertical = block_count * EDGE
    own = rad_index * azi_count + azi_index
    row_first = rad_index * (azi_count * block_count)
    place = jnp.stack([azi_index, own * block_count, row_first, own]).astype(jnp.int32)

    packed = pack(place, assignment, blocks, azi_count)
    arrived = [
        lax.ppermute(packed[d - 1], "azi", [(i, (i + d) % azi_count) for i in range(azi_count)])
        for d in range(1, azi_count)
    ]
    first_sums, table = column_sums(place, assignment, blocks, azi_count)
    azi_cells = EDGE * azi_count
    first_mean = sum_azi(first_sums) / azi_cells

    factor = jnp.where(levels == 0, 1.0, jnp.where(levels == 1, 2.0, 4.0)).astype(F32) * time_step
    ratio = jnp.broadcast_to(jnp.repeat(factor, EDGE)[None, :], (CHANNELS, vertical))
    relax = jnp.broadcast_to((time_step * damping)[:, None], (CHANNELS, vertical))
    weights = 0.5 * coupling.transpose(1, 0, 2).reshape(CHANNELS, 3 * CHANNELS)
    cells = (rad_index * EDGE + jnp.arange(EDGE)).astype(F32)
    shear = shear_rate * ((cells + 0.5) * (2.0 / (EDGE * rad_count)) - 1.0)

    start, *edges = unpack(table, blocks, arrived, azi_count)
    state, *rest = first_stage(
        shear, start, exchange(*edges), first_mean, weights, ratio, relax
    )
    second_mean = sum_azi(rest[4]) / azi_cells
    final, tendency = second_stage(
        shear, start, state, exchange(*rest[:4]), second_mean, weights, ratio, relax, blocks.shape
    )
    return final, tendency


def solution(mesh):
    in_specs = (P(("rad", "azi"), None, None), P(), P(("rad", "azi")), P(), P())
    out_specs = (P(("rad", "azi"), None, None), P(("rad", "azi"), None, None))
    return jax.shard_map(
        on_device, mesh=mesh, in_specs=in_specs, out_specs=out_specs, check_vma=False
    )
```

time: 485 us -> 212 us (0.44)
  waiting for transfers between devices: 219 us -> 44.8 us
  local copies, waits for them, and re-layouts: 165 us -> 3.87 us
  Pallas kernels: 0 us -> 112 us
  other arithmetic: 37.9 us -> 3.45 us
  starting transfers between devices: 15.5 us -> 46.4 us
  matrix products: 30 us -> 0 us
  between operations: 14.4 us -> 0.87 us
    all_gather x1 -> x0, waiting for transfers between devices: 153 us -> none  [on_device(): arrived = lax.all_gather(blocks, 'azi', axis=0, tiled=True)]
    pallas_call x0 -> x5, Pallas kernels: none -> 112 us  [the longest x1 57.9 us: pack(): pl.pallas_call(functools.partial(pack_kernel, azi_count, blocks.shape[0])...]
    reshape x6 -> x0, local copies, waits for them, and re-layouts: 82.4 us -> none  [the longest x2 30.6 us: to_blocks(): split_field.transpose(3, 0, 1, 2, 4)]
    psum x2 -> x0, waiting for transfers between devices: 64.6 us -> none  [sum_columns(): return lax.psum(jnp.sum(state_field, axis=2), 'azi') / azi_cells]
    transpose x3 -> x0, local copies, waits for them, and re-layouts: 53.5 us -> none  [the longest x2 35.8 us: to_blocks(): split_field.transpose(3, 0, 1, 2, 4)]
    ppermute x8 -> x21, waiting for transfers between devices: 0.02 us -> 44.8 us  [the longest x6 21 us: sum_azi(): lax.ppermute(values, 'azi', [(i, i ^ step) for i in range(count)])]
    ppermute x8 -> x21, starting transfers between devices: 15.3 us -> 46.4 us  [the longest x7 12.5 us: on_device(): lax.ppermute(packed[d - 1], 'azi', [(i, (i + d) % azi_count) for i in ran...]
    dot_general x6 -> x0, matrix products: 30 us -> none  [flux_change(): jnp.einsum('ce,e...->c...', matrix, summed, precision=lax.Precision.HIGHEST)]
  transfers between devices with their start and end apart: 11 -> 21, of which waited for: 3 -> 9; matrix products, arithmetic and copies ran while one was open for 7% -> 1% of each run, Pallas kernels for 0% -> 31%
where the time goes in v1:
time: 212 us; the launch traced here: 211 us
  Pallas kernels  112 us (53%)
  starting transfers between devices  46.4 us (22%)
  waiting for transfers between devices  44.8 us (21%)
  local copies, waits for them, and re-layouts  3.87 us (2%)
  other arithmetic  3.45 us (2%)
    pallas_call x1, Pallas kernels, pack(): pl.pallas_call(functools.partial(pack_kernel, azi_count, blocks.shape[0])...  57.9 us
    pallas_call x1, Pallas kernels, second_stage(): pl.pallas_call(second_kernel, out_shape=[jax.ShapeDtypeStruct(out_shape,...  21.3 us
    ppermute x6, waiting for transfers between devices, sum_azi(): lax.ppermute(values, 'azi', [(i, i ^ step) for i in range(count)])  21 us
    pallas_call x1, Pallas kernels, first_stage(): pl.pallas_call(first_kernel, out_shape=field_shapes(vertical) + [jax.Shap...  16.6 us
    ppermute x7, waiting for transfers between devices, on_device(): lax.ppermute(packed[d - 1], 'azi', [(i, (i + d) % azi_count) for i in ran...  12.9 us
    ppermute x7, starting transfers between devices, on_device(): lax.ppermute(packed[d - 1], 'azi', [(i, (i + d) % azi_count) for i in ran...  12.5 us
    ppermute x2, starting transfers between devices, exchange(): lax.ppermute(azi_head, 'azi', [((i + 1) % azi, i) for i in range(azi)])  11.5 us
    pallas_call x1, Pallas kernels, unpack(): pl.pallas_call(functools.partial(unpack_kernel, azi_count, block_count),...  8.13 us
  transfers between devices with their start and end apart: 21, of which 9 were waited for; matrix products, arithmetic and copies ran while one was open for 1% of the time, Pallas kernels for 31%

profile of v1, /device:TPU:0, one launch (start us, length us, event | category | flops | bytes accessed | tf_op | source)
XLA Modules:
  0.0 211.2 jit_solution(15293102976980620528)
XLA Ops:
  1.3 7.9 %column_sums.1 = (f32[16,8,256]{2,1,0:T(8,128)}, s32[18]{0:T(128)}) custom-call(s32[4]{0:T(128)} %pad_add_fusion.place, s32[512]{0:T(512)} %assignment.3, f32[16,8,4096]{2,1,0:T(8,128)} %blocks.5), custom_call_target="tpu_custom_call" | custom-call | tf_op jit(solution)/shard_map/column_sums/pallas_call | solution.py:153
  9.7 57.9 %pack.1 = (f32[2,8,4096]{2,1,0:T(8,128)}, f32[2,8,4096]{2,1,0:T(8,128)}, f32[2,8,4096]{2,1,0:T(8,128)}, f32[2,8,4096]{2,1,0:T(8,128)}, f32[2,8,4096]{2,1,0:T(8,1...) custom-call(s32[4]{0:T(128)} %pad_add_fusion.place, s32[512]{0:T(512)} %assignment.3, f32[16,8,4096]{2,1,0:T(8,128)} %blocks.5), custom_call_target="tpu_custom_call" | custom-call | tf_op jit(solution)/shard_map/pack/pallas_call | solution.py:82
  67.7 3.0 %collective-permute-start.1 = (f32[2,8,4096]{2,1,0:T(8,128)}, f32[2,8,4096]{2,1,0:T(8,128)S(1)}, u32[]{:S(2)}, u32[]{:S(2)}) collective-permute-start(f32[2,8,4096]{2,1,0:T(8,128)} %get-tuple-element.24), channel_id=1, source_target_pairs={{0,2},{1,3},{2,4},{3,5},{4,6},{5,7},{6,0},{7,1},{8,10},{9,11},{10,... | collective-permute-start | bytes 786440 | tf_op jit(solution)/shard_map/ppermute | solution.py:441
  70.7 2.1 collective-permute-start.2
  74.1 1.6 collective-permute-start.12
  75.7 16.0 %collective-permute-done.12 = f32[16,8,256]{2,1,0:T(8,128)S(1)} collective-permute-done((f32[16,8,256]{2,1,0:T(8,128)S(1)}, f32[16,8,256]{2,1,0:T(8,128)S(1)}, u32[]{:S(2)}, u32[]{:S(2)}) %collective-permute-start.12) | collective-permute-done | bytes 131104 | tf_op jit(solution)/shard_map/ppermute | solution.py:413
  91.7 4.6 %collective-permute-start.4 = (f32[2,8,4096]{2,1,0:T(8,128)}, f32[2,8,4096]{2,1,0:T(8,128)S(1)}, u32[]{:S(2)}, u32[]{:S(2)}) collective-permute-start(f32[2,8,4096]{2,1,0:T(8,128)} %get-tuple-element.27), channel_id=1, source_target_pairs={{0,5},{1,6},{2,7},{3,0},{4,1},{5,2},{6,3},{7,4},{8,13},{9,14},{10,... | collective-permute-start | bytes 786440 | tf_op jit(solution)/shard_map/ppermute | solution.py:441
  96.4 1.4 collective-permute-start.5
  97.8 1.3 collective-permute-done.2.refs_2_
  99.3 10.7 %collective-permute-done.4.refs_4_ = f32[2,8,4096]{2,1,0:T(8,128)S(1)} collective-permute-done((f32[2,8,4096]{2,1,0:T(8,128)}, f32[2,8,4096]{2,1,0:T(8,128)S(1)}, u32[]{:S(2)}, u32[]{:S(2)}) %collective-permute-start.4) | collective-permute-done | bytes 262176 | tf_op jit(solution)/shard_map/ppermute | solution.py:441
  111.5 8.1 %unpack.1 = (f32[16,16,8,256]{3,2,1,0:T(8,128)}, f32[2,16,8,256]{3,2,1,0:T(8,128)}, f32[2,16,8,256]{3,2,1,0:T(8,128)}, f32[16,2,8,256]{3,2,1,0:T(8,128)}, f32[16,2,8,256]{3,2,1,0:T(8,128)}) custom-call(s32[18]{0:T(128)} %get-tuple-element.22.table, f32[16,8,4096]{2,1,0:T(8,128)} %blocks.5, f32[2,8,4096]{2,1,0:T(8,128)} %copy-done, f32[2,8,4096]{2,1,0:T(8,128)} %copy-done.1, ...), custom_call_target="tpu_custom_call" | custom-call | tf_op jit(solution)/shard_map/unpack/pallas_call | solution.py:224
  119.6 3.4 %collective-permute-start.7 = (f32[2,16,8,256]{3,2,1,0:T(8,128)}, f32[2,16,8,256]{3,2,1,0:T(8,128)S(1)}, u32[]{:S(2)}, u32[]{:S(2)}) collective-permute-start(f32[2,16,8,256]{3,2,1,0:T(8,128)} %get-tuple-element.31), channel_id=1, source_target_pairs={{0,8},{8,16},{16,24},{1,9},{9,17},{17,25},{2,10},{10,18},{18,26},{... | collective-permute-start | bytes 786440 | tf_op jit(solution)/shard_map/ppermute | solution.py:421
  123.1 1.3 collective-permute-start.8
  124.4 4.8 %collective-permute-start.9 = (f32[16,2,8,256]{3,2,1,0:T(8,128)}, f32[16,2,8,256]{3,2,1,0:T(8,128)S(1)}, u32[]{:S(2)}, u32[]{:S(2)}) collective-permute-start(f32[16,2,8,256]{3,2,1,0:T(8,128)} %get-tuple-element.33), channel_id=1, source_target_pairs={{0,1},{1,2},{2,3},{3,4},{4,5},{5,6},{6,7},{7,0},{8,9},{9,10},{10,1... | collective-permute-start | bytes 786440 | tf_op jit(solution)/shard_map/ppermute | solution.py:423
  129.1 8.0 %collective-permute-start.10 = (f32[16,2,8,256]{3,2,1,0:T(8,128)}, f32[16,2,8,256]{3,2,1,0:T(8,128)S(1)}, u32[]{:S(2)}, u32[]{:S(2)}) collective-permute-start(f32[16,2,8,256]{3,2,1,0:T(8,128)} %get-tuple-element.34), channel_id=1, source_target_pairs={{1,0},{2,1},{3,2},{4,3},{5,4},{6,5},{7,6},{0,7},{9,8},{10,9},{11,1... | collective-permute-start | bytes 786440 | tf_op jit(solution)/shard_map/ppermute | solution.py:424
  139.2 4.3 %collective-permute-done.9.low_azi = f32[16,2,8,256]{3,2,1,0:T(8,128)S(1)} collective-permute-done((f32[16,2,8,256]{3,2,1,0:T(8,128)}, f32[16,2,8,256]{3,2,1,0:T(8,128)S(1)}, u32[]{:S(2)}, u32[]{:S(2)}) %collective-permute-start.9) | collective-permute-done | bytes 262176 | tf_op jit(solution)/shard_map/ppermute | solution.py:423
  144.9 16.6 %first_stage.1 = (f32[16,16,8,256]{3,2,1,0:T(8,128)}, f32[2,16,8,256]{3,2,1,0:T(8,128)}, f32[2,16,8,256]{3,2,1,0:T(8,128)}, f32[16,2,8,256]{3,2,1,0:T(8,128)}, f...) custom-call(f32[16]{0:T(128)} %add_multiply_fusion.2.shear, f32[16,16,8,256]{3,2,1,0:T(8,128)} %get-tuple-element.30.field.start, ...), custom_call_target="tpu_custom_call" | custom-call | tf_op jit(solution)/shard_map/first_stage/pallas_call | solution.py:344
  164.2 4.3 %collective-permute-start.19 = (f32[16,8,256]{2,1,0:T(8,128)S(1)}, f32[16,8,256]{2,1,0:T(8,128)S(1)}, u32[]{:S(2)}, u32[]{:S(2)}) collective-permute-start(f32[16,8,256]{2,1,0:T(8,128)S(1)} %add.38), channel_id=1, source_target_pairs={{0,2},{1,3},{2,0},{3,1},{4,6},{5,7},{6,4},{7,5},{8,10},{9,11},{10,... | collective-permute-start | bytes 393224 | tf_op jit(solution)/shard_map/ppermute | solution.py:413
  168.5 3.8 %collective-permute-done.19 = f32[16,8,256]{2,1,0:T(8,128)S(1)} collective-permute-done((f32[16,8,256]{2,1,0:T(8,128)S(1)}, f32[16,8,256]{2,1,0:T(8,128)S(1)}, u32[]{:S(2)}, u32[]{:S(2)}) %collective-permute-start.19) | collective-permute-done | bytes 131104 | tf_op jit(solution)/shard_map/ppermute | solution.py:413
  173.4 3.4 %collective-permute-start.14 = (f32[2,16,8,256]{3,2,1,0:T(8,128)}, f32[2,16,8,256]{3,2,1,0:T(8,128)S(1)}, u32[]{:S(2)}, u32[]{:S(2)}) collective-permute-start(f32[2,16,8,256]{3,2,1,0:T(8,128)} %get-tuple-element.37), channel_id=1, source_target_pairs={{0,8},{8,16},{16,24},{1,9},{9,17},{17,25},{2,10},{10,18},{18,26},{... | collective-permute-start | bytes 786440 | tf_op jit(solution)/shard_map/ppermute | solution.py:421
  176.8 1.3 collective-permute-start.15
  178.2 3.5 %collective-permute-start.17 = (f32[16,2,8,256]{3,2,1,0:T(8,128)}, f32[16,2,8,256]{3,2,1,0:T(8,128)S(1)}, u32[]{:S(2)}, u32[]{:S(2)}) collective-permute-start(f32[16,2,8,256]{3,2,1,0:T(8,128)} %get-tuple-element.40), channel_id=1, source_target_pairs={{1,0},{2,1},{3,2},{4,3},{5,4},{6,5},{7,6},{0,7},{9,8},{10,9},{11,1... | collective-permute-start | bytes 786440 | tf_op jit(solution)/shard_map/ppermute | solution.py:424
  182.4 6.6 %collective-permute-done.15.high_rad = f32[2,16,8,256]{3,2,1,0:T(8,128)S(1)} collective-permute-done((f32[2,16,8,256]{3,2,1,0:T(8,128)}, f32[2,16,8,256]{3,2,1,0:T(8,128)S(1)}, u32[]{:S(2)}, u32[]{:S(2)}) %collective-permute-start.15) | collective-permute-done | bytes 262176 | tf_op jit(solution)/shard_map/ppermute | solution.py:422
  189.9 21.3 %second_stage.1 = (f32[16,8,4096]{2,1,0:T(8,128)}, f32[16,8,4096]{2,1,0:T(8,128)}) custom-call(f32[16]{0:T(128)} %add_multiply_fusion.2.shear, f32[16,16,8,256]{3,2,1,0:T(8,128)} %get-tuple-element.30.field.start, f32[16,16,8,256]{3,2,1,0:T(8,128)} %get-tuple-element.36.field, f32[2,16,8,256]{3,2,1,0:T(8,128)} %copy-done.7, f32[2,16,8,256]{3,2,1,0:T(8,128)} %copy-done.8, ...), custom_call_target="tpu_custom_call" | custom-call | tf_op jit(solution)/shard_map/second_stage/pallas_call | solution.py:393
  (78 shorter events, 13.0 us)
Async XLA Ops:
  1.2 74.5 %copy-start.16 = (f32[3,8,8]{2,1,0:T(8,128)S(1)}, f32[3,8,8]{2,1,0:T(8,128)}, u32[]{:S(2)}) copy-start(f32[3,8,8]{2,1,0:T(8,128)} %param.8) | copy-start | bytes 2308
  1.3 96.5 %copy-start.17 = (s32[16]{0:T(128)S(1)}, s32[16]{0:T(128)}, u32[]{:S(2)}) copy-start(s32[16]{0:T(128)} %param.7) | copy-start | bytes 196
  1.3 97.9 %copy-start.18 = (f32[8]{0:T(128)S(1)}, f32[8]{0:T(128)}, u32[]{:S(2)}) copy-start(f32[8]{0:T(128)} %param.9) | copy-start | bytes 100
  9.2 64.9 %collective-permute-start.11 = (f32[16,8,256]{2,1,0:T(8,128)}, f32[16,8,256]{2,1,0:T(8,128)S(1)}, u32[]{:S(2)}, u32[]{:S(2)}) collective-permute-start(f32[16,8,256]{2,1,0:T(8,128)} %get-tuple-element.35), channel_id=1, source_target_pairs={{0,1},{1,0},{2,3},{3,2},{4,5},{5,4},{6,7},{7,6},{8,9},{9,8},{10,11... | collective-permute-start | bytes 393224 | tf_op jit(solution)/shard_map/ppermute | solution.py:413
  67.6 28.8 %collective-permute-start = (f32[2,8,4096]{2,1,0:T(8,128)}, f32[2,8,4096]{2,1,0:T(8,128)S(1)}, u32[]{:S(2)}, u32[]{:S(2)}) collective-permute-start(f32[2,8,4096]{2,1,0:T(8,128)} %get-tuple-element.23), channel_id=1, source_target_pairs={{0,1},{1,2},{2,3},{3,4},{4,5},{5,6},{6,7},{7,0},{8,9},{9,10},{10,1... | collective-permute-start | bytes 786440 | tf_op jit(solution)/shard_map/ppermute | solution.py:441
  67.7 30.0 %collective-permute-start.1 = (f32[2,8,4096]{2,1,0:T(8,128)}, f32[2,8,4096]{2,1,0:T(8,128)S(1)}, u32[]{:S(2)}, u32[]{:S(2)}) collective-permute-start(f32[2,8,4096]{2,1,0:T(8,128)} %get-tuple-element.24), channel_id=1, source_target_pairs={{0,2},{1,3},{2,4},{3,5},{4,6},{5,7},{6,0},{7,1},{8,10},{9,11},{10,... | collective-permute-start | bytes 786440 | tf_op jit(solution)/shard_map/ppermute | solution.py:441
  70.7 28.4 %collective-permute-start.2 = (f32[2,8,4096]{2,1,0:T(8,128)}, f32[2,8,4096]{2,1,0:T(8,128)S(1)}, u32[]{:S(2)}, u32[]{:S(2)}) collective-permute-start(f32[2,8,4096]{2,1,0:T(8,128)} %get-tuple-element.25), channel_id=1, source_target_pairs={{0,3},{1,4},{2,5},{3,6},{4,7},{5,0},{6,1},{7,2},{8,11},{9,12},{10,... | collective-permute-start | bytes 786440 | tf_op jit(solution)/shard_map/ppermute | solution.py:441
  72.8 26.5 %collective-permute-start.3 = (f32[2,8,4096]{2,1,0:T(8,128)}, f32[2,8,4096]{2,1,0:T(8,128)S(1)}, u32[]{:S(2)}, u32[]{:S(2)}) collective-permute-start(f32[2,8,4096]{2,1,0:T(8,128)} %get-tuple-element.26), channel_id=1, source_target_pairs={{0,4},{1,5},{2,6},{3,7},{4,0},{5,1},{6,2},{7,3},{8,12},{9,13},{10,... | collective-permute-start | bytes 786440 | tf_op jit(solution)/shard_map/ppermute | solution.py:441
  74.1 17.6 %collective-permute-start.12 = (f32[16,8,256]{2,1,0:T(8,128)S(1)}, f32[16,8,256]{2,1,0:T(8,128)S(1)}, u32[]{:S(2)}, u32[]{:S(2)}) collective-permute-start(f32[16,8,256]{2,1,0:T(8,128)S(1)} %add.35), channel_id=1, source_target_pairs={{0,2},{1,3},{2,0},{3,1},{4,6},{5,7},{6,4},{7,5},{8,10},{9,11},{10,... | collective-permute-start | bytes 393224 | tf_op jit(solution)/shard_map/ppermute | solution.py:413
  91.7 18.3 %collective-permute-start.4 = (f32[2,8,4096]{2,1,0:T(8,128)}, f32[2,8,4096]{2,1,0:T(8,128)S(1)}, u32[]{:S(2)}, u32[]{:S(2)}) collective-permute-start(f32[2,8,4096]{2,1,0:T(8,128)} %get-tuple-element.27), channel_id=1, source_target_pairs={{0,5},{1,6},{2,7},{3,0},{4,1},{5,2},{6,3},{7,4},{8,13},{9,14},{10,... | collective-permute-start | bytes 786440 | tf_op jit(solution)/shard_map/ppermute | solution.py:441
  96.4 14.3 %collective-permute-start.5 = (f32[2,8,4096]{2,1,0:T(8,128)}, f32[2,8,4096]{2,1,0:T(8,128)S(1)}, u32[]{:S(2)}, u32[]{:S(2)}) collective-permute-start(f32[2,8,4096]{2,1,0:T(8,128)} %get-tuple-element.28), channel_id=1, source_target_pairs={{0,6},{1,7},{2,0},{3,1},{4,2},{5,3},{6,4},{7,5},{8,14},{9,15},{10,... | collective-permute-start | bytes 786440 | tf_op jit(solution)/shard_map/ppermute | solution.py:441
  97.7 13.0 %collective-permute-start.6 = (f32[2,8,4096]{2,1,0:T(8,128)}, f32[2,8,4096]{2,1,0:T(8,128)S(1)}, u32[]{:S(2)}, u32[]{:S(2)}) collective-permute-start(f32[2,8,4096]{2,1,0:T(8,128)} %get-tuple-element.29), channel_id=1, source_target_pairs={{0,7},{1,0},{2,1},{3,2},{4,3},{5,4},{6,5},{7,6},{8,15},{9,8},{10,9... | collective-permute-start | bytes 786440 | tf_op jit(solution)/shard_map/ppermute | solution.py:441
  99.1 39.4 %collective-permute-start.13 = (f32[16,8,256]{2,1,0:T(8,128)S(1)}, f32[16,8,256]{2,1,0:T(8,128)S(1)}, u32[]{:S(2)}, u32[]{:S(2)}) collective-permute-start(f32[16,8,256]{2,1,0:T(8,128)S(1)} %add.36), channel_id=1, source_target_pairs={{0,4},{1,5},{2,6},{3,7},{4,0},{5,1},{6,2},{7,3},{8,12},{9,13},{10,... | collective-permute-start | bytes 393224 | tf_op jit(solution)/shard_map/ppermute | solution.py:413
  119.6 19.6 %collective-permute-start.7 = (f32[2,16,8,256]{3,2,1,0:T(8,128)}, f32[2,16,8,256]{3,2,1,0:T(8,128)S(1)}, u32[]{:S(2)}, u32[]{:S(2)}) collective-permute-start(f32[2,16,8,256]{3,2,1,0:T(8,128)} %get-tuple-element.31), channel_id=1, source_target_pairs={{0,8},{8,16},{16,24},{1,9},{9,17},{17,25},{2,10},{10,18},{18,26},{... | collective-permute-start | bytes 786440 | tf_op jit(solution)/shard_map/ppermute | solution.py:421
  123.1 16.1 %collective-permute-start.8 = (f32[2,16,8,256]{3,2,1,0:T(8,128)}, f32[2,16,8,256]{3,2,1,0:T(8,128)S(1)}, u32[]{:S(2)}, u32[]{:S(2)}) collective-permute-start(f32[2,16,8,256]{3,2,1,0:T(8,128)} %get-tuple-element.32), channel_id=1, source_target_pairs={{8,0},{16,8},{24,16},{9,1},{17,9},{25,17},{10,2},{18,10},{26,18},{... | collective-permute-start | bytes 786440 | tf_op jit(solution)/shard_map/ppermute | solution.py:422
  124.4 19.2 %collective-permute-start.9 = (f32[16,2,8,256]{3,2,1,0:T(8,128)}, f32[16,2,8,256]{3,2,1,0:T(8,128)S(1)}, u32[]{:S(2)}, u32[]{:S(2)}) collective-permute-start(f32[16,2,8,256]{3,2,1,0:T(8,128)} %get-tuple-element.33), channel_id=1, source_target_pairs={{0,1},{1,2},{2,3},{3,4},{4,5},{5,6},{6,7},{7,0},{8,9},{9,10},{10,1... | collective-permute-start | bytes 786440 | tf_op jit(solution)/shard_map/ppermute | solution.py:423
  129.1 14.4 %collective-permute-start.10 = (f32[16,2,8,256]{3,2,1,0:T(8,128)}, f32[16,2,8,256]{3,2,1,0:T(8,128)S(1)}, u32[]{:S(2)}, u32[]{:S(2)}) collective-permute-start(f32[16,2,8,256]{3,2,1,0:T(8,128)} %get-tuple-element.34), channel_id=1, source_target_pairs={{1,0},{2,1},{3,2},{4,3},{5,4},{6,5},{7,6},{0,7},{9,8},{10,9},{11,1... | collective-permute-start | bytes 786440 | tf_op jit(solution)/shard_map/ppermute | solution.py:424
  161.5 1.8 collective-permute-start.18
  164.2 8.1 %collective-permute-start.19 = (f32[16,8,256]{2,1,0:T(8,128)S(1)}, f32[16,8,256]{2,1,0:T(8,128)S(1)}, u32[]{:S(2)}, u32[]{:S(2)}) collective-permute-start(f32[16,8,256]{2,1,0:T(8,128)S(1)} %add.38), channel_id=1, source_target_pairs={{0,2},{1,3},{2,0},{3,1},{4,6},{5,7},{6,4},{7,5},{8,10},{9,11},{10,... | collective-permute-start | bytes 393224 | tf_op jit(solution)/shard_map/ppermute | solution.py:413
  172.3 9.4 %collective-permute-start.20 = (f32[16,8,256]{2,1,0:T(8,128)S(1)}, f32[16,8,256]{2,1,0:T(8,128)S(1)}, u32[]{:S(2)}, u32[]{:S(2)}) collective-permute-start(f32[16,8,256]{2,1,0:T(8,128)S(1)} %add.39), channel_id=1, source_target_pairs={{0,4},{1,5},{2,6},{3,7},{4,0},{5,1},{6,2},{7,3},{8,12},{9,13},{10,... | collective-permute-start | bytes 393224 | tf_op jit(solution)/shard_map/ppermute | solution.py:413
  173.4 9.0 %collective-permute-start.14 = (f32[2,16,8,256]{3,2,1,0:T(8,128)}, f32[2,16,8,256]{3,2,1,0:T(8,128)S(1)}, u32[]{:S(2)}, u32[]{:S(2)}) collective-permute-start(f32[2,16,8,256]{3,2,1,0:T(8,128)} %get-tuple-element.37), channel_id=1, source_target_pairs={{0,8},{8,16},{16,24},{1,9},{9,17},{17,25},{2,10},{10,18},{18,26},{... | collective-permute-start | bytes 786440 | tf_op jit(solution)/shard_map/ppermute | solution.py:421
  176.8 12.1 %collective-permute-start.15 = (f32[2,16,8,256]{3,2,1,0:T(8,128)}, f32[2,16,8,256]{3,2,1,0:T(8,128)S(1)}, u32[]{:S(2)}, u32[]{:S(2)}) collective-permute-start(f32[2,16,8,256]{3,2,1,0:T(8,128)} %get-tuple-element.38), channel_id=1, source_target_pairs={{8,0},{16,8},{24,16},{9,1},{17,9},{25,17},{10,2},{18,10},{26,18},{... | collective-permute-start | bytes 786440 | tf_op jit(solution)/shard_map/ppermute | solution.py:422
  178.1 10.9 %collective-permute-start.16 = (f32[16,2,8,256]{3,2,1,0:T(8,128)}, f32[16,2,8,256]{3,2,1,0:T(8,128)S(1)}, u32[]{:S(2)}, u32[]{:S(2)}) collective-permute-start(f32[16,2,8,256]{3,2,1,0:T(8,128)} %get-tuple-element.39), channel_id=1, source_target_pairs={{0,1},{1,2},{2,3},{3,4},{4,5},{5,6},{6,7},{7,0},{8,9},{9,10},{10,1... | collective-permute-start | bytes 786440 | tf_op jit(solution)/shard_map/ppermute | solution.py:423
  178.2 10.8 %collective-permute-start.17 = (f32[16,2,8,256]{3,2,1,0:T(8,128)}, f32[16,2,8,256]{3,2,1,0:T(8,128)S(1)}, u32[]{:S(2)}, u32[]{:S(2)}) collective-permute-start(f32[16,2,8,256]{3,2,1,0:T(8,128)} %get-tuple-element.40), channel_id=1, source_target_pairs={{1,0},{2,1},{3,2},{4,3},{5,4},{6,5},{7,6},{0,7},{9,8},{10,9},{11,1... | collective-permute-start | bytes 786440 | tf_op jit(solution)/shard_map/ppermute | solution.py:424
  (16 other events, 140.7 us)

commit v2 on v0

v2 whole, which is shorter than its diff:
```python
import functools

import jax
import jax.numpy as jnp
from jax import lax
from jax.experimental import pallas as pl
from jax.experimental.pallas import tpu as pltpu
from jax.sharding import PartitionSpec as P

EDGE = 16
CHANNELS = 8
CAPACITY = 2
LANES = 128

time_step = 0.02
signal_speed = 2.0
shear_rate = -1.5

ANY = pl.BlockSpec(memory_space=pl.ANY)
SMEM = pl.BlockSpec(memory_space=pltpu.SMEM)
HBM = pl.BlockSpec(memory_space=pltpu.HBM)
VMEM = pl.BlockSpec(memory_space=pltpu.VMEM)
MIB = 1 << 20
COST = pl.CostEstimate(flops=0, bytes_accessed=0, transcendentals=0)
F32 = jnp.float32


def minmod(a, b):
    return jnp.maximum(jnp.minimum(a, b), jnp.minimum(jnp.maximum(a, b), 0.0))


def lane_group():
    return lax.broadcasted_iota(jnp.int32, (CHANNELS, LANES), 1) // EDGE


def swap_groups(rows, group):
    rows = list(rows)
    for bit in (1, 2, 4):
        low = (group & bit) == 0
        shift = EDGE * bit
        for i in range(8):
            if i & bit:
                continue
            a, b = rows[i], rows[i + bit]
            rows[i] = jnp.where(low, a, pltpu.roll(b, shift, 1))
            rows[i + bit] = jnp.where(low, pltpu.roll(a, LANES - shift, 1), b)
    return rows


def own_place():
    azi_count = lax.axis_size("azi")
    azi = lax.axis_index("azi")
    return azi, lax.axis_index("rad") * azi_count + azi


def pack_kernel(azi_count, block_count, assignment, blocks, *refs):
    outs = refs[:azi_count]
    table, sent, fill, sems = refs[azi_count:]
    azi, own = own_place()
    first = own * block_count
    row_first = (own - azi) * block_count
    spots = azi_count * CAPACITY
    for i in range(azi_count):
        fill[i] = 0
    for i in range(spots):
        sent[i] = 0
        table[i] = -1

    def note(j, carry):
        device = lax.div(assignment[first + j], block_count)
        shift = lax.rem(lax.rem(device, azi_count) - azi + azi_count, azi_count)
        k = fill[shift]
        sent[shift * CAPACITY + k] = j
        fill[shift] = k + 1
        return carry

    lax.fori_loop(0, block_count, note, 0)
    copies = []
    for shift in range(azi_count):
        for k in range(CAPACITY):
            spot = shift * CAPACITY + k
            copy = pltpu.make_async_copy(blocks.at[sent[spot]], outs[shift].at[k], sems.at[spot])
            copy.start()
            copies.append(copy)

    def source(s, carry):
        shift = lax.rem(azi - s + azi_count, azi_count)
        start = row_first + s * block_count
        found = jnp.int32(0)
        for j in range(block_count):
            slot = assignment[start + j] - first
            ours = (slot >= 0) & (slot < block_count)
            table[jnp.where(ours, shift * CAPACITY + found, spots)] = slot
            found = found + ours.astype(jnp.int32)
        return carry

    lax.fori_loop(0, azi_count, source, 0)
    for copy in copies:
        copy.wait()


def pack(assignment, blocks, azi_count):
    shape = (CAPACITY,) + blocks.shape[1:]
    spots = azi_count * CAPACITY
    *packed, table = pl.pallas_call(
        functools.partial(pack_kernel, azi_count, blocks.shape[0]),
        out_shape=[pltpu.VMEM(shape, F32)] * azi_count
        + [jax.ShapeDtypeStruct((spots + 1,), jnp.int32)],
        in_specs=[SMEM, HBM],
        out_specs=[VMEM] * azi_count + [SMEM],
        scratch_shapes=[
            pltpu.SMEM((spots,), jnp.int32),
            pltpu.SMEM((azi_count,), jnp.int32),
            pltpu.SemaphoreType.DMA((spots,)),
        ],
        compiler_params=pltpu.CompilerParams(vmem_limit_bytes=4 * MIB),
        name="pack",
    )(assignment, pltpu.with_memory_space_constraint(blocks, pltpu.HBM))
    return packed, table


def coefficients(block_count, levels, damping, coupling, weights, ratio, relax):
    group = lane_group()
    for d in range(3):
        weights[:, d * CHANNELS : (d + 1) * CHANNELS] = 0.5 * coupling[d]
    for half in range(block_count // 8):
        factor = jnp.zeros((CHANNELS, LANES), F32)
        for i in range(8):
            level = levels[half * 8 + i]
            scale = jnp.where(level == 0, 1.0, jnp.where(level == 1, 2.0, 4.0)) * time_step
            factor = jnp.where(group == i, scale, factor)
        ratio[:, half * LANES : (half + 1) * LANES] = factor
    channel = lax.broadcasted_iota(jnp.int32, relax.shape, 0)
    pull = jnp.zeros(relax.shape, F32)
    for c in range(CHANNELS):
        pull = jnp.where(channel == c, time_step * damping[c], pull)
    relax[...] = pull


def unpack_kernel(azi_count, block_count, table, levels, damping, coupling, *refs):
    arrived = refs[:azi_count]
    field, rad_head, rad_tail, azi_head, azi_tail, sums, held, weights, ratio, relax, sems = refs[
        azi_count:
    ]

    def copy_of(shift, k):
        spot = shift * CAPACITY + k
        slot = jnp.maximum(table[spot], 0)
        return pltpu.make_async_copy(arrived[shift].at[k], held.at[slot], sems.at[spot])

    spots = [(shift, k) for shift in range(azi_count) for k in range(CAPACITY)]
    for shift, k in spots:

        @pl.when(table[shift * CAPACITY + k] >= 0)
        def _(shift=shift, k=k):
            copy_of(shift, k).start()

    coefficients(block_count, levels, damping, coupling, weights, ratio, relax)
    for shift, k in spots:

        @pl.when(table[shift * CAPACITY + k] >= 0)
        def _(shift=shift, k=k):
            copy_of(shift, k).wait()

    group = lane_group()

    def row(x, carry):
        base = x * (EDGE * EDGE)
        for half in range(block_count // 8):
            lanes = slice(half * LANES, (half + 1) * LANES)
            running = None
            for upper in range(2):
                at = pl.ds(pl.multiple_of(base + upper * LANES, LANES), LANES)
                tiles = swap_groups([held[half * 8 + i, :, at] for i in range(8)], group)
                for i in range(8):
                    field[x, upper * 8 + i, :, lanes] = tiles[i]
                    running = tiles[i] if running is None else running + tiles[i]
                for i in range(2):
                    if upper == 0:
                        azi_head[x, i, :, lanes] = tiles[i]
                    else:
                        azi_tail[x, i, :, lanes] = tiles[6 + i]
            sums[x, :, lanes] = running
        return carry

    lax.fori_loop(0, EDGE, row, 0)
    rad_head[...] = field[0:2]
    rad_tail[...] = field[EDGE - 2 : EDGE]


def field_shapes(vertical):
    rad = pltpu.VMEM((2, EDGE, CHANNELS, vertical), F32)
    azi = pltpu.VMEM((EDGE, 2, CHANNELS, vertical), F32)
    field = pltpu.VMEM((EDGE, EDGE, CHANNELS, vertical), F32)
    return [field, rad, rad, azi, azi, pltpu.VMEM((EDGE, CHANNELS, vertical), F32)]


def unpack(table, levels, damping, coupling, arrived, block_shape):
    azi_count = len(arrived)
    vertical = block_shape[0] * EDGE
    return pl.pallas_call(
        functools.partial(unpack_kernel, azi_count, block_shape[0]),
        out_shape=field_shapes(vertical)
        + [
            pltpu.VMEM(block_shape, F32),
            pltpu.VMEM((CHANNELS, 3 * CHANNELS), F32),
            pltpu.VMEM((CHANNELS, vertical), F32),
            pltpu.VMEM((CHANNELS, vertical), F32),
        ],
        in_specs=[SMEM, SMEM, SMEM, VMEM] + [ANY] * azi_count,
        out_specs=[VMEM] * 10,
        scratch_shapes=[pltpu.SemaphoreType.DMA((azi_count * CAPACITY,))],
        compiler_params=pltpu.CompilerParams(vmem_limit_bytes=16 * MIB),
        name="unpack",
    )(table, levels, damping, coupling, *arrived)


def shear_of(x):
    cell = (lax.axis_index("rad") * EDGE + x).astype(F32)
    return shear_rate * ((cell + 0.5) * (2.0 / (EDGE * lax.axis_size("rad"))) - 1.0)


def mean_of(sums, x):
    return sums[x] * (1.0 / (EDGE * lax.axis_size("azi")))


def start_radius(get, x, y, carry_slope, carry_plus):
    u = [get(x + i, y) for i in (-2, -1, 0, 1)]
    e = [u[i + 1] - u[i] for i in range(3)]
    before, slope = minmod(e[0], e[1]), minmod(e[1], e[2])
    carry_slope[y] = slope
    carry_plus[y] = e[1] + 0.5 * (slope - before)


def stage_row(get, x, cells, carry_slope, carry_plus, left, step, pull, outs):
    settled, sums_azi, jumps_azi = outs
    low = cells[0]
    u = [get(x, low + i) for i in (-2, -1, 0, 1)]
    vertical = u[0].shape[-1]
    e = [u[i + 1] - u[i] for i in range(3)]
    before, slope = minmod(e[0], e[1]), minmod(e[1], e[2])
    plus = e[1] + 0.5 * (slope - before)
    cell, upper, face = u[2], u[3], e[2]
    for y in cells:
        beyond = get(x, y + 2)
        face_next = beyond - upper
        slope_next = minmod(face, face_next)
        k = 0.5 * (slope_next - slope)
        minus = face - k
        sum_azi = plus + minus
        jump_azi = minus - plus
        plus = face + k
        slope, face = slope_next, face_next
        r1, r2 = get(x + 1, y), get(x + 2, y)
        e1 = r1 - cell
        s1 = minmod(e1, r2 - r1)
        k = 0.5 * (s1 - carry_slope[y])
        minus = e1 - k
        before = carry_plus[y]
        sum_rad = before + minus
        jump = minus - before
        carry_plus[y] = e1 + k
        carry_slope[y] = s1
        f1 = pltpu.roll(cell, vertical - 1, 1) - cell
        g1 = minmod(pltpu.roll(f1, 1, 1), f1)
        k = 0.5 * (pltpu.roll(g1, vertical - 1, 1) - g1)
        minus = f1 - k
        before = pltpu.roll(f1 + k, 1, 1)
        sum_vert = before + minus
        jump = jump + (minus - before)
        stack = []
        for part in (sum_rad, sum_azi, sum_vert):
            high = part.astype(jnp.bfloat16).astype(F32)
            stack += [high, part - high]
        stack = jnp.concatenate(stack, axis=0).astype(jnp.bfloat16)
        pair = lax.dot_general(left, stack, (((1,), (0,)), ((), ())), preferred_element_type=F32)
        flux = (pair[:CHANNELS] + pair[CHANNELS:]) - jump
        settled[x, y] = cell - step * flux - pull * cell
        sums_azi[x, y] = step * sum_azi
        jumps_azi[x, y] = step * jump_azi
        cell, upper = upper, beyond


def split_weights(weights):
    w = weights[...]
    high = w.astype(jnp.bfloat16).astype(F32)
    both = jnp.concatenate([high, w - high], axis=0)
    columns = [both[:, CHANNELS * (i // 2) : CHANNELS * (i // 2 + 1)] for i in range(6)]
    return jnp.concatenate(columns, axis=1).astype(jnp.bfloat16)


def sweep(get, rows, runs, carry_slope, carry_plus, left, ratio, relax, outs):
    for cells in runs:
        for y in cells:
            start_radius(get, rows[0], y, carry_slope, carry_plus)

    def row(x, carry):
        for cells in runs:
            stage_row(
                get, x, cells, carry_slope, carry_plus, left, ratio[...], relax[...], outs
            )
        return carry

    lax.fori_loop(rows[0], rows[1], row, 0)


INNER = range(2, EDGE - 2)
HEAD, TAIL = range(0, 2), range(EDGE - 2, EDGE)


def inner_kernel(field, weights, ratio, relax, *refs):
    outs, carries = refs[:3], refs[3:]

    def get(x, y):
        return field[x, y]

    sweep(get, (2, EDGE - 2), (INNER,), *carries, split_weights(weights), ratio, relax, outs)


def inner_stage(field, weights, ratio, relax):
    vertical = field.shape[-1]
    return pl.pallas_call(
        inner_kernel,
        out_shape=[pltpu.VMEM(field.shape, F32)] * 3,
        in_specs=[VMEM] * 4,
        out_specs=[VMEM] * 3,
        scratch_shapes=[pltpu.VMEM((EDGE, CHANNELS, vertical), F32)] * 2,
        compiler_params=pltpu.CompilerParams(vmem_limit_bytes=16 * MIB),
        cost_estimate=COST,
        name="inner_stage",
    )(field, weights, ratio, relax)


def outer_kernel(
    field, low_rad, high_rad, low_azi, high_azi, weights, ratio, relax, one, two, three, *refs
):
    del one, two, three
    outs = refs[:3]
    padded, carry_slope, carry_plus, sems = refs[3:]
    load_padded(field, low_rad, high_rad, low_azi, high_azi, padded, sems)

    def get(x, y):
        return padded[x + 2, y + 2]

    rest = (carry_slope, carry_plus, split_weights(weights), ratio, relax, outs)
    sweep(get, (0, 2), (range(EDGE),), *rest)
    sweep(get, (2, EDGE - 2), (HEAD, TAIL), *rest)
    sweep(get, (EDGE - 2, EDGE), (range(EDGE),), *rest)


def outer_stage(field, halos, weights, ratio, relax, parts):
    vertical = field.shape[-1]
    return pl.pallas_call(
        outer_kernel,
        out_shape=[pltpu.VMEM(field.shape, F32)] * 3,
        in_specs=[ANY] * 5 + [VMEM] * 6,
        out_specs=[VMEM] * 3,
        scratch_shapes=[
            pltpu.VMEM((EDGE + 4, EDGE + 4, CHANNELS, vertical), F32),
            pltpu.VMEM((EDGE, CHANNELS, vertical), F32),
            pltpu.VMEM((EDGE, CHANNELS, vertical), F32),
            pltpu.SemaphoreType.DMA((5,)),
        ],
        input_output_aliases={8: 0, 9: 1, 10: 2},
        compiler_params=pltpu.CompilerParams(vmem_limit_bytes=16 * MIB),
        cost_estimate=COST,
        name="outer_stage",
    )(field, *halos, weights, ratio, relax, *parts)


def speeds(average, x):
    velocity = jnp.broadcast_to(average[2:3, :], average.shape) + shear_of(x)
    return 0.5 * velocity, 0.5 * jnp.abs(velocity) + 0.5 * signal_speed


def split_weights(weights):
    w = weights[...]
    high = w.astype(jnp.bfloat16).astype(F32)
    both = jnp.concatenate([high, w - high], axis=0)
    columns = [both[:, CHANNELS * (i // 2) : CHANNELS * (i // 2 + 1)] for i in range(6)]
    return jnp.concatenate(columns, axis=1).astype(jnp.bfloat16)


def load_padded(field, low_rad, high_rad, low_azi, high_azi, padded, sems):
    middle = pl.ds(2, EDGE)
    copies = [
        (field, padded.at[middle, middle]),
        (low_rad, padded.at[pl.ds(0, 2), middle]),
        (high_rad, padded.at[pl.ds(EDGE + 2, 2), middle]),
        (low_azi, padded.at[middle, pl.ds(0, 2)]),
        (high_azi, padded.at[middle, pl.ds(EDGE + 2, 2)]),
    ]
    copies = [pltpu.make_async_copy(a, b, sems.at[i]) for i, (a, b) in enumerate(copies)]
    for copy in copies:
        copy.start()
    for copy in copies:
        copy.wait()


def join_kernel(
    settled, sums_azi, jumps_azi, column, relax,
    state, rad_head, rad_tail, azi_head, azi_tail, sums,
):
    def row(x, carry):
        average = mean_of(column, x)
        half_velocity, half_signal = speeds(average, x)
        pulled = relax[...] * average
        running = None
        for y in range(EDGE):
            value = (
                (settled[x, y] + pulled)
                - half_velocity * sums_azi[x, y]
                + half_signal * jumps_azi[x, y]
            )
            state[x, y] = value
            if y < 2:
                azi_head[x, y] = value
            if y >= EDGE - 2:
                azi_tail[x, y - (EDGE - 2)] = value
            running = value if running is None else running + value
        sums[x] = running
        return carry

    lax.fori_loop(0, EDGE, row, 0)
    rad_head[...] = state[0:2]
    rad_tail[...] = state[EDGE - 2 : EDGE]


def join_stage(parts, column, relax):
    vertical = parts[0].shape[-1]
    return pl.pallas_call(
        join_kernel,
        out_shape=field_shapes(vertical),
        in_specs=[VMEM] * 5,
        out_specs=[VMEM] * 6,
        compiler_params=pltpu.CompilerParams(vmem_limit_bytes=8 * MIB),
        name="join_stage",
    )(*parts, column, relax)


def final_kernel(
    held, settled, sums_azi, jumps_azi, column, relax,
    final, tendency, final_rows, tendency_rows, out_sems,
):
    group = lane_group()
    halves = held.shape[0] // 8

    def out_copies(x):
        at = pl.ds(pl.multiple_of(x * (EDGE * EDGE), LANES), EDGE * EDGE)
        return [
            pltpu.make_async_copy(a.at[:, :, at], b.at[:, :, at], out_sems.at[i, x])
            for i, (a, b) in enumerate(((final_rows, final), (tendency_rows, tendency)))
        ]

    def row(x, carry):
        average = mean_of(column, x)
        half_velocity, half_signal = speeds(average, x)
        pulled = relax[...] * average
        base = x * (EDGE * EDGE)
        for half in range(halves):
            lanes = slice(half * LANES, (half + 1) * LANES)
            for upper in range(2):
                at = pl.ds(pl.multiple_of(base + upper * LANES, LANES), LANES)
                results = []
                for i in range(8):
                    y = upper * 8 + i
                    results.append(
                        (settled[x, y, :, lanes] + pulled[:, lanes])
                        - half_velocity[:, lanes] * sums_azi[x, y, :, lanes]
                        + half_signal[:, lanes] * jumps_azi[x, y, :, lanes]
                    )
                for i, tile in enumerate(swap_groups(results, group)):
                    start = held[half * 8 + i, :, at]
                    change = 0.5 * (tile - start)
                    final_rows[half * 8 + i, :, at] = start + change
                    tendency_rows[half * 8 + i, :, at] = change * (1.0 / time_step)
        for copy in out_copies(x):
            copy.start()
        return carry

    lax.fori_loop(0, EDGE, row, 0)

    def finish_row(x, carry):
        for copy in out_copies(x):
            copy.wait()
        return carry

    lax.fori_loop(0, EDGE, finish_row, 0)


def final_stage(held, parts, column, relax):
    return pl.pallas_call(
        final_kernel,
        out_shape=[jax.ShapeDtypeStruct(held.shape, F32)] * 2,
        in_specs=[VMEM] * 6,
        out_specs=[HBM] * 2,
        scratch_shapes=[
            pltpu.VMEM(held.shape, F32),
            pltpu.VMEM(held.shape, F32),
            pltpu.SemaphoreType.DMA((2, EDGE)),
        ],
        compiler_params=pltpu.CompilerParams(vmem_limit_bytes=8 * MIB),
        name="final_stage",
    )(held, *parts, column, relax)


def sum_azi(values, beside):
    count = lax.axis_size("azi")
    if count & (count - 1):
        return lax.psum(values, "azi"), beside
    step = 1
    while step < count:
        other = lax.ppermute(values, "azi", [(i, i ^ step) for i in range(count)])
        if step == 2:
            other, beside = lax.optimization_barrier((other, beside))
        values = values + other
        step *= 2
    return values, beside


def exchange(rad_head, rad_tail, azi_head, azi_tail):
    rad, azi = lax.axis_size("rad"), lax.axis_size("azi")
    return (
        lax.ppermute(rad_tail, "rad", [(i, i + 1) for i in range(rad - 1)]),
        lax.ppermute(rad_head, "rad", [(i + 1, i) for i in range(rad - 1)]),
        lax.ppermute(azi_tail, "azi", [(i, (i + 1) % azi) for i in range(azi)]),
        lax.ppermute(azi_head, "azi", [((i + 1) % azi, i) for i in range(azi)]),
    )


def on_device(blocks, assignment, levels, coupling, damping):
    azi_count = lax.axis_size("azi")
    packed, table = pack(assignment, blocks, azi_count)
    arrived = [packed[0]] + [
        lax.ppermute(packed[d], "azi", [(i, (i + d) % azi_count) for i in range(azi_count)])
        for d in range(1, azi_count)
    ]
    start, *edges, sums, held, weights, ratio, relax = unpack(
        table, levels, damping, coupling, arrived, blocks.shape
    )

    def section(field, edges, sums):
        halos = exchange(*edges)
        parts = inner_stage(field, weights, ratio, relax)
        column, parts = sum_azi(sums, parts)
        return outer_stage(field, halos, weights, ratio, relax, parts), column

    parts, column = section(start, edges, sums)
    state, *edges, sums = join_stage(parts, column, relax)
    parts, column = section(state, edges, sums)
    return final_stage(held, parts, column, relax)


def solution(mesh):
    in_specs = (P(("rad", "azi"), None, None), P(), P(("rad", "azi")), P(), P())
    out_specs = (P(("rad", "azi"), None, None), P(("rad", "azi"), None, None))
    return jax.shard_map(
        on_device, mesh=mesh, in_specs=in_specs, out_specs=out_specs, check_vma=False
    )
```

time: 485 us -> 120 us (0.25)
  waiting for transfers between devices: 219 us -> 25 us
  local copies, waits for them, and re-layouts: 165 us -> 0.69 us
  Pallas kernels: 0 us -> 44 us
  other arithmetic: 37.9 us -> 0.11 us
  starting transfers between devices: 15.5 us -> 48.8 us
  matrix products: 30 us -> 0 us
  between operations: 14.4 us -> 0.89 us
    all_gather x1 -> x0, waiting for transfers between devices: 153 us -> none  [on_device(): arrived = lax.all_gather(blocks, 'azi', axis=0, tiled=True)]
    reshape x6 -> x0, local copies, waits for them, and re-layouts: 82.4 us -> none  [the longest x2 30.6 us: to_blocks(): split_field.transpose(3, 0, 1, 2, 4)]
    psum x2 -> x0, waiting for transfers between devices: 64.6 us -> none  [sum_columns(): return lax.psum(jnp.sum(state_field, axis=2), 'azi') / azi_cells]
    transpose x3 -> x0, local copies, waits for them, and re-layouts: 53.5 us -> none  [the longest x2 35.8 us: to_blocks(): split_field.transpose(3, 0, 1, 2, 4)]
    pallas_call x0 -> x8, Pallas kernels: none -> 44 us  [the longest x2 15.2 us: outer_stage(): pl.pallas_call(outer_kernel, out_shape=[pltpu.VMEM(field.shape, F32)] * 3...]
    ppermute x8 -> x21, starting transfers between devices: 15.3 us -> 48.8 us  [the longest x7 15.6 us: on_device(): lax.ppermute(packed[d], 'azi', [(i, (i + d) % azi_count) for i in range(a...]
    dot_general x6 -> x0, matrix products: 30 us -> none  [flux_change(): jnp.einsum('ce,e...->c...', matrix, summed, precision=lax.Precision.HIGHEST)]
    ppermute x8 -> x21, waiting for transfers between devices: 0.02 us -> 25 us  [the longest x7 21.7 us: on_device(): lax.ppermute(packed[d], 'azi', [(i, (i + d) % azi_count) for i in range(a...]
  transfers between devices with their start and end apart: 11 -> 21, of which waited for: 3 -> 6; matrix products, arithmetic and copies ran while one was open for 7% -> 0% of each run, Pallas kernels for 0% -> 23%
where the time goes in v2:
time: 120 us
  starting transfers between devices  48.8 us (41%)
  Pallas kernels  44 us (37%)
  waiting for transfers between devices  25 us (21%)
    ppermute x7, waiting for transfers between devices, on_device(): lax.ppermute(packed[d], 'azi', [(i, (i + d) % azi_count) for i in range(a...  21.7 us
    ppermute x7, starting transfers between devices, on_device(): lax.ppermute(packed[d], 'azi', [(i, (i + d) % azi_count) for i in range(a...  15.6 us
    pallas_call x2, Pallas kernels, outer_stage(): pl.pallas_call(outer_kernel, out_shape=[pltpu.VMEM(field.shape, F32)] * 3...  15.2 us
    ppermute x6, starting transfers between devices, sum_azi(): other = lax.ppermute(values, 'azi', [(i, i ^ step) for i in range(count)])  15.2 us
    pallas_call x2, Pallas kernels, inner_stage(): pl.pallas_call(inner_kernel, out_shape=[pltpu.VMEM(field.shape, F32)] * 3...  11.9 us
    ppermute x2, starting transfers between devices, exchange(): lax.ppermute(rad_tail, 'rad', [(i, i + 1) for i in range(rad - 1)])  8.4 us
    pallas_call x1, Pallas kernels, unpack(): pl.pallas_call(functools.partial(unpack_kernel, azi_count, block_shape[0]...  7.68 us
    ppermute x2, starting transfers between devices, exchange(): lax.ppermute(azi_head, 'azi', [((i + 1) % azi, i) for i in range(azi)])  7.08 us
  transfers between devices with their start and end apart: 21, of which 6 were waited for; matrix products, arithmetic and copies ran while one was open for 0% of the time, Pallas kernels for 23%

profile of v2, /device:TPU:0, one launch (start us, length us, event | category | flops | bytes accessed | tf_op | source)
XLA Modules:
  0.0 119.6 jit_solution(17943834981892266047)
XLA Ops:
  1.3 3.3 %pack.1 = (f32[2,8,4096]{2,1,0:T(8,128)S(1)}, f32[2,8,4096]{2,1,0:T(8,128)S(1)}, f32[2,8,4096]{2,1,0:T(8,128)S(1)}, f32[2,8,4096]{2,1,0:T(8,128)S(1)}, f32[2,8,4...) custom-call(s32[512]{0:T(512)S(1)} %copy-done.1, ...), custom_call_target="tpu_custom_call" | custom-call | tf_op jit(solution)/shard_map/pack/pallas_call | solution.py:105
  5.1 2.6 %collective-permute-start.1 = (f32[2,8,4096]{2,1,0:T(8,128)S(1)}, f32[2,8,4096]{2,1,0:T(8,128)S(1)}, u32[]{:S(2)}, u32[]{:S(2)}) collective-permute-start(f32[2,8,4096]{2,1,0:T(8,128)S(1)} %get-tuple-element.50), channel_id=1, source_target_pairs={{0,2},{1,3},{2,4},{3,5},{4,6},{5,7},{6,0},{7,1},{8,10},{9,11},{10,... | collective-permute-start | bytes 786440 | tf_op jit(solution)/shard_map/ppermute | solution.py:535
  7.8 2.5 %collective-permute-start.2 = (f32[2,8,4096]{2,1,0:T(8,128)S(1)}, f32[2,8,4096]{2,1,0:T(8,128)S(1)}, u32[]{:S(2)}, u32[]{:S(2)}) collective-permute-start(f32[2,8,4096]{2,1,0:T(8,128)S(1)} %get-tuple-element.51), channel_id=1, source_target_pairs={{0,3},{1,4},{2,5},{3,6},{4,7},{5,0},{6,1},{7,2},{8,11},{9,12},{10,... | collective-permute-start | bytes 786440 | tf_op jit(solution)/shard_map/ppermute | solution.py:535
  10.3 1.2 %collective-permute-start.3 = (f32[2,8,4096]{2,1,0:T(8,128)S(1)}, f32[2,8,4096]{2,1,0:T(8,128)S(1)}, u32[]{:S(2)}, u32[]{:S(2)}) collective-permute-start(f32[2,8,4096]{2,1,0:T(8,128)S(1)} %get-tuple-element.52), channel_id=1, source_target_pairs={{0,4},{1,5},{2,6},{3,7},{4,0},{5,1},{6,2},{7,3},{8,12},{9,13},{10,... | collective-permute-start | bytes 786440 | tf_op jit(solution)/shard_map/ppermute | solution.py:535
  12.7 2.6 %collective-permute-done.refs_1_ = f32[2,8,4096]{2,1,0:T(8,128)S(1)} collective-permute-done((f32[2,8,4096]{2,1,0:T(8,128)S(1)}, f32[2,8,4096]{2,1,0:T(8,128)S(1)}, u32[]{:S(2)}, u32[]{:S(2)}) %collective-permute-start) | collective-permute-done | bytes 262176 | tf_op jit(solution)/shard_map/ppermute | solution.py:535
  15.3 2.5 %collective-permute-start.5 = (f32[2,8,4096]{2,1,0:T(8,128)S(1)}, f32[2,8,4096]{2,1,0:T(8,128)S(1)}, u32[]{:S(2)}, u32[]{:S(2)}) collective-permute-start(f32[2,8,4096]{2,1,0:T(8,128)S(1)} %get-tuple-element.54), channel_id=1, source_target_pairs={{0,6},{1,7},{2,0},{3,1},{4,2},{5,3},{6,4},{7,5},{8,14},{9,15},{10,... | collective-permute-start | bytes 786440 | tf_op jit(solution)/shard_map/ppermute | solution.py:535
  17.7 5.0 %collective-permute-start.6 = (f32[2,8,4096]{2,1,0:T(8,128)S(1)}, f32[2,8,4096]{2,1,0:T(8,128)S(1)}, u32[]{:S(2)}, u32[]{:S(2)}) collective-permute-start(f32[2,8,4096]{2,1,0:T(8,128)S(1)} %get-tuple-element.55), channel_id=1, source_target_pairs={{0,7},{1,0},{2,1},{3,2},{4,3},{5,4},{6,5},{7,6},{8,15},{9,8},{10,9... | collective-permute-start | bytes 786440 | tf_op jit(solution)/shard_map/ppermute | solution.py:535
  22.8 15.7 %collective-permute-done.2.refs_3_ = f32[2,8,4096]{2,1,0:T(8,128)S(1)} collective-permute-done((f32[2,8,4096]{2,1,0:T(8,128)S(1)}, f32[2,8,4096]{2,1,0:T(8,128)S(1)}, u32[]{:S(2)}, u32[]{:S(2)}) %collective-permute-start.2) | collective-permute-done | bytes 262176 | tf_op jit(solution)/shard_map/ppermute | solution.py:535
  38.6 3.3 %collective-permute-done.6.refs_7_ = f32[2,8,4096]{2,1,0:T(8,128)S(1)} collective-permute-done((f32[2,8,4096]{2,1,0:T(8,128)S(1)}, f32[2,8,4096]{2,1,0:T(8,128)S(1)}, u32[]{:S(2)}, u32[]{:S(2)}) %collective-permute-start.6) | collective-permute-done | bytes 262176 | tf_op jit(solution)/shard_map/ppermute | solution.py:535
  42.0 7.7 %unpack.1 = (f32[16,16,8,256]{3,2,1,0:T(8,128)S(1)}, f32[2,16,8,256]{3,2,1,0:T(8,128)S(1)}, f32[2,16,8,256]{3,2,1,0:T(8,128)S(1)}, f32[16,2,8,256]{3,2,1,0:T(8,1...) custom-call(s32[17]{0:T(128)S(1)} %get-tuple-element.47.table, ...), custom_call_target="tpu_custom_call" | custom-call | tf_op jit(solution)/shard_map/unpack/pallas_call | solution.py:201
  49.7 2.2 %collective-permute-start.11 = (f32[16,8,256]{2,1,0:T(8,128)S(1)}, f32[16,8,256]{2,1,0:T(8,128)S(1)}, u32[]{:S(2)}, u32[]{:S(2)}) collective-permute-start(f32[16,8,256]{2,1,0:T(8,128)S(1)} %get-tuple-element.65), channel_id=1, source_target_pairs={{0,1},{1,0},{2,3},{3,2},{4,5},{5,4},{6,7},{7,6},{8,9},{9,8},{10,11... | collective-permute-start | bytes 393224 | tf_op jit(solution)/shard_map/ppermute | solution.py:513
  51.9 3.9 %collective-permute-start.7 = (f32[2,16,8,256]{3,2,1,0:T(8,128)S(1)}, f32[2,16,8,256]{3,2,1,0:T(8,128)S(1)}, u32[]{:S(2)}, u32[]{:S(2)}) collective-permute-start(f32[2,16,8,256]{3,2,1,0:T(8,128)S(1)} %get-tuple-element.58), channel_id=1, source_target_pairs={{0,8},{8,16},{16,24},{1,9},{9,17},{17,25},{2,10},{10,18},{18,26},{... | collective-permute-start | bytes 786440 | tf_op jit(solution)/shard_map/ppermute | solution.py:524
  55.8 1.3 %collective-permute-start.8 = (f32[2,16,8,256]{3,2,1,0:T(8,128)S(1)}, f32[2,16,8,256]{3,2,1,0:T(8,128)S(1)}, u32[]{:S(2)}, u32[]{:S(2)}) collective-permute-start(f32[2,16,8,256]{3,2,1,0:T(8,128)S(1)} %get-tuple-element.59), channel_id=1, source_target_pairs={{8,0},{16,8},{24,16},{9,1},{17,9},{25,17},{10,2},{18,10},{26,18},{... | collective-permute-start | bytes 786440 | tf_op jit(solution)/shard_map/ppermute | solution.py:525
  57.1 11.7 %collective-permute-start.12 = (f32[16,8,256]{2,1,0:T(8,128)S(1)}, f32[16,8,256]{2,1,0:T(8,128)S(1)}, u32[]{:S(2)}, u32[]{:S(2)}) collective-permute-start(f32[16,8,256]{2,1,0:T(8,128)S(1)} %add.18), channel_id=1, source_target_pairs={{0,2},{1,3},{2,0},{3,1},{4,6},{5,7},{6,4},{7,5},{8,10},{9,11},{10,... | collective-permute-start | bytes 393224 | tf_op jit(solution)/shard_map/ppermute | solution.py:513
  68.9 3.5 %collective-permute-start.10 = (f32[16,2,8,256]{3,2,1,0:T(8,128)S(1)}, f32[16,2,8,256]{3,2,1,0:T(8,128)S(1)}, u32[]{:S(2)}, u32[]{:S(2)}) collective-permute-start(f32[16,2,8,256]{3,2,1,0:T(8,128)S(1)} %get-tuple-element.61), channel_id=1, source_target_pairs={{1,0},{2,1},{3,2},{4,3},{5,4},{6,5},{7,6},{0,7},{9,8},{10,9},{11,1... | collective-permute-start | bytes 786440 | tf_op jit(solution)/shard_map/ppermute | solution.py:527
  72.4 6.0 %inner_stage.2 = (f32[16,16,8,256]{3,2,1,0:T(8,128)S(1)}, f32[16,16,8,256]{3,2,1,0:T(8,128)S(1)}, f32[16,16,8,256]{3,2,1,0:T(8,128)S(1)}) custom-call(f32[16,16,8,256]{3,2,1,0:T(8,128)S(1)} %get-tuple-element.57.field, f32[8,24]{1,0:T(8,128)S(1)} %get-tuple-element.62.weights, f32[8,256]{1,0:T(8,128)S(1)} %get-tuple-element.63.ratio, ...), custom_call_target="tpu_custom_call" | custom-call | tf_op jit(solution)/shard_map/inner_stage/pallas_call | solution.py:322
  79.1 7.6 %outer_stage.2 = (f32[16,16,8,256]{3,2,1,0:T(8,128)S(1)}, f32[16,16,8,256]{3,2,1,0:T(8,128)S(1)}, f32[16,16,8,256]{3,2,1,0:T(8,128)S(1)}) custom-call(f32[16,16,8,256]{3,2,1,0:T(8,128)S(1)} %get-tuple-element.57.field, f32[2,16,8,256]{3,2,1,0:T(8,128)S(1)} %collective-permute-done.7.low_rad, ...), custom_call_target="tpu_custom_call", output_to_operand_aliasing={{0}: (8, {}), {1}: (9, {}), {2}: (10, {})} | custom-call | tf_op jit(solution)/shard_map/outer_stage/pallas_call | solution.py:353
  87.5 4.5 %collective-permute-start.14 = (f32[2,16,8,256]{3,2,1,0:T(8,128)S(1)}, f32[2,16,8,256]{3,2,1,0:T(8,128)S(1)}, u32[]{:S(2)}, u32[]{:S(2)}) collective-permute-start(f32[2,16,8,256]{3,2,1,0:T(8,128)S(1)} %get-tuple-element.77), channel_id=1, source_target_pairs={{0,8},{8,16},{16,24},{1,9},{9,17},{17,25},{2,10},{10,18},{18,26},{... | collective-permute-start | bytes 786440 | tf_op jit(solution)/shard_map/ppermute | solution.py:524
  92.1 1.3 %collective-permute-start.15 = (f32[2,16,8,256]{3,2,1,0:T(8,128)S(1)}, f32[2,16,8,256]{3,2,1,0:T(8,128)S(1)}, u32[]{:S(2)}, u32[]{:S(2)}) collective-permute-start(f32[2,16,8,256]{3,2,1,0:T(8,128)S(1)} %get-tuple-element.78), channel_id=1, source_target_pairs={{8,0},{16,8},{24,16},{9,1},{17,9},{25,17},{10,2},{18,10},{26,18},{... | collective-permute-start | bytes 786440 | tf_op jit(solution)/shard_map/ppermute | solution.py:525
  94.4 3.5 %collective-permute-start.17 = (f32[16,2,8,256]{3,2,1,0:T(8,128)S(1)}, f32[16,2,8,256]{3,2,1,0:T(8,128)S(1)}, u32[]{:S(2)}, u32[]{:S(2)}) collective-permute-start(f32[16,2,8,256]{3,2,1,0:T(8,128)S(1)} %get-tuple-element.80), channel_id=1, source_target_pairs={{1,0},{2,1},{3,2},{4,3},{5,4},{6,5},{7,6},{0,7},{9,8},{10,9},{11,1... | collective-permute-start | bytes 786440 | tf_op jit(solution)/shard_map/ppermute | solution.py:527
  97.9 6.0 %inner_stage.3 = (f32[16,16,8,256]{3,2,1,0:T(8,128)S(1)}, f32[16,16,8,256]{3,2,1,0:T(8,128)S(1)}, f32[16,16,8,256]{3,2,1,0:T(8,128)S(1)}) custom-call(f32[16,16,8,256]{3,2,1,0:T(8,128)S(1)} %get-tuple-element.76.field, f32[8,24]{1,0:T(8,128)S(1)} %get-tuple-element.62.weights, f32[8,256]{1,0:T(8,128)S(1)} %get-tuple-element.63.ratio, ...), custom_call_target="tpu_custom_call" | custom-call | tf_op jit(solution)/shard_map/inner_stage/pallas_call | solution.py:322
  104.0 2.7 %collective-permute-done.15.high_rad = f32[2,16,8,256]{3,2,1,0:T(8,128)S(1)} collective-permute-done((f32[2,16,8,256]{3,2,1,0:T(8,128)S(1)}, f32[2,16,8,256]{3,2,1,0:T(8,128)S(1)}, u32[]{:S(2)}, u32[]{:S(2)}) %collective-permute-start.15) | collective-permute-done | bytes 262176 | tf_op jit(solution)/shard_map/ppermute | solution.py:525
  106.7 7.6 %outer_stage.3 = (f32[16,16,8,256]{3,2,1,0:T(8,128)S(1)}, f32[16,16,8,256]{3,2,1,0:T(8,128)S(1)}, f32[16,16,8,256]{3,2,1,0:T(8,128)S(1)}) custom-call(f32[16,16,8,256]{3,2,1,0:T(8,128)S(1)} %get-tuple-element.76.field, f32[2,16,8,256]{3,2,1,0:T(8,128)S(1)} %collective-permute-done.14.low_rad, ...), custom_call_target="tpu_custom_call", output_to_operand_aliasing={{0}: (8, {}), {1}: (9, {}), {2}: (10, {})} | custom-call | tf_op jit(solution)/shard_map/outer_stage/pallas_call | solution.py:353
  114.4 5.2 %final_stage.1 = (f32[16,8,4096]{2,1,0:T(8,128)}, f32[16,8,4096]{2,1,0:T(8,128)}) custom-call(f32[16,8,4096]{2,1,0:T(8,128)S(1)} %get-tuple-element.56.held, f32[16,16,8,256]{3,2,1,0:T(8,128)S(1)} %get-tuple-element.88.settled, f32[16,16,8,256]{3,2,1,0:T(8,128)S(1)} %get-tuple-element.89.sums_azi, f32[16,16,8,256]{3,2,1,0:T(8,128)S(1)} %get-tuple-element.90.jumps_azi, ...), custom_call_target="tpu_custom_call" | custom-call | tf_op jit(solution)/shard_map/final_stage/pallas_call | solution.py:492
  (40 shorter events, 5.2 us)
Async XLA Ops:
  0.6 41.3 %copy-start = (f32[3,8,8]{2,1,0:T(8,128)S(1)}, f32[3,8,8]{2,1,0:T(8,128)}, u32[]{:S(2)}) copy-start(f32[3,8,8]{2,1,0:T(8,128)} %coupling.1) | copy-start | bytes 2308
  1.3 40.6 %copy-start.2 = (s32[16]{0:T(128)S(1)}, s32[16]{0:T(128)}, u32[]{:S(2)}) copy-start(s32[16]{0:T(128)} %levels.1) | copy-start | bytes 196
  1.3 40.6 %copy-start.3 = (f32[8]{0:T(128)S(1)}, f32[8]{0:T(128)}, u32[]{:S(2)}) copy-start(f32[8]{0:T(128)} %damping.1) | copy-start | bytes 100
  4.6 10.7 %collective-permute-start = (f32[2,8,4096]{2,1,0:T(8,128)S(1)}, f32[2,8,4096]{2,1,0:T(8,128)S(1)}, u32[]{:S(2)}, u32[]{:S(2)}) collective-permute-start(f32[2,8,4096]{2,1,0:T(8,128)S(1)} %get-tuple-element.49), channel_id=1, source_target_pairs={{0,1},{1,2},{2,3},{3,4},{4,5},{5,6},{6,7},{7,0},{8,9},{9,10},{10,1... | collective-permute-start | bytes 786440 | tf_op jit(solution)/shard_map/ppermute | solution.py:535
  5.1 12.6 %collective-permute-start.1 = (f32[2,8,4096]{2,1,0:T(8,128)S(1)}, f32[2,8,4096]{2,1,0:T(8,128)S(1)}, u32[]{:S(2)}, u32[]{:S(2)}) collective-permute-start(f32[2,8,4096]{2,1,0:T(8,128)S(1)} %get-tuple-element.50), channel_id=1, source_target_pairs={{0,2},{1,3},{2,4},{3,5},{4,6},{5,7},{6,0},{7,1},{8,10},{9,11},{10,... | collective-permute-start | bytes 786440 | tf_op jit(solution)/shard_map/ppermute | solution.py:535
  7.8 30.7 %collective-permute-start.2 = (f32[2,8,4096]{2,1,0:T(8,128)S(1)}, f32[2,8,4096]{2,1,0:T(8,128)S(1)}, u32[]{:S(2)}, u32[]{:S(2)}) collective-permute-start(f32[2,8,4096]{2,1,0:T(8,128)S(1)} %get-tuple-element.51), channel_id=1, source_target_pairs={{0,3},{1,4},{2,5},{3,6},{4,7},{5,0},{6,1},{7,2},{8,11},{9,12},{10,... | collective-permute-start | bytes 786440 | tf_op jit(solution)/shard_map/ppermute | solution.py:535
  10.3 28.3 %collective-permute-start.3 = (f32[2,8,4096]{2,1,0:T(8,128)S(1)}, f32[2,8,4096]{2,1,0:T(8,128)S(1)}, u32[]{:S(2)}, u32[]{:S(2)}) collective-permute-start(f32[2,8,4096]{2,1,0:T(8,128)S(1)} %get-tuple-element.52), channel_id=1, source_target_pairs={{0,4},{1,5},{2,6},{3,7},{4,0},{5,1},{6,2},{7,3},{8,12},{9,13},{10,... | collective-permute-start | bytes 786440 | tf_op jit(solution)/shard_map/ppermute | solution.py:535
  11.5 27.1 %collective-permute-start.4 = (f32[2,8,4096]{2,1,0:T(8,128)S(1)}, f32[2,8,4096]{2,1,0:T(8,128)S(1)}, u32[]{:S(2)}, u32[]{:S(2)}) collective-permute-start(f32[2,8,4096]{2,1,0:T(8,128)S(1)} %get-tuple-element.53), channel_id=1, source_target_pairs={{0,5},{1,6},{2,7},{3,0},{4,1},{5,2},{6,3},{7,4},{8,13},{9,14},{10,... | collective-permute-start | bytes 786440 | tf_op jit(solution)/shard_map/ppermute | solution.py:535
  15.3 23.4 %collective-permute-start.5 = (f32[2,8,4096]{2,1,0:T(8,128)S(1)}, f32[2,8,4096]{2,1,0:T(8,128)S(1)}, u32[]{:S(2)}, u32[]{:S(2)}) collective-permute-start(f32[2,8,4096]{2,1,0:T(8,128)S(1)} %get-tuple-element.54), channel_id=1, source_target_pairs={{0,6},{1,7},{2,0},{3,1},{4,2},{5,3},{6,4},{7,5},{8,14},{9,15},{10,... | collective-permute-start | bytes 786440 | tf_op jit(solution)/shard_map/ppermute | solution.py:535
  17.7 24.2 %collective-permute-start.6 = (f32[2,8,4096]{2,1,0:T(8,128)S(1)}, f32[2,8,4096]{2,1,0:T(8,128)S(1)}, u32[]{:S(2)}, u32[]{:S(2)}) collective-permute-start(f32[2,8,4096]{2,1,0:T(8,128)S(1)} %get-tuple-element.55), channel_id=1, source_target_pairs={{0,7},{1,0},{2,1},{3,2},{4,3},{5,4},{6,5},{7,6},{8,15},{9,8},{10,9... | collective-permute-start | bytes 786440 | tf_op jit(solution)/shard_map/ppermute | solution.py:535
  49.7 7.4 %collective-permute-start.11 = (f32[16,8,256]{2,1,0:T(8,128)S(1)}, f32[16,8,256]{2,1,0:T(8,128)S(1)}, u32[]{:S(2)}, u32[]{:S(2)}) collective-permute-start(f32[16,8,256]{2,1,0:T(8,128)S(1)} %get-tuple-element.65), channel_id=1, source_target_pairs={{0,1},{1,0},{2,3},{3,2},{4,5},{5,4},{6,7},{7,6},{8,9},{9,8},{10,11... | collective-permute-start | bytes 393224 | tf_op jit(solution)/shard_map/ppermute | solution.py:513
  51.9 26.6 %collective-permute-start.7 = (f32[2,16,8,256]{3,2,1,0:T(8,128)S(1)}, f32[2,16,8,256]{3,2,1,0:T(8,128)S(1)}, u32[]{:S(2)}, u32[]{:S(2)}) collective-permute-start(f32[2,16,8,256]{3,2,1,0:T(8,128)S(1)} %get-tuple-element.58), channel_id=1, source_target_pairs={{0,8},{8,16},{16,24},{1,9},{9,17},{17,25},{2,10},{10,18},{18,26},{... | collective-permute-start | bytes 786440 | tf_op jit(solution)/shard_map/ppermute | solution.py:524
  55.8 22.7 %collective-permute-start.8 = (f32[2,16,8,256]{3,2,1,0:T(8,128)S(1)}, f32[2,16,8,256]{3,2,1,0:T(8,128)S(1)}, u32[]{:S(2)}, u32[]{:S(2)}) collective-permute-start(f32[2,16,8,256]{3,2,1,0:T(8,128)S(1)} %get-tuple-element.59), channel_id=1, source_target_pairs={{8,0},{16,8},{24,16},{9,1},{17,9},{25,17},{10,2},{18,10},{26,18},{... | collective-permute-start | bytes 786440 | tf_op jit(solution)/shard_map/ppermute | solution.py:525
  57.1 21.3 %collective-permute-start.12 = (f32[16,8,256]{2,1,0:T(8,128)S(1)}, f32[16,8,256]{2,1,0:T(8,128)S(1)}, u32[]{:S(2)}, u32[]{:S(2)}) collective-permute-start(f32[16,8,256]{2,1,0:T(8,128)S(1)} %add.18), channel_id=1, source_target_pairs={{0,2},{1,3},{2,0},{3,1},{4,6},{5,7},{6,4},{7,5},{8,10},{9,11},{10,... | collective-permute-start | bytes 393224 | tf_op jit(solution)/shard_map/ppermute | solution.py:513
  68.9 10.2 %collective-permute-start.9 = (f32[16,2,8,256]{3,2,1,0:T(8,128)S(1)}, f32[16,2,8,256]{3,2,1,0:T(8,128)S(1)}, u32[]{:S(2)}, u32[]{:S(2)}) collective-permute-start(f32[16,2,8,256]{3,2,1,0:T(8,128)S(1)} %get-tuple-element.60), channel_id=1, source_target_pairs={{0,1},{1,2},{2,3},{3,4},{4,5},{5,6},{6,7},{7,0},{8,9},{9,10},{10,1... | collective-permute-start | bytes 786440 | tf_op jit(solution)/shard_map/ppermute | solution.py:526
  68.9 10.2 %collective-permute-start.10 = (f32[16,2,8,256]{3,2,1,0:T(8,128)S(1)}, f32[16,2,8,256]{3,2,1,0:T(8,128)S(1)}, u32[]{:S(2)}, u32[]{:S(2)}) collective-permute-start(f32[16,2,8,256]{3,2,1,0:T(8,128)S(1)} %get-tuple-element.61), channel_id=1, source_target_pairs={{1,0},{2,1},{3,2},{4,3},{5,4},{6,5},{7,6},{0,7},{9,8},{10,9},{11,1... | collective-permute-start | bytes 786440 | tf_op jit(solution)/shard_map/ppermute | solution.py:527
  78.4 8.3 %collective-permute-start.13 = (f32[16,8,256]{2,1,0:T(8,128)S(1)}, f32[16,8,256]{2,1,0:T(8,128)S(1)}, u32[]{:S(2)}, u32[]{:S(2)}) collective-permute-start(f32[16,8,256]{2,1,0:T(8,128)S(1)} %add.19), channel_id=1, source_target_pairs={{0,4},{1,5},{2,6},{3,7},{4,0},{5,1},{6,2},{7,3},{8,12},{9,13},{10,... | collective-permute-start | bytes 393224 | tf_op jit(solution)/shard_map/ppermute | solution.py:513
  87.5 5.9 %collective-permute-start.18 = (f32[16,8,256]{2,1,0:T(8,128)S(1)}, f32[16,8,256]{2,1,0:T(8,128)S(1)}, u32[]{:S(2)}, u32[]{:S(2)}) collective-permute-start(f32[16,8,256]{2,1,0:T(8,128)S(1)} %get-tuple-element.81), channel_id=1, source_target_pairs={{0,1},{1,0},{2,3},{3,2},{4,5},{5,4},{6,7},{7,6},{8,9},{9,8},{10,11... | collective-permute-start | bytes 393224 | tf_op jit(solution)/shard_map/ppermute | solution.py:513
  87.5 16.5 %collective-permute-start.14 = (f32[2,16,8,256]{3,2,1,0:T(8,128)S(1)}, f32[2,16,8,256]{3,2,1,0:T(8,128)S(1)}, u32[]{:S(2)}, u32[]{:S(2)}) collective-permute-start(f32[2,16,8,256]{3,2,1,0:T(8,128)S(1)} %get-tuple-element.77), channel_id=1, source_target_pairs={{0,8},{8,16},{16,24},{1,9},{9,17},{17,25},{2,10},{10,18},{18,26},{... | collective-permute-start | bytes 786440 | tf_op jit(solution)/shard_map/ppermute | solution.py:524
  92.1 14.6 %collective-permute-start.15 = (f32[2,16,8,256]{3,2,1,0:T(8,128)S(1)}, f32[2,16,8,256]{3,2,1,0:T(8,128)S(1)}, u32[]{:S(2)}, u32[]{:S(2)}) collective-permute-start(f32[2,16,8,256]{3,2,1,0:T(8,128)S(1)} %get-tuple-element.78), channel_id=1, source_target_pairs={{8,0},{16,8},{24,16},{9,1},{17,9},{25,17},{10,2},{18,10},{26,18},{... | collective-permute-start | bytes 786440 | tf_op jit(solution)/shard_map/ppermute | solution.py:525
  93.4 10.5 %collective-permute-start.19 = (f32[16,8,256]{2,1,0:T(8,128)S(1)}, f32[16,8,256]{2,1,0:T(8,128)S(1)}, u32[]{:S(2)}, u32[]{:S(2)}) collective-permute-start(f32[16,8,256]{2,1,0:T(8,128)S(1)} %add.21), channel_id=1, source_target_pairs={{0,2},{1,3},{2,0},{3,1},{4,6},{5,7},{6,4},{7,5},{8,10},{9,11},{10,... | collective-permute-start | bytes 393224 | tf_op jit(solution)/shard_map/ppermute | solution.py:513
  94.4 12.3 %collective-permute-start.16 = (f32[16,2,8,256]{3,2,1,0:T(8,128)S(1)}, f32[16,2,8,256]{3,2,1,0:T(8,128)S(1)}, u32[]{:S(2)}, u32[]{:S(2)}) collective-permute-start(f32[16,2,8,256]{3,2,1,0:T(8,128)S(1)} %get-tuple-element.79), channel_id=1, source_target_pairs={{0,1},{1,2},{2,3},{3,4},{4,5},{5,6},{6,7},{7,0},{8,9},{9,10},{10,1... | collective-permute-start | bytes 786440 | tf_op jit(solution)/shard_map/ppermute | solution.py:526
  94.4 12.3 %collective-permute-start.17 = (f32[16,2,8,256]{3,2,1,0:T(8,128)S(1)}, f32[16,2,8,256]{3,2,1,0:T(8,128)S(1)}, u32[]{:S(2)}, u32[]{:S(2)}) collective-permute-start(f32[16,2,8,256]{3,2,1,0:T(8,128)S(1)} %get-tuple-element.80), channel_id=1, source_target_pairs={{1,0},{2,1},{3,2},{4,3},{5,4},{6,5},{7,6},{0,7},{9,8},{10,9},{11,1... | collective-permute-start | bytes 786440 | tf_op jit(solution)/shard_map/ppermute | solution.py:527
  103.9 10.4 %collective-permute-start.20 = (f32[16,8,256]{2,1,0:T(8,128)S(1)}, f32[16,8,256]{2,1,0:T(8,128)S(1)}, u32[]{:S(2)}, u32[]{:S(2)}) collective-permute-start(f32[16,8,256]{2,1,0:T(8,128)S(1)} %add.22), channel_id=1, source_target_pairs={{0,4},{1,5},{2,6},{3,7},{4,0},{5,1},{6,2},{7,3},{8,12},{9,13},{10,... | collective-permute-start | bytes 393224 | tf_op jit(solution)/shard_map/ppermute | solution.py:513
  (1 other events, 0.7 us)

commit v3 on v2

--- a/solution.py
+++ b/solution.py
@@ -137,8 +137,12 @@
     relax[...] = pull
 
 
+def order_of(azi_count):
+    return [0] + sorted(range(1, azi_count), key=lambda d: abs(2 * d - azi_count))
+
+
 def unpack_kernel(azi_count, block_count, table, levels, damping, coupling, *refs):
-    arrived = refs[:azi_count]
+    arrived = {d: refs[i] for i, d in enumerate(order_of(azi_count))}
     field, rad_head, rad_tail, azi_head, azi_tail, sums, held, weights, ratio, relax, sems = refs[
         azi_count:
     ]
@@ -183,7 +187,7 @@
             sums[x, :, lanes] = running
         return carry
 
-    lax.fori_loop(0, EDGE, row, 0)
+    lax.fori_loop(0, EDGE, row, 0, unroll=2)
     rad_head[...] = field[0:2]
     rad_tail[...] = field[EDGE - 2 : EDGE]
 
@@ -212,7 +216,7 @@
         scratch_shapes=[pltpu.SemaphoreType.DMA((azi_count * CAPACITY,))],
         compiler_params=pltpu.CompilerParams(vmem_limit_bytes=16 * MIB),
         name="unpack",
-    )(table, levels, damping, coupling, *arrived)
+    )(table, levels, damping, coupling, *(arrived[d] for d in order_of(azi_count)))
 
 
 def shear_of(x):
@@ -289,7 +293,7 @@
     return jnp.concatenate(columns, axis=1).astype(jnp.bfloat16)
 
 
-def sweep(get, rows, runs, carry_slope, carry_plus, left, ratio, relax, outs):
+def sweep(get, rows, runs, carry_slope, carry_plus, left, ratio, relax, outs, unroll=1):
     for cells in runs:
         for y in cells:
             start_radius(get, rows[0], y, carry_slope, carry_plus)
@@ -301,7 +305,7 @@
             )
         return carry
 
-    lax.fori_loop(rows[0], rows[1], row, 0)
+    lax.fori_loop(rows[0], rows[1], row, 0, unroll=unroll)
 
 
 INNER = range(2, EDGE - 2)
@@ -314,7 +318,7 @@
     def get(x, y):
         return field[x, y]
 
-    sweep(get, (2, EDGE - 2), (INNER,), *carries, split_weights(weights), ratio, relax, outs)
+    sweep(get, (2, EDGE - 2), (INNER,), *carries, split_weights(weights), ratio, relax, outs, unroll=4)
 
 
 def inner_stage(field, weights, ratio, relax):
@@ -332,7 +336,7 @@
 
 
 def outer_kernel(
-    field, low_rad, high_rad, low_azi, high_azi, weights, ratio, relax, one, two, three, *refs
+    field, low_azi, high_azi, low_rad, high_rad, weights, ratio, relax, one, two, three, *refs
 ):
     del one, two, three
     outs = refs[:3]
@@ -344,7 +348,7 @@
 
     rest = (carry_slope, carry_plus, split_weights(weights), ratio, relax, outs)
     sweep(get, (0, 2), (range(EDGE),), *rest)
-    sweep(get, (2, EDGE - 2), (HEAD, TAIL), *rest)
+    sweep(get, (2, EDGE - 2), (HEAD, TAIL), *rest, unroll=12)
     sweep(get, (EDGE - 2, EDGE), (range(EDGE),), *rest)
 
 
@@ -478,7 +482,7 @@
             copy.start()
         return carry
 
-    lax.fori_loop(0, EDGE, row, 0)
+    lax.fori_loop(0, EDGE, row, 0, unroll=2)
 
     def finish_row(x, carry):
         for copy in out_copies(x):
@@ -521,10 +525,10 @@
 def exchange(rad_head, rad_tail, azi_head, azi_tail):
     rad, azi = lax.axis_size("rad"), lax.axis_size("azi")
     return (
+        lax.ppermute(azi_tail, "azi", [(i, (i + 1) % azi) for i in range(azi)]),
+        lax.ppermute(azi_head, "azi", [((i + 1) % azi, i) for i in range(azi)]),
         lax.ppermute(rad_tail, "rad", [(i, i + 1) for i in range(rad - 1)]),
         lax.ppermute(rad_head, "rad", [(i + 1, i) for i in range(rad - 1)]),
-        lax.ppermute(azi_tail, "azi", [(i, (i + 1) % azi) for i in range(azi)]),
-        lax.ppermute(azi_head, "azi", [((i + 1) % azi, i) for i in range(azi)]),
     )
 
 

time: 120 us -> 111 us (0.925)
  Pallas kernels: 44 us -> 28.7 us
  waiting for transfers between devices: 25 us -> 38.5 us
  starting transfers between devices: 48.8 us -> 41.4 us
    pallas_call x2, Pallas kernels: 15.2 us -> 7.29 us  [outer_stage(): pl.pallas_call(outer_kernel, out_shape=[pltpu.VMEM(field.shape, F32)] * 3...]
    ppermute x2, waiting for transfers between devices: 2.69 us -> 9.93 us  [exchange(): lax.ppermute(rad_head, 'rad', [(i + 1, i) for i in range(rad - 1)])]
    ppermute x7, waiting for transfers between devices: 21.7 us -> 28.2 us  [on_device(): lax.ppermute(packed[d], 'azi', [(i, (i + d) % azi_count) for i in range(a...]
    pallas_call x2, Pallas kernels: 11.9 us -> 6.74 us  [inner_stage(): pl.pallas_call(inner_kernel, out_shape=[pltpu.VMEM(field.shape, F32)] * 3...]
    ppermute x7, starting transfers between devices: 15.6 us -> 10.6 us  [on_device(): lax.ppermute(packed[d], 'azi', [(i, (i + d) % azi_count) for i in range(a...]
    ppermute x6, starting transfers between devices: 15.2 us -> 12.2 us  [sum_azi(): other = lax.ppermute(values, 'azi', [(i, i ^ step) for i in range(count)])]
    ppermute x2, starting transfers between devices: 7.08 us -> 8.74 us  [exchange(): lax.ppermute(azi_head, 'azi', [((i + 1) % azi, i) for i in range(azi)])]
    ppermute x2, starting transfers between devices: 8.4 us -> 6.81 us  [exchange(): lax.ppermute(rad_tail, 'rad', [(i, i + 1) for i in range(rad - 1)])]
  transfers between devices with their start and end apart: 21 -> 21, of which waited for: 6 -> 7; matrix products, arithmetic and copies ran while one was open for 0% -> 0% of each run, Pallas kernels for 23% -> 13%
where the time goes in v3:
time: 111 us; the launch traced here: 110 us
  starting transfers between devices  41.4 us (37%)
  waiting for transfers between devices  38.5 us (35%)
  Pallas kernels  28.7 us (26%)
    ppermute x7, waiting for transfers between devices, on_device(): lax.ppermute(packed[d], 'azi', [(i, (i + d) % azi_count) for i in range(a...  28.2 us
    ppermute x6, starting transfers between devices, sum_azi(): other = lax.ppermute(values, 'azi', [(i, i ^ step) for i in range(count)])  12.2 us
    ppermute x7, starting transfers between devices, on_device(): lax.ppermute(packed[d], 'azi', [(i, (i + d) % azi_count) for i in range(a...  10.6 us
    ppermute x2, waiting for transfers between devices, exchange(): lax.ppermute(rad_head, 'rad', [(i + 1, i) for i in range(rad - 1)])  9.93 us
    ppermute x2, starting transfers between devices, exchange(): lax.ppermute(azi_head, 'azi', [((i + 1) % azi, i) for i in range(azi)])  8.74 us
    pallas_call x2, Pallas kernels, outer_stage(): pl.pallas_call(outer_kernel, out_shape=[pltpu.VMEM(field.shape, F32)] * 3...  7.29 us
    ppermute x2, starting transfers between devices, exchange(): lax.ppermute(rad_tail, 'rad', [(i, i + 1) for i in range(rad - 1)])  6.81 us
    pallas_call x2, Pallas kernels, inner_stage(): pl.pallas_call(inner_kernel, out_shape=[pltpu.VMEM(field.shape, F32)] * 3...  6.74 us
  transfers between devices with their start and end apart: 21, of which 7 were waited for; matrix products, arithmetic and copies ran while one was open for 0% of the time, Pallas kernels for 13%

profile of v3, /device:TPU:0, one launch (start us, length us, event | category | flops | bytes accessed | tf_op | source)
XLA Modules:
  0.0 110.2 jit_solution(10079739695534588041)
XLA Ops:
  1.3 3.3 %pack.1 = (f32[2,8,4096]{2,1,0:T(8,128)S(1)}, f32[2,8,4096]{2,1,0:T(8,128)S(1)}, f32[2,8,4096]{2,1,0:T(8,128)S(1)}, f32[2,8,4096]{2,1,0:T(8,128)S(1)}, f32[2,8,4...) custom-call(s32[512]{0:T(512)S(1)} %copy-done.1, ...), custom_call_target="tpu_custom_call" | custom-call | tf_op jit(solution)/shard_map/pack/pallas_call | solution.py:105
  4.6 4.1 %collective-permute-start = (f32[2,8,4096]{2,1,0:T(8,128)S(1)}, f32[2,8,4096]{2,1,0:T(8,128)S(1)}, u32[]{:S(2)}, u32[]{:S(2)}) collective-permute-start(f32[2,8,4096]{2,1,0:T(8,128)S(1)} %get-tuple-element.49), channel_id=1, source_target_pairs={{0,4},{1,5},{2,6},{3,7},{4,0},{5,1},{6,2},{7,3},{8,12},{9,13},{10,... | collective-permute-start | bytes 786440 | tf_op jit(solution)/shard_map/ppermute | solution.py:539
  9.5 1.9 %collective-permute-start.2 = (f32[2,8,4096]{2,1,0:T(8,128)S(1)}, f32[2,8,4096]{2,1,0:T(8,128)S(1)}, u32[]{:S(2)}, u32[]{:S(2)}) collective-permute-start(f32[2,8,4096]{2,1,0:T(8,128)S(1)} %get-tuple-element.51), channel_id=1, source_target_pairs={{0,5},{1,6},{2,7},{3,0},{4,1},{5,2},{6,3},{7,4},{8,13},{9,14},{10,... | collective-permute-start | bytes 786440 | tf_op jit(solution)/shard_map/ppermute | solution.py:539
  11.4 1.6 %collective-permute-start.3 = (f32[2,8,4096]{2,1,0:T(8,128)S(1)}, f32[2,8,4096]{2,1,0:T(8,128)S(1)}, u32[]{:S(2)}, u32[]{:S(2)}) collective-permute-start(f32[2,8,4096]{2,1,0:T(8,128)S(1)} %get-tuple-element.52), channel_id=1, source_target_pairs={{0,2},{1,3},{2,4},{3,5},{4,6},{5,7},{6,0},{7,1},{8,10},{9,11},{10,... | collective-permute-start | bytes 786440 | tf_op jit(solution)/shard_map/ppermute | solution.py:539
  12.9 2.2 %collective-permute-start.4 = (f32[2,8,4096]{2,1,0:T(8,128)S(1)}, f32[2,8,4096]{2,1,0:T(8,128)S(1)}, u32[]{:S(2)}, u32[]{:S(2)}) collective-permute-start(f32[2,8,4096]{2,1,0:T(8,128)S(1)} %get-tuple-element.53), channel_id=1, source_target_pairs={{0,6},{1,7},{2,0},{3,1},{4,2},{5,3},{6,4},{7,5},{8,14},{9,15},{10,... | collective-permute-start | bytes 786440 | tf_op jit(solution)/shard_map/ppermute | solution.py:539
  15.2 20.4 %collective-permute-done.refs_1_ = f32[2,8,4096]{2,1,0:T(8,128)S(1)} collective-permute-done((f32[2,8,4096]{2,1,0:T(8,128)S(1)}, f32[2,8,4096]{2,1,0:T(8,128)S(1)}, u32[]{:S(2)}, u32[]{:S(2)}) %collective-permute-start) | collective-permute-done | bytes 262176 | tf_op jit(solution)/shard_map/ppermute | solution.py:539
  35.6 4.0 %collective-permute-done.1.refs_2_ = f32[2,8,4096]{2,1,0:T(8,128)S(1)} collective-permute-done((f32[2,8,4096]{2,1,0:T(8,128)S(1)}, f32[2,8,4096]{2,1,0:T(8,128)S(1)}, u32[]{:S(2)}, u32[]{:S(2)}) %collective-permute-start.1) | collective-permute-done | bytes 262176 | tf_op jit(solution)/shard_map/ppermute | solution.py:539
  39.5 3.8 %collective-permute-done.5.refs_6_ = f32[2,8,4096]{2,1,0:T(8,128)S(1)} collective-permute-done((f32[2,8,4096]{2,1,0:T(8,128)S(1)}, f32[2,8,4096]{2,1,0:T(8,128)S(1)}, u32[]{:S(2)}, u32[]{:S(2)}) %collective-permute-start.5) | collective-permute-done | bytes 262176 | tf_op jit(solution)/shard_map/ppermute | solution.py:539
  43.5 6.7 %unpack.1 = (f32[16,16,8,256]{3,2,1,0:T(8,128)S(1)}, f32[2,16,8,256]{3,2,1,0:T(8,128)S(1)}, f32[2,16,8,256]{3,2,1,0:T(8,128)S(1)}, f32[16,2,8,256]{3,2,1,0:T(8,1...) custom-call(s32[17]{0:T(128)S(1)} %get-tuple-element.47.table, ...), custom_call_target="tpu_custom_call" | custom-call | tf_op jit(solution)/shard_map/unpack/pallas_call | solution.py:205
  50.2 2.9 %collective-permute-start.11 = (f32[16,8,256]{2,1,0:T(8,128)S(1)}, f32[16,8,256]{2,1,0:T(8,128)S(1)}, u32[]{:S(2)}, u32[]{:S(2)}) collective-permute-start(f32[16,8,256]{2,1,0:T(8,128)S(1)} %get-tuple-element.65), channel_id=1, source_target_pairs={{0,1},{1,0},{2,3},{3,2},{4,5},{5,4},{6,7},{7,6},{8,9},{9,8},{10,11... | collective-permute-start | bytes 393224 | tf_op jit(solution)/shard_map/ppermute | solution.py:517
  53.1 5.6 %collective-permute-start.8 = (f32[16,2,8,256]{3,2,1,0:T(8,128)S(1)}, f32[16,2,8,256]{3,2,1,0:T(8,128)S(1)}, u32[]{:S(2)}, u32[]{:S(2)}) collective-permute-start(f32[16,2,8,256]{3,2,1,0:T(8,128)S(1)} %get-tuple-element.59), channel_id=1, source_target_pairs={{1,0},{2,1},{3,2},{4,3},{5,4},{6,5},{7,6},{0,7},{9,8},{10,9},{11,1... | collective-permute-start | bytes 786440 | tf_op jit(solution)/shard_map/ppermute | solution.py:529
  58.8 5.0 %collective-permute-start.12 = (f32[16,8,256]{2,1,0:T(8,128)S(1)}, f32[16,8,256]{2,1,0:T(8,128)S(1)}, u32[]{:S(2)}, u32[]{:S(2)}) collective-permute-start(f32[16,8,256]{2,1,0:T(8,128)S(1)} %add.18), channel_id=1, source_target_pairs={{0,2},{1,3},{2,0},{3,1},{4,6},{5,7},{6,4},{7,5},{8,10},{9,11},{10,... | collective-permute-start | bytes 393224 | tf_op jit(solution)/shard_map/ppermute | solution.py:517
  63.8 3.4 %collective-permute-start.9 = (f32[2,16,8,256]{3,2,1,0:T(8,128)S(1)}, f32[2,16,8,256]{3,2,1,0:T(8,128)S(1)}, u32[]{:S(2)}, u32[]{:S(2)}) collective-permute-start(f32[2,16,8,256]{3,2,1,0:T(8,128)S(1)} %get-tuple-element.60), channel_id=1, source_target_pairs={{0,8},{8,16},{16,24},{1,9},{9,17},{17,25},{2,10},{10,18},{18,26},{... | collective-permute-start | bytes 786440 | tf_op jit(solution)/shard_map/ppermute | solution.py:530
  68.5 3.4 %inner_stage.2 = (f32[16,16,8,256]{3,2,1,0:T(8,128)S(1)}, f32[16,16,8,256]{3,2,1,0:T(8,128)S(1)}, f32[16,16,8,256]{3,2,1,0:T(8,128)S(1)}) custom-call(f32[16,16,8,256]{3,2,1,0:T(8,128)S(1)} %get-tuple-element.57.field, f32[8,24]{1,0:T(8,128)S(1)} %get-tuple-element.62.weights, f32[8,256]{1,0:T(8,128)S(1)} %get-tuple-element.63.ratio, ...), custom_call_target="tpu_custom_call" | custom-call | tf_op jit(solution)/shard_map/inner_stage/pallas_call | solution.py:326
  71.9 2.3 %collective-permute-start.13 = (f32[16,8,256]{2,1,0:T(8,128)S(1)}, f32[16,8,256]{2,1,0:T(8,128)S(1)}, u32[]{:S(2)}, u32[]{:S(2)}) collective-permute-start(f32[16,8,256]{2,1,0:T(8,128)S(1)} %add.19), channel_id=1, source_target_pairs={{0,4},{1,5},{2,6},{3,7},{4,0},{5,1},{6,2},{7,3},{8,12},{9,13},{10,... | collective-permute-start | bytes 393224 | tf_op jit(solution)/shard_map/ppermute | solution.py:517
  74.3 6.8 %collective-permute-done.10.high_rad = f32[2,16,8,256]{3,2,1,0:T(8,128)S(1)} collective-permute-done((f32[2,16,8,256]{3,2,1,0:T(8,128)S(1)}, f32[2,16,8,256]{3,2,1,0:T(8,128)S(1)}, u32[]{:S(2)}, u32[]{:S(2)}) %collective-permute-start.10) | collective-permute-done | bytes 262176 | tf_op jit(solution)/shard_map/ppermute | solution.py:531
  81.1 3.6 %outer_stage.2 = (f32[16,16,8,256]{3,2,1,0:T(8,128)S(1)}, f32[16,16,8,256]{3,2,1,0:T(8,128)S(1)}, f32[16,16,8,256]{3,2,1,0:T(8,128)S(1)}) custom-call(f32[16,16,8,256]{3,2,1,0:T(8,128)S(1)} %get-tuple-element.57.field, f32[16,2,8,256]{3,2,1,0:T(8,128)S(1)} %collective-permute-done.7.low_azi, ...), custom_call_target="tpu_custom_call", output_to_operand_aliasing={{0}: (8, {}), {1}: (9, {}), {2}: (10, {})} | custom-call | tf_op jit(solution)/shard_map/outer_stage/pallas_call | solution.py:357
  86.0 3.1 %collective-permute-start.15 = (f32[16,2,8,256]{3,2,1,0:T(8,128)S(1)}, f32[16,2,8,256]{3,2,1,0:T(8,128)S(1)}, u32[]{:S(2)}, u32[]{:S(2)}) collective-permute-start(f32[16,2,8,256]{3,2,1,0:T(8,128)S(1)} %get-tuple-element.78), channel_id=1, source_target_pairs={{1,0},{2,1},{3,2},{4,3},{5,4},{6,5},{7,6},{0,7},{9,8},{10,9},{11,1... | collective-permute-start | bytes 786440 | tf_op jit(solution)/shard_map/ppermute | solution.py:529
  89.2 3.4 %collective-permute-start.16 = (f32[2,16,8,256]{3,2,1,0:T(8,128)S(1)}, f32[2,16,8,256]{3,2,1,0:T(8,128)S(1)}, u32[]{:S(2)}, u32[]{:S(2)}) collective-permute-start(f32[2,16,8,256]{3,2,1,0:T(8,128)S(1)} %get-tuple-element.79), channel_id=1, source_target_pairs={{0,8},{8,16},{16,24},{1,9},{9,17},{17,25},{2,10},{10,18},{18,26},{... | collective-permute-start | bytes 786440 | tf_op jit(solution)/shard_map/ppermute | solution.py:530
  94.0 3.4 %inner_stage.3 = (f32[16,16,8,256]{3,2,1,0:T(8,128)S(1)}, f32[16,16,8,256]{3,2,1,0:T(8,128)S(1)}, f32[16,16,8,256]{3,2,1,0:T(8,128)S(1)}) custom-call(f32[16,16,8,256]{3,2,1,0:T(8,128)S(1)} %get-tuple-element.76.field, f32[8,24]{1,0:T(8,128)S(1)} %get-tuple-element.62.weights, f32[8,256]{1,0:T(8,128)S(1)} %get-tuple-element.63.ratio, ...), custom_call_target="tpu_custom_call" | custom-call | tf_op jit(solution)/shard_map/inner_stage/pallas_call | solution.py:326
  97.7 1.8 %collective-permute-start.20 = (f32[16,8,256]{2,1,0:T(8,128)S(1)}, f32[16,8,256]{2,1,0:T(8,128)S(1)}, u32[]{:S(2)}, u32[]{:S(2)}) collective-permute-start(f32[16,8,256]{2,1,0:T(8,128)S(1)} %add.22), channel_id=1, source_target_pairs={{0,4},{1,5},{2,6},{3,7},{4,0},{5,1},{6,2},{7,3},{8,12},{9,13},{10,... | collective-permute-start | bytes 393224 | tf_op jit(solution)/shard_map/ppermute | solution.py:517
  99.5 3.1 %collective-permute-done.17.high_rad = f32[2,16,8,256]{3,2,1,0:T(8,128)S(1)} collective-permute-done((f32[2,16,8,256]{3,2,1,0:T(8,128)S(1)}, f32[2,16,8,256]{3,2,1,0:T(8,128)S(1)}, u32[]{:S(2)}, u32[]{:S(2)}) %collective-permute-start.17) | collective-permute-done | bytes 262176 | tf_op jit(solution)/shard_map/ppermute | solution.py:531
  102.6 3.6 %outer_stage.3 = (f32[16,16,8,256]{3,2,1,0:T(8,128)S(1)}, f32[16,16,8,256]{3,2,1,0:T(8,128)S(1)}, f32[16,16,8,256]{3,2,1,0:T(8,128)S(1)}) custom-call(f32[16,16,8,256]{3,2,1,0:T(8,128)S(1)} %get-tuple-element.76.field, f32[16,2,8,256]{3,2,1,0:T(8,128)S(1)} %collective-permute-done.14.low_azi, ...), custom_call_target="tpu_custom_call", output_to_operand_aliasing={{0}: (8, {}), {1}: (9, {}), {2}: (10, {})} | custom-call | tf_op jit(solution)/shard_map/outer_stage/pallas_call | solution.py:357
  106.3 3.9 %final_stage.1 = (f32[16,8,4096]{2,1,0:T(8,128)}, f32[16,8,4096]{2,1,0:T(8,128)}) custom-call(f32[16,8,4096]{2,1,0:T(8,128)S(1)} %get-tuple-element.56.held, f32[16,16,8,256]{3,2,1,0:T(8,128)S(1)} %get-tuple-element.88.settled, f32[16,16,8,256]{3,2,1,0:T(8,128)S(1)} %get-tuple-element.89.sums_azi, f32[16,16,8,256]{3,2,1,0:T(8,128)S(1)} %get-tuple-element.90.jumps_azi, ...), custom_call_target="tpu_custom_call" | custom-call | tf_op jit(solution)/shard_map/final_stage/pallas_call | solution.py:496
  (40 shorter events, 6.0 us)
Async XLA Ops:
  0.6 42.8 %copy-start = (f32[3,8,8]{2,1,0:T(8,128)S(1)}, f32[3,8,8]{2,1,0:T(8,128)}, u32[]{:S(2)}) copy-start(f32[3,8,8]{2,1,0:T(8,128)} %coupling.1) | copy-start | bytes 2308
  1.3 42.1 %copy-start.2 = (s32[16]{0:T(128)S(1)}, s32[16]{0:T(128)}, u32[]{:S(2)}) copy-start(s32[16]{0:T(128)} %levels.1) | copy-start | bytes 196
  1.3 42.1 %copy-start.3 = (f32[8]{0:T(128)S(1)}, f32[8]{0:T(128)}, u32[]{:S(2)}) copy-start(f32[8]{0:T(128)} %damping.1) | copy-start | bytes 100
  4.6 30.9 %collective-permute-start = (f32[2,8,4096]{2,1,0:T(8,128)S(1)}, f32[2,8,4096]{2,1,0:T(8,128)S(1)}, u32[]{:S(2)}, u32[]{:S(2)}) collective-permute-start(f32[2,8,4096]{2,1,0:T(8,128)S(1)} %get-tuple-element.49), channel_id=1, source_target_pairs={{0,4},{1,5},{2,6},{3,7},{4,0},{5,1},{6,2},{7,3},{8,12},{9,13},{10,... | collective-permute-start | bytes 786440 | tf_op jit(solution)/shard_map/ppermute | solution.py:539
  8.7 30.8 %collective-permute-start.1 = (f32[2,8,4096]{2,1,0:T(8,128)S(1)}, f32[2,8,4096]{2,1,0:T(8,128)S(1)}, u32[]{:S(2)}, u32[]{:S(2)}) collective-permute-start(f32[2,8,4096]{2,1,0:T(8,128)S(1)} %get-tuple-element.50), channel_id=1, source_target_pairs={{0,3},{1,4},{2,5},{3,6},{4,7},{5,0},{6,1},{7,2},{8,11},{9,12},{10,... | collective-permute-start | bytes 786440 | tf_op jit(solution)/shard_map/ppermute | solution.py:539
  9.5 30.1 %collective-permute-start.2 = (f32[2,8,4096]{2,1,0:T(8,128)S(1)}, f32[2,8,4096]{2,1,0:T(8,128)S(1)}, u32[]{:S(2)}, u32[]{:S(2)}) collective-permute-start(f32[2,8,4096]{2,1,0:T(8,128)S(1)} %get-tuple-element.51), channel_id=1, source_target_pairs={{0,5},{1,6},{2,7},{3,0},{4,1},{5,2},{6,3},{7,4},{8,13},{9,14},{10,... | collective-permute-start | bytes 786440 | tf_op jit(solution)/shard_map/ppermute | solution.py:539
  11.4 28.2 %collective-permute-start.3 = (f32[2,8,4096]{2,1,0:T(8,128)S(1)}, f32[2,8,4096]{2,1,0:T(8,128)S(1)}, u32[]{:S(2)}, u32[]{:S(2)}) collective-permute-start(f32[2,8,4096]{2,1,0:T(8,128)S(1)} %get-tuple-element.52), channel_id=1, source_target_pairs={{0,2},{1,3},{2,4},{3,5},{4,6},{5,7},{6,0},{7,1},{8,10},{9,11},{10,... | collective-permute-start | bytes 786440 | tf_op jit(solution)/shard_map/ppermute | solution.py:539
  12.9 26.6 %collective-permute-start.4 = (f32[2,8,4096]{2,1,0:T(8,128)S(1)}, f32[2,8,4096]{2,1,0:T(8,128)S(1)}, u32[]{:S(2)}, u32[]{:S(2)}) collective-permute-start(f32[2,8,4096]{2,1,0:T(8,128)S(1)} %get-tuple-element.53), channel_id=1, source_target_pairs={{0,6},{1,7},{2,0},{3,1},{4,2},{5,3},{6,4},{7,5},{8,14},{9,15},{10,... | collective-permute-start | bytes 786440 | tf_op jit(solution)/shard_map/ppermute | solution.py:539
  35.6 7.8 %collective-permute-start.5 = (f32[2,8,4096]{2,1,0:T(8,128)S(1)}, f32[2,8,4096]{2,1,0:T(8,128)S(1)}, u32[]{:S(2)}, u32[]{:S(2)}) collective-permute-start(f32[2,8,4096]{2,1,0:T(8,128)S(1)} %get-tuple-element.54), channel_id=1, source_target_pairs={{0,1},{1,2},{2,3},{3,4},{4,5},{5,6},{6,7},{7,0},{8,9},{9,10},{10,1... | collective-permute-start | bytes 786440 | tf_op jit(solution)/shard_map/ppermute | solution.py:539
  39.5 3.9 %collective-permute-start.6 = (f32[2,8,4096]{2,1,0:T(8,128)S(1)}, f32[2,8,4096]{2,1,0:T(8,128)S(1)}, u32[]{:S(2)}, u32[]{:S(2)}) collective-permute-start(f32[2,8,4096]{2,1,0:T(8,128)S(1)} %get-tuple-element.55), channel_id=1, source_target_pairs={{0,7},{1,0},{2,1},{3,2},{4,3},{5,4},{6,5},{7,6},{8,15},{9,8},{10,9... | collective-permute-start | bytes 786440 | tf_op jit(solution)/shard_map/ppermute | solution.py:539
  50.2 8.6 %collective-permute-start.11 = (f32[16,8,256]{2,1,0:T(8,128)S(1)}, f32[16,8,256]{2,1,0:T(8,128)S(1)}, u32[]{:S(2)}, u32[]{:S(2)}) collective-permute-start(f32[16,8,256]{2,1,0:T(8,128)S(1)} %get-tuple-element.65), channel_id=1, source_target_pairs={{0,1},{1,0},{2,3},{3,2},{4,5},{5,4},{6,7},{7,6},{8,9},{9,8},{10,11... | collective-permute-start | bytes 393224 | tf_op jit(solution)/shard_map/ppermute | solution.py:517
  53.1 21.2 %collective-permute-start.7 = (f32[16,2,8,256]{3,2,1,0:T(8,128)S(1)}, f32[16,2,8,256]{3,2,1,0:T(8,128)S(1)}, u32[]{:S(2)}, u32[]{:S(2)}) collective-permute-start(f32[16,2,8,256]{3,2,1,0:T(8,128)S(1)} %get-tuple-element.58), channel_id=1, source_target_pairs={{0,1},{1,2},{2,3},{3,4},{4,5},{5,6},{6,7},{7,0},{8,9},{9,10},{10,1... | collective-permute-start | bytes 786440 | tf_op jit(solution)/shard_map/ppermute | solution.py:528
  53.1 21.1 %collective-permute-start.8 = (f32[16,2,8,256]{3,2,1,0:T(8,128)S(1)}, f32[16,2,8,256]{3,2,1,0:T(8,128)S(1)}, u32[]{:S(2)}, u32[]{:S(2)}) collective-permute-start(f32[16,2,8,256]{3,2,1,0:T(8,128)S(1)} %get-tuple-element.59), channel_id=1, source_target_pairs={{1,0},{2,1},{3,2},{4,3},{5,4},{6,5},{7,6},{0,7},{9,8},{10,9},{11,1... | collective-permute-start | bytes 786440 | tf_op jit(solution)/shard_map/ppermute | solution.py:529
  58.8 13.1 %collective-permute-start.12 = (f32[16,8,256]{2,1,0:T(8,128)S(1)}, f32[16,8,256]{2,1,0:T(8,128)S(1)}, u32[]{:S(2)}, u32[]{:S(2)}) collective-permute-start(f32[16,8,256]{2,1,0:T(8,128)S(1)} %add.18), channel_id=1, source_target_pairs={{0,2},{1,3},{2,0},{3,1},{4,6},{5,7},{6,4},{7,5},{8,10},{9,11},{10,... | collective-permute-start | bytes 393224 | tf_op jit(solution)/shard_map/ppermute | solution.py:517
  63.8 10.4 %collective-permute-start.9 = (f32[2,16,8,256]{3,2,1,0:T(8,128)S(1)}, f32[2,16,8,256]{3,2,1,0:T(8,128)S(1)}, u32[]{:S(2)}, u32[]{:S(2)}) collective-permute-start(f32[2,16,8,256]{3,2,1,0:T(8,128)S(1)} %get-tuple-element.60), channel_id=1, source_target_pairs={{0,8},{8,16},{16,24},{1,9},{9,17},{17,25},{2,10},{10,18},{18,26},{... | collective-permute-start | bytes 786440 | tf_op jit(solution)/shard_map/ppermute | solution.py:530
  67.2 13.8 %collective-permute-start.10 = (f32[2,16,8,256]{3,2,1,0:T(8,128)S(1)}, f32[2,16,8,256]{3,2,1,0:T(8,128)S(1)}, u32[]{:S(2)}, u32[]{:S(2)}) collective-permute-start(f32[2,16,8,256]{3,2,1,0:T(8,128)S(1)} %get-tuple-element.61), channel_id=1, source_target_pairs={{8,0},{16,8},{24,16},{9,1},{17,9},{25,17},{10,2},{18,10},{26,18},{... | collective-permute-start | bytes 786440 | tf_op jit(solution)/shard_map/ppermute | solution.py:531
  71.9 12.8 %collective-permute-start.13 = (f32[16,8,256]{2,1,0:T(8,128)S(1)}, f32[16,8,256]{2,1,0:T(8,128)S(1)}, u32[]{:S(2)}, u32[]{:S(2)}) collective-permute-start(f32[16,8,256]{2,1,0:T(8,128)S(1)} %add.19), channel_id=1, source_target_pairs={{0,4},{1,5},{2,6},{3,7},{4,0},{5,1},{6,2},{7,3},{8,12},{9,13},{10,... | collective-permute-start | bytes 393224 | tf_op jit(solution)/shard_map/ppermute | solution.py:517
  85.5 3.7 %collective-permute-start.18 = (f32[16,8,256]{2,1,0:T(8,128)S(1)}, f32[16,8,256]{2,1,0:T(8,128)S(1)}, u32[]{:S(2)}, u32[]{:S(2)}) collective-permute-start(f32[16,8,256]{2,1,0:T(8,128)S(1)} %get-tuple-element.81), channel_id=1, source_target_pairs={{0,1},{1,0},{2,3},{3,2},{4,5},{5,4},{6,7},{7,6},{8,9},{9,8},{10,11... | collective-permute-start | bytes 393224 | tf_op jit(solution)/shard_map/ppermute | solution.py:517
  85.5 13.9 %collective-permute-start.14 = (f32[16,2,8,256]{3,2,1,0:T(8,128)S(1)}, f32[16,2,8,256]{3,2,1,0:T(8,128)S(1)}, u32[]{:S(2)}, u32[]{:S(2)}) collective-permute-start(f32[16,2,8,256]{3,2,1,0:T(8,128)S(1)} %get-tuple-element.77), channel_id=1, source_target_pairs={{0,1},{1,2},{2,3},{3,4},{4,5},{5,6},{6,7},{7,0},{8,9},{9,10},{10,1... | collective-permute-start | bytes 786440 | tf_op jit(solution)/shard_map/ppermute | solution.py:528
  86.0 13.4 %collective-permute-start.15 = (f32[16,2,8,256]{3,2,1,0:T(8,128)S(1)}, f32[16,2,8,256]{3,2,1,0:T(8,128)S(1)}, u32[]{:S(2)}, u32[]{:S(2)}) collective-permute-start(f32[16,2,8,256]{3,2,1,0:T(8,128)S(1)} %get-tuple-element.78), channel_id=1, source_target_pairs={{1,0},{2,1},{3,2},{4,3},{5,4},{6,5},{7,6},{0,7},{9,8},{10,9},{11,1... | collective-permute-start | bytes 786440 | tf_op jit(solution)/shard_map/ppermute | solution.py:529
  89.2 8.5 %collective-permute-start.19 = (f32[16,8,256]{2,1,0:T(8,128)S(1)}, f32[16,8,256]{2,1,0:T(8,128)S(1)}, u32[]{:S(2)}, u32[]{:S(2)}) collective-permute-start(f32[16,8,256]{2,1,0:T(8,128)S(1)} %add.21), channel_id=1, source_target_pairs={{0,2},{1,3},{2,0},{3,1},{4,6},{5,7},{6,4},{7,5},{8,10},{9,11},{10,... | collective-permute-start | bytes 393224 | tf_op jit(solution)/shard_map/ppermute | solution.py:517
  89.2 10.2 %collective-permute-start.16 = (f32[2,16,8,256]{3,2,1,0:T(8,128)S(1)}, f32[2,16,8,256]{3,2,1,0:T(8,128)S(1)}, u32[]{:S(2)}, u32[]{:S(2)}) collective-permute-start(f32[2,16,8,256]{3,2,1,0:T(8,128)S(1)} %get-tuple-element.79), channel_id=1, source_target_pairs={{0,8},{8,16},{16,24},{1,9},{9,17},{17,25},{2,10},{10,18},{18,26},{... | collective-permute-start | bytes 786440 | tf_op jit(solution)/shard_map/ppermute | solution.py:530
  92.7 9.9 %collective-permute-start.17 = (f32[2,16,8,256]{3,2,1,0:T(8,128)S(1)}, f32[2,16,8,256]{3,2,1,0:T(8,128)S(1)}, u32[]{:S(2)}, u32[]{:S(2)}) collective-permute-start(f32[2,16,8,256]{3,2,1,0:T(8,128)S(1)} %get-tuple-element.80), channel_id=1, source_target_pairs={{8,0},{16,8},{24,16},{9,1},{17,9},{25,17},{10,2},{18,10},{26,18},{... | collective-permute-start | bytes 786440 | tf_op jit(solution)/shard_map/ppermute | solution.py:531
  97.7 8.6 %collective-permute-start.20 = (f32[16,8,256]{2,1,0:T(8,128)S(1)}, f32[16,8,256]{2,1,0:T(8,128)S(1)}, u32[]{:S(2)}, u32[]{:S(2)}) collective-permute-start(f32[16,8,256]{2,1,0:T(8,128)S(1)} %add.22), channel_id=1, source_target_pairs={{0,4},{1,5},{2,6},{3,7},{4,0},{5,1},{6,2},{7,3},{8,12},{9,13},{10,... | collective-permute-start | bytes 393224 | tf_op jit(solution)/shard_map/ppermute | solution.py:517
  (1 other events, 0.7 us)

commit v4 on v3

--- a/solution.py
+++ b/solution.py
@@ -74,7 +74,7 @@
         fill[shift] = k + 1
         return carry
 
-    lax.fori_loop(0, block_count, note, 0)
+    lax.fori_loop(0, block_count, note, 0, unroll=True)
     copies = []
     for shift in range(azi_count):
         for k in range(CAPACITY):
@@ -336,7 +336,7 @@
 
 
 def outer_kernel(
-    field, low_azi, high_azi, low_rad, high_rad, weights, ratio, relax, one, two, three, *refs
+    field, low_azi, low_rad, high_azi, high_rad, weights, ratio, relax, one, two, three, *refs
 ):
     del one, two, three
     outs = refs[:3]
@@ -526,8 +526,8 @@
     rad, azi = lax.axis_size("rad"), lax.axis_size("azi")
     return (
         lax.ppermute(azi_tail, "azi", [(i, (i + 1) % azi) for i in range(azi)]),
+        lax.ppermute(rad_tail, "rad", [(i, i + 1) for i in range(rad - 1)]),
         lax.ppermute(azi_head, "azi", [((i + 1) % azi, i) for i in range(azi)]),
-        lax.ppermute(rad_tail, "rad", [(i, i + 1) for i in range(rad - 1)]),
         lax.ppermute(rad_head, "rad", [(i + 1, i) for i in range(rad - 1)]),
     )
 

time: 111 us -> 109 us (0.982)
    ppermute x2, starting transfers between devices: 8.74 us -> 3.91 us  [exchange(): lax.ppermute(azi_head, 'azi', [((i + 1) % azi, i) for i in range(azi)])]
    ppermute x6, starting transfers between devices: 12.2 us -> 15 us  [sum_azi(): other = lax.ppermute(values, 'azi', [(i, i ^ step) for i in range(count)])]
    ppermute x2, starting transfers between devices: 6.81 us -> 8.03 us  [exchange(): lax.ppermute(rad_tail, 'rad', [(i, i + 1) for i in range(rad - 1)])]
  transfers between devices with their start and end apart: 21 -> 21, of which waited for: 7 -> 6; matrix products, arithmetic and copies ran while one was open for 0% -> 0% of each run, Pallas kernels for 13% -> 13%
where the time goes in v4:
time: 109 us; the launch traced here: 108 us
  starting transfers between devices  40.6 us (37%)
  waiting for transfers between devices  37.6 us (34%)
  Pallas kernels  28.4 us (26%)
    ppermute x7, waiting for transfers between devices, on_device(): lax.ppermute(packed[d], 'azi', [(i, (i + d) % azi_count) for i in range(a...  28.2 us
    ppermute x6, starting transfers between devices, sum_azi(): other = lax.ppermute(values, 'azi', [(i, i ^ step) for i in range(count)])  15 us
    ppermute x7, starting transfers between devices, on_device(): lax.ppermute(packed[d], 'azi', [(i, (i + d) % azi_count) for i in range(a...  10.6 us
    ppermute x2, waiting for transfers between devices, exchange(): lax.ppermute(rad_head, 'rad', [(i + 1, i) for i in range(rad - 1)])  9.32 us
    ppermute x2, starting transfers between devices, exchange(): lax.ppermute(rad_tail, 'rad', [(i, i + 1) for i in range(rad - 1)])  8.03 us
    pallas_call x2, Pallas kernels, outer_stage(): pl.pallas_call(outer_kernel, out_shape=[pltpu.VMEM(field.shape, F32)] * 3...  7.29 us
    pallas_call x2, Pallas kernels, inner_stage(): pl.pallas_call(inner_kernel, out_shape=[pltpu.VMEM(field.shape, F32)] * 3...  6.74 us
    pallas_call x1, Pallas kernels, unpack(): pl.pallas_call(functools.partial(unpack_kernel, azi_count, block_shape[0]...  6.72 us
  transfers between devices with their start and end apart: 21, of which 6 were waited for; matrix products, arithmetic and copies ran while one was open for 0% of the time, Pallas kernels for 13%

profile of v4, /device:TPU:0, one launch (start us, length us, event | category | flops | bytes accessed | tf_op | source)
XLA Modules:
  0.0 108.4 jit_solution(11754441013512407931)
XLA Ops:
  1.3 3.1 %pack.1 = (f32[2,8,4096]{2,1,0:T(8,128)S(1)}, f32[2,8,4096]{2,1,0:T(8,128)S(1)}, f32[2,8,4096]{2,1,0:T(8,128)S(1)}, f32[2,8,4096]{2,1,0:T(8,128)S(1)}, f32[2,8,4...) custom-call(s32[512]{0:T(512)S(1)} %copy-done.1, ...), custom_call_target="tpu_custom_call" | custom-call | tf_op jit(solution)/shard_map/pack/pallas_call | solution.py:105
  4.4 4.1 %collective-permute-start = (f32[2,8,4096]{2,1,0:T(8,128)S(1)}, f32[2,8,4096]{2,1,0:T(8,128)S(1)}, u32[]{:S(2)}, u32[]{:S(2)}) collective-permute-start(f32[2,8,4096]{2,1,0:T(8,128)S(1)} %get-tuple-element.49), channel_id=1, source_target_pairs={{0,4},{1,5},{2,6},{3,7},{4,0},{5,1},{6,2},{7,3},{8,12},{9,13},{10,... | collective-permute-start | bytes 786440 | tf_op jit(solution)/shard_map/ppermute | solution.py:539
  9.2 1.9 %collective-permute-start.2 = (f32[2,8,4096]{2,1,0:T(8,128)S(1)}, f32[2,8,4096]{2,1,0:T(8,128)S(1)}, u32[]{:S(2)}, u32[]{:S(2)}) collective-permute-start(f32[2,8,4096]{2,1,0:T(8,128)S(1)} %get-tuple-element.51), channel_id=1, source_target_pairs={{0,5},{1,6},{2,7},{3,0},{4,1},{5,2},{6,3},{7,4},{8,13},{9,14},{10,... | collective-permute-start | bytes 786440 | tf_op jit(solution)/shard_map/ppermute | solution.py:539
  11.1 1.6 %collective-permute-start.3 = (f32[2,8,4096]{2,1,0:T(8,128)S(1)}, f32[2,8,4096]{2,1,0:T(8,128)S(1)}, u32[]{:S(2)}, u32[]{:S(2)}) collective-permute-start(f32[2,8,4096]{2,1,0:T(8,128)S(1)} %get-tuple-element.52), channel_id=1, source_target_pairs={{0,2},{1,3},{2,4},{3,5},{4,6},{5,7},{6,0},{7,1},{8,10},{9,11},{10,... | collective-permute-start | bytes 786440 | tf_op jit(solution)/shard_map/ppermute | solution.py:539
  12.7 2.2 %collective-permute-start.4 = (f32[2,8,4096]{2,1,0:T(8,128)S(1)}, f32[2,8,4096]{2,1,0:T(8,128)S(1)}, u32[]{:S(2)}, u32[]{:S(2)}) collective-permute-start(f32[2,8,4096]{2,1,0:T(8,128)S(1)} %get-tuple-element.53), channel_id=1, source_target_pairs={{0,6},{1,7},{2,0},{3,1},{4,2},{5,3},{6,4},{7,5},{8,14},{9,15},{10,... | collective-permute-start | bytes 786440 | tf_op jit(solution)/shard_map/ppermute | solution.py:539
  15.0 20.4 %collective-permute-done.refs_1_ = f32[2,8,4096]{2,1,0:T(8,128)S(1)} collective-permute-done((f32[2,8,4096]{2,1,0:T(8,128)S(1)}, f32[2,8,4096]{2,1,0:T(8,128)S(1)}, u32[]{:S(2)}, u32[]{:S(2)}) %collective-permute-start) | collective-permute-done | bytes 262176 | tf_op jit(solution)/shard_map/ppermute | solution.py:539
  35.3 4.0 %collective-permute-done.1.refs_2_ = f32[2,8,4096]{2,1,0:T(8,128)S(1)} collective-permute-done((f32[2,8,4096]{2,1,0:T(8,128)S(1)}, f32[2,8,4096]{2,1,0:T(8,128)S(1)}, u32[]{:S(2)}, u32[]{:S(2)}) %collective-permute-start.1) | collective-permute-done | bytes 262176 | tf_op jit(solution)/shard_map/ppermute | solution.py:539
  39.3 3.8 %collective-permute-done.5.refs_6_ = f32[2,8,4096]{2,1,0:T(8,128)S(1)} collective-permute-done((f32[2,8,4096]{2,1,0:T(8,128)S(1)}, f32[2,8,4096]{2,1,0:T(8,128)S(1)}, u32[]{:S(2)}, u32[]{:S(2)}) %collective-permute-start.5) | collective-permute-done | bytes 262176 | tf_op jit(solution)/shard_map/ppermute | solution.py:539
  43.2 6.7 %unpack.1 = (f32[16,16,8,256]{3,2,1,0:T(8,128)S(1)}, f32[2,16,8,256]{3,2,1,0:T(8,128)S(1)}, f32[2,16,8,256]{3,2,1,0:T(8,128)S(1)}, f32[16,2,8,256]{3,2,1,0:T(8,1...) custom-call(s32[17]{0:T(128)S(1)} %get-tuple-element.47.table, ...), custom_call_target="tpu_custom_call" | custom-call | tf_op jit(solution)/shard_map/unpack/pallas_call | solution.py:205
  50.0 2.9 %collective-permute-start.11 = (f32[16,8,256]{2,1,0:T(8,128)S(1)}, f32[16,8,256]{2,1,0:T(8,128)S(1)}, u32[]{:S(2)}, u32[]{:S(2)}) collective-permute-start(f32[16,8,256]{2,1,0:T(8,128)S(1)} %get-tuple-element.65), channel_id=1, source_target_pairs={{0,1},{1,0},{2,3},{3,2},{4,5},{5,4},{6,7},{7,6},{8,9},{9,8},{10,11... | collective-permute-start | bytes 393224 | tf_op jit(solution)/shard_map/ppermute | solution.py:517
  52.9 3.7 %collective-permute-start.8 = (f32[2,16,8,256]{3,2,1,0:T(8,128)S(1)}, f32[2,16,8,256]{3,2,1,0:T(8,128)S(1)}, u32[]{:S(2)}, u32[]{:S(2)}) collective-permute-start(f32[2,16,8,256]{3,2,1,0:T(8,128)S(1)} %get-tuple-element.59), channel_id=1, source_target_pairs={{0,8},{8,16},{16,24},{1,9},{9,17},{17,25},{2,10},{10,18},{18,26},{... | collective-permute-start | bytes 786440 | tf_op jit(solution)/shard_map/ppermute | solution.py:529
  56.7 9.0 %collective-permute-start.12 = (f32[16,8,256]{2,1,0:T(8,128)S(1)}, f32[16,8,256]{2,1,0:T(8,128)S(1)}, u32[]{:S(2)}, u32[]{:S(2)}) collective-permute-start(f32[16,8,256]{2,1,0:T(8,128)S(1)} %add.18), channel_id=1, source_target_pairs={{0,2},{1,3},{2,0},{3,1},{4,6},{5,7},{6,4},{7,5},{8,10},{9,11},{10,... | collective-permute-start | bytes 393224 | tf_op jit(solution)/shard_map/ppermute | solution.py:517
  65.7 2.4 %collective-permute-start.9 = (f32[16,2,8,256]{3,2,1,0:T(8,128)S(1)}, f32[16,2,8,256]{3,2,1,0:T(8,128)S(1)}, u32[]{:S(2)}, u32[]{:S(2)}) collective-permute-start(f32[16,2,8,256]{3,2,1,0:T(8,128)S(1)} %get-tuple-element.60), channel_id=1, source_target_pairs={{1,0},{2,1},{3,2},{4,3},{5,4},{6,5},{7,6},{0,7},{9,8},{10,9},{11,1... | collective-permute-start | bytes 786440 | tf_op jit(solution)/shard_map/ppermute | solution.py:530
  68.1 1.3 %collective-permute-start.10 = (f32[2,16,8,256]{3,2,1,0:T(8,128)S(1)}, f32[2,16,8,256]{3,2,1,0:T(8,128)S(1)}, u32[]{:S(2)}, u32[]{:S(2)}) collective-permute-start(f32[2,16,8,256]{3,2,1,0:T(8,128)S(1)} %get-tuple-element.61), channel_id=1, source_target_pairs={{8,0},{16,8},{24,16},{9,1},{17,9},{25,17},{10,2},{18,10},{26,18},{... | collective-permute-start | bytes 786440 | tf_op jit(solution)/shard_map/ppermute | solution.py:531
  69.4 3.4 %inner_stage.2 = (f32[16,16,8,256]{3,2,1,0:T(8,128)S(1)}, f32[16,16,8,256]{3,2,1,0:T(8,128)S(1)}, f32[16,16,8,256]{3,2,1,0:T(8,128)S(1)}) custom-call(f32[16,16,8,256]{3,2,1,0:T(8,128)S(1)} %get-tuple-element.57.field, f32[8,24]{1,0:T(8,128)S(1)} %get-tuple-element.62.weights, f32[8,256]{1,0:T(8,128)S(1)} %get-tuple-element.63.ratio, ...), custom_call_target="tpu_custom_call" | custom-call | tf_op jit(solution)/shard_map/inner_stage/pallas_call | solution.py:326
  73.5 3.9 %collective-permute-done.10.high_rad = f32[2,16,8,256]{3,2,1,0:T(8,128)S(1)} collective-permute-done((f32[2,16,8,256]{3,2,1,0:T(8,128)S(1)}, f32[2,16,8,256]{3,2,1,0:T(8,128)S(1)}, u32[]{:S(2)}, u32[]{:S(2)}) %collective-permute-start.10) | collective-permute-done | bytes 262176 | tf_op jit(solution)/shard_map/ppermute | solution.py:531
  77.4 3.6 %outer_stage.2 = (f32[16,16,8,256]{3,2,1,0:T(8,128)S(1)}, f32[16,16,8,256]{3,2,1,0:T(8,128)S(1)}, f32[16,16,8,256]{3,2,1,0:T(8,128)S(1)}) custom-call(f32[16,16,8,256]{3,2,1,0:T(8,128)S(1)} %get-tuple-element.57.field, f32[16,2,8,256]{3,2,1,0:T(8,128)S(1)} %collective-permute-done.7.low_azi, ...), custom_call_target="tpu_custom_call", output_to_operand_aliasing={{0}: (8, {}), {1}: (9, {}), {2}: (10, {})} | custom-call | tf_op jit(solution)/shard_map/outer_stage/pallas_call | solution.py:357
  82.4 4.3 %collective-permute-start.15 = (f32[2,16,8,256]{3,2,1,0:T(8,128)S(1)}, f32[2,16,8,256]{3,2,1,0:T(8,128)S(1)}, u32[]{:S(2)}, u32[]{:S(2)}) collective-permute-start(f32[2,16,8,256]{3,2,1,0:T(8,128)S(1)} %get-tuple-element.78), channel_id=1, source_target_pairs={{0,8},{8,16},{16,24},{1,9},{9,17},{17,25},{2,10},{10,18},{18,26},{... | collective-permute-start | bytes 786440 | tf_op jit(solution)/shard_map/ppermute | solution.py:529
  86.7 1.6 %collective-permute-start.19 = (f32[16,8,256]{2,1,0:T(8,128)S(1)}, f32[16,8,256]{2,1,0:T(8,128)S(1)}, u32[]{:S(2)}, u32[]{:S(2)}) collective-permute-start(f32[16,8,256]{2,1,0:T(8,128)S(1)} %add.21), channel_id=1, source_target_pairs={{0,2},{1,3},{2,0},{3,1},{4,6},{5,7},{6,4},{7,5},{8,10},{9,11},{10,... | collective-permute-start | bytes 393224 | tf_op jit(solution)/shard_map/ppermute | solution.py:517
  88.3 1.5 %collective-permute-start.16 = (f32[16,2,8,256]{3,2,1,0:T(8,128)S(1)}, f32[16,2,8,256]{3,2,1,0:T(8,128)S(1)}, u32[]{:S(2)}, u32[]{:S(2)}) collective-permute-start(f32[16,2,8,256]{3,2,1,0:T(8,128)S(1)} %get-tuple-element.79), channel_id=1, source_target_pairs={{1,0},{2,1},{3,2},{4,3},{5,4},{6,5},{7,6},{0,7},{9,8},{10,9},{11,1... | collective-permute-start | bytes 786440 | tf_op jit(solution)/shard_map/ppermute | solution.py:530
  91.1 3.4 %inner_stage.3 = (f32[16,16,8,256]{3,2,1,0:T(8,128)S(1)}, f32[16,16,8,256]{3,2,1,0:T(8,128)S(1)}, f32[16,16,8,256]{3,2,1,0:T(8,128)S(1)}) custom-call(f32[16,16,8,256]{3,2,1,0:T(8,128)S(1)} %get-tuple-element.76.field, f32[8,24]{1,0:T(8,128)S(1)} %get-tuple-element.62.weights, f32[8,256]{1,0:T(8,128)S(1)} %get-tuple-element.63.ratio, ...), custom_call_target="tpu_custom_call" | custom-call | tf_op jit(solution)/shard_map/inner_stage/pallas_call | solution.py:326
  95.3 5.4 %collective-permute-done.17.high_rad = f32[2,16,8,256]{3,2,1,0:T(8,128)S(1)} collective-permute-done((f32[2,16,8,256]{3,2,1,0:T(8,128)S(1)}, f32[2,16,8,256]{3,2,1,0:T(8,128)S(1)}, u32[]{:S(2)}, u32[]{:S(2)}) %collective-permute-start.17) | collective-permute-done | bytes 262176 | tf_op jit(solution)/shard_map/ppermute | solution.py:531
  100.7 3.6 %outer_stage.3 = (f32[16,16,8,256]{3,2,1,0:T(8,128)S(1)}, f32[16,16,8,256]{3,2,1,0:T(8,128)S(1)}, f32[16,16,8,256]{3,2,1,0:T(8,128)S(1)}) custom-call(f32[16,16,8,256]{3,2,1,0:T(8,128)S(1)} %get-tuple-element.76.field, f32[16,2,8,256]{3,2,1,0:T(8,128)S(1)} %collective-permute-done.14.low_azi, ...), custom_call_target="tpu_custom_call", output_to_operand_aliasing={{0}: (8, {}), {1}: (9, {}), {2}: (10, {})} | custom-call | tf_op jit(solution)/shard_map/outer_stage/pallas_call | solution.py:357
  104.4 3.9 %final_stage.1 = (f32[16,8,4096]{2,1,0:T(8,128)}, f32[16,8,4096]{2,1,0:T(8,128)}) custom-call(f32[16,8,4096]{2,1,0:T(8,128)S(1)} %get-tuple-element.56.held, f32[16,16,8,256]{3,2,1,0:T(8,128)S(1)} %get-tuple-element.88.settled, f32[16,16,8,256]{3,2,1,0:T(8,128)S(1)} %get-tuple-element.89.sums_azi, f32[16,16,8,256]{3,2,1,0:T(8,128)S(1)} %get-tuple-element.90.jumps_azi, ...), custom_call_target="tpu_custom_call" | custom-call | tf_op jit(solution)/shard_map/final_stage/pallas_call | solution.py:496
  (40 shorter events, 5.8 us)
Async XLA Ops:
  0.6 42.6 %copy-start = (f32[3,8,8]{2,1,0:T(8,128)S(1)}, f32[3,8,8]{2,1,0:T(8,128)}, u32[]{:S(2)}) copy-start(f32[3,8,8]{2,1,0:T(8,128)} %coupling.1) | copy-start | bytes 2308
  1.3 41.9 %copy-start.2 = (s32[16]{0:T(128)S(1)}, s32[16]{0:T(128)}, u32[]{:S(2)}) copy-start(s32[16]{0:T(128)} %levels.1) | copy-start | bytes 196
  1.3 41.9 %copy-start.3 = (f32[8]{0:T(128)S(1)}, f32[8]{0:T(128)}, u32[]{:S(2)}) copy-start(f32[8]{0:T(128)} %damping.1) | copy-start | bytes 100
  4.4 30.9 %collective-permute-start = (f32[2,8,4096]{2,1,0:T(8,128)S(1)}, f32[2,8,4096]{2,1,0:T(8,128)S(1)}, u32[]{:S(2)}, u32[]{:S(2)}) collective-permute-start(f32[2,8,4096]{2,1,0:T(8,128)S(1)} %get-tuple-element.49), channel_id=1, source_target_pairs={{0,4},{1,5},{2,6},{3,7},{4,0},{5,1},{6,2},{7,3},{8,12},{9,13},{10,... | collective-permute-start | bytes 786440 | tf_op jit(solution)/shard_map/ppermute | solution.py:539
  8.5 30.8 %collective-permute-start.1 = (f32[2,8,4096]{2,1,0:T(8,128)S(1)}, f32[2,8,4096]{2,1,0:T(8,128)S(1)}, u32[]{:S(2)}, u32[]{:S(2)}) collective-permute-start(f32[2,8,4096]{2,1,0:T(8,128)S(1)} %get-tuple-element.50), channel_id=1, source_target_pairs={{0,3},{1,4},{2,5},{3,6},{4,7},{5,0},{6,1},{7,2},{8,11},{9,12},{10,... | collective-permute-start | bytes 786440 | tf_op jit(solution)/shard_map/ppermute | solution.py:539
  9.2 30.1 %collective-permute-start.2 = (f32[2,8,4096]{2,1,0:T(8,128)S(1)}, f32[2,8,4096]{2,1,0:T(8,128)S(1)}, u32[]{:S(2)}, u32[]{:S(2)}) collective-permute-start(f32[2,8,4096]{2,1,0:T(8,128)S(1)} %get-tuple-element.51), channel_id=1, source_target_pairs={{0,5},{1,6},{2,7},{3,0},{4,1},{5,2},{6,3},{7,4},{8,13},{9,14},{10,... | collective-permute-start | bytes 786440 | tf_op jit(solution)/shard_map/ppermute | solution.py:539
  11.1 28.2 %collective-permute-start.3 = (f32[2,8,4096]{2,1,0:T(8,128)S(1)}, f32[2,8,4096]{2,1,0:T(8,128)S(1)}, u32[]{:S(2)}, u32[]{:S(2)}) collective-permute-start(f32[2,8,4096]{2,1,0:T(8,128)S(1)} %get-tuple-element.52), channel_id=1, source_target_pairs={{0,2},{1,3},{2,4},{3,5},{4,6},{5,7},{6,0},{7,1},{8,10},{9,11},{10,... | collective-permute-start | bytes 786440 | tf_op jit(solution)/shard_map/ppermute | solution.py:539
  12.7 26.6 %collective-permute-start.4 = (f32[2,8,4096]{2,1,0:T(8,128)S(1)}, f32[2,8,4096]{2,1,0:T(8,128)S(1)}, u32[]{:S(2)}, u32[]{:S(2)}) collective-permute-start(f32[2,8,4096]{2,1,0:T(8,128)S(1)} %get-tuple-element.53), channel_id=1, source_target_pairs={{0,6},{1,7},{2,0},{3,1},{4,2},{5,3},{6,4},{7,5},{8,14},{9,15},{10,... | collective-permute-start | bytes 786440 | tf_op jit(solution)/shard_map/ppermute | solution.py:539
  35.3 7.8 %collective-permute-start.5 = (f32[2,8,4096]{2,1,0:T(8,128)S(1)}, f32[2,8,4096]{2,1,0:T(8,128)S(1)}, u32[]{:S(2)}, u32[]{:S(2)}) collective-permute-start(f32[2,8,4096]{2,1,0:T(8,128)S(1)} %get-tuple-element.54), channel_id=1, source_target_pairs={{0,1},{1,2},{2,3},{3,4},{4,5},{5,6},{6,7},{7,0},{8,9},{9,10},{10,1... | collective-permute-start | bytes 786440 | tf_op jit(solution)/shard_map/ppermute | solution.py:539
  39.3 3.9 %collective-permute-start.6 = (f32[2,8,4096]{2,1,0:T(8,128)S(1)}, f32[2,8,4096]{2,1,0:T(8,128)S(1)}, u32[]{:S(2)}, u32[]{:S(2)}) collective-permute-start(f32[2,8,4096]{2,1,0:T(8,128)S(1)} %get-tuple-element.55), channel_id=1, source_target_pairs={{0,7},{1,0},{2,1},{3,2},{4,3},{5,4},{6,5},{7,6},{8,15},{9,8},{10,9... | collective-permute-start | bytes 786440 | tf_op jit(solution)/shard_map/ppermute | solution.py:539
  50.0 6.7 %collective-permute-start.11 = (f32[16,8,256]{2,1,0:T(8,128)S(1)}, f32[16,8,256]{2,1,0:T(8,128)S(1)}, u32[]{:S(2)}, u32[]{:S(2)}) collective-permute-start(f32[16,8,256]{2,1,0:T(8,128)S(1)} %get-tuple-element.65), channel_id=1, source_target_pairs={{0,1},{1,0},{2,3},{3,2},{4,5},{5,4},{6,7},{7,6},{8,9},{9,8},{10,11... | collective-permute-start | bytes 393224 | tf_op jit(solution)/shard_map/ppermute | solution.py:517
  52.9 20.6 %collective-permute-start.7 = (f32[16,2,8,256]{3,2,1,0:T(8,128)S(1)}, f32[16,2,8,256]{3,2,1,0:T(8,128)S(1)}, u32[]{:S(2)}, u32[]{:S(2)}) collective-permute-start(f32[16,2,8,256]{3,2,1,0:T(8,128)S(1)} %get-tuple-element.58), channel_id=1, source_target_pairs={{0,1},{1,2},{2,3},{3,4},{4,5},{5,6},{6,7},{7,0},{8,9},{9,10},{10,1... | collective-permute-start | bytes 786440 | tf_op jit(solution)/shard_map/ppermute | solution.py:528
  52.9 20.6 %collective-permute-start.8 = (f32[2,16,8,256]{3,2,1,0:T(8,128)S(1)}, f32[2,16,8,256]{3,2,1,0:T(8,128)S(1)}, u32[]{:S(2)}, u32[]{:S(2)}) collective-permute-start(f32[2,16,8,256]{3,2,1,0:T(8,128)S(1)} %get-tuple-element.59), channel_id=1, source_target_pairs={{0,8},{8,16},{16,24},{1,9},{9,17},{17,25},{2,10},{10,18},{18,26},{... | collective-permute-start | bytes 786440 | tf_op jit(solution)/shard_map/ppermute | solution.py:529
  56.7 16.1 %collective-permute-start.12 = (f32[16,8,256]{2,1,0:T(8,128)S(1)}, f32[16,8,256]{2,1,0:T(8,128)S(1)}, u32[]{:S(2)}, u32[]{:S(2)}) collective-permute-start(f32[16,8,256]{2,1,0:T(8,128)S(1)} %add.18), channel_id=1, source_target_pairs={{0,2},{1,3},{2,0},{3,1},{4,6},{5,7},{6,4},{7,5},{8,10},{9,11},{10,... | collective-permute-start | bytes 393224 | tf_op jit(solution)/shard_map/ppermute | solution.py:517
  65.7 7.8 %collective-permute-start.9 = (f32[16,2,8,256]{3,2,1,0:T(8,128)S(1)}, f32[16,2,8,256]{3,2,1,0:T(8,128)S(1)}, u32[]{:S(2)}, u32[]{:S(2)}) collective-permute-start(f32[16,2,8,256]{3,2,1,0:T(8,128)S(1)} %get-tuple-element.60), channel_id=1, source_target_pairs={{1,0},{2,1},{3,2},{4,3},{5,4},{6,5},{7,6},{0,7},{9,8},{10,9},{11,1... | collective-permute-start | bytes 786440 | tf_op jit(solution)/shard_map/ppermute | solution.py:530
  68.1 9.3 %collective-permute-start.10 = (f32[2,16,8,256]{3,2,1,0:T(8,128)S(1)}, f32[2,16,8,256]{3,2,1,0:T(8,128)S(1)}, u32[]{:S(2)}, u32[]{:S(2)}) collective-permute-start(f32[2,16,8,256]{3,2,1,0:T(8,128)S(1)} %get-tuple-element.61), channel_id=1, source_target_pairs={{8,0},{16,8},{24,16},{9,1},{17,9},{25,17},{10,2},{18,10},{26,18},{... | collective-permute-start | bytes 786440 | tf_op jit(solution)/shard_map/ppermute | solution.py:531
  72.8 8.2 %collective-permute-start.13 = (f32[16,8,256]{2,1,0:T(8,128)S(1)}, f32[16,8,256]{2,1,0:T(8,128)S(1)}, u32[]{:S(2)}, u32[]{:S(2)}) collective-permute-start(f32[16,8,256]{2,1,0:T(8,128)S(1)} %add.19), channel_id=1, source_target_pairs={{0,4},{1,5},{2,6},{3,7},{4,0},{5,1},{6,2},{7,3},{8,12},{9,13},{10,... | collective-permute-start | bytes 393224 | tf_op jit(solution)/shard_map/ppermute | solution.py:517
  81.8 4.9 %collective-permute-start.18 = (f32[16,8,256]{2,1,0:T(8,128)S(1)}, f32[16,8,256]{2,1,0:T(8,128)S(1)}, u32[]{:S(2)}, u32[]{:S(2)}) collective-permute-start(f32[16,8,256]{2,1,0:T(8,128)S(1)} %get-tuple-element.81), channel_id=1, source_target_pairs={{0,1},{1,0},{2,3},{3,2},{4,5},{5,4},{6,7},{7,6},{8,9},{9,8},{10,11... | collective-permute-start | bytes 393224 | tf_op jit(solution)/shard_map/ppermute | solution.py:517
  81.9 13.4 %collective-permute-start.14 = (f32[16,2,8,256]{3,2,1,0:T(8,128)S(1)}, f32[16,2,8,256]{3,2,1,0:T(8,128)S(1)}, u32[]{:S(2)}, u32[]{:S(2)}) collective-permute-start(f32[16,2,8,256]{3,2,1,0:T(8,128)S(1)} %get-tuple-element.77), channel_id=1, source_target_pairs={{0,1},{1,2},{2,3},{3,4},{4,5},{5,6},{6,7},{7,0},{8,9},{9,10},{10,1... | collective-permute-start | bytes 786440 | tf_op jit(solution)/shard_map/ppermute | solution.py:528
  82.4 12.9 %collective-permute-start.15 = (f32[2,16,8,256]{3,2,1,0:T(8,128)S(1)}, f32[2,16,8,256]{3,2,1,0:T(8,128)S(1)}, u32[]{:S(2)}, u32[]{:S(2)}) collective-permute-start(f32[2,16,8,256]{3,2,1,0:T(8,128)S(1)} %get-tuple-element.78), channel_id=1, source_target_pairs={{0,8},{8,16},{16,24},{1,9},{9,17},{17,25},{2,10},{10,18},{18,26},{... | collective-permute-start | bytes 786440 | tf_op jit(solution)/shard_map/ppermute | solution.py:529
  86.7 7.8 %collective-permute-start.19 = (f32[16,8,256]{2,1,0:T(8,128)S(1)}, f32[16,8,256]{2,1,0:T(8,128)S(1)}, u32[]{:S(2)}, u32[]{:S(2)}) collective-permute-start(f32[16,8,256]{2,1,0:T(8,128)S(1)} %add.21), channel_id=1, source_target_pairs={{0,2},{1,3},{2,0},{3,1},{4,6},{5,7},{6,4},{7,5},{8,10},{9,11},{10,... | collective-permute-start | bytes 393224 | tf_op jit(solution)/shard_map/ppermute | solution.py:517
  88.3 7.0 %collective-permute-start.16 = (f32[16,2,8,256]{3,2,1,0:T(8,128)S(1)}, f32[16,2,8,256]{3,2,1,0:T(8,128)S(1)}, u32[]{:S(2)}, u32[]{:S(2)}) collective-permute-start(f32[16,2,8,256]{3,2,1,0:T(8,128)S(1)} %get-tuple-element.79), channel_id=1, source_target_pairs={{1,0},{2,1},{3,2},{4,3},{5,4},{6,5},{7,6},{0,7},{9,8},{10,9},{11,1... | collective-permute-start | bytes 786440 | tf_op jit(solution)/shard_map/ppermute | solution.py:530
  89.8 10.9 %collective-permute-start.17 = (f32[2,16,8,256]{3,2,1,0:T(8,128)S(1)}, f32[2,16,8,256]{3,2,1,0:T(8,128)S(1)}, u32[]{:S(2)}, u32[]{:S(2)}) collective-permute-start(f32[2,16,8,256]{3,2,1,0:T(8,128)S(1)} %get-tuple-element.80), channel_id=1, source_target_pairs={{8,0},{16,8},{24,16},{9,1},{17,9},{25,17},{10,2},{18,10},{26,18},{... | collective-permute-start | bytes 786440 | tf_op jit(solution)/shard_map/ppermute | solution.py:531
  94.5 9.9 %collective-permute-start.20 = (f32[16,8,256]{2,1,0:T(8,128)S(1)}, f32[16,8,256]{2,1,0:T(8,128)S(1)}, u32[]{:S(2)}, u32[]{:S(2)}) collective-permute-start(f32[16,8,256]{2,1,0:T(8,128)S(1)} %add.22), channel_id=1, source_target_pairs={{0,4},{1,5},{2,6},{3,7},{4,0},{5,1},{6,2},{7,3},{8,12},{9,13},{10,... | collective-permute-start | bytes 393224 | tf_op jit(solution)/shard_map/ppermute | solution.py:517
  (1 other events, 0.7 us)

commit v5 on v4

--- a/solution.py
+++ b/solution.py
@@ -347,9 +347,9 @@
         return padded[x + 2, y + 2]
 
     rest = (carry_slope, carry_plus, split_weights(weights), ratio, relax, outs)
-    sweep(get, (0, 2), (range(EDGE),), *rest)
+    sweep(get, (0, 2), (range(EDGE // 2), range(EDGE // 2, EDGE)), *rest)
     sweep(get, (2, EDGE - 2), (HEAD, TAIL), *rest, unroll=12)
-    sweep(get, (EDGE - 2, EDGE), (range(EDGE),), *rest)
+    sweep(get, (EDGE - 2, EDGE), (range(EDGE // 2), range(EDGE // 2, EDGE)), *rest)
 
 
 def outer_stage(field, halos, weights, ratio, relax, parts):

time: 109 us -> 109 us (level)
  no operation moved by 1% of the time
where the time goes in v5:
time: 109 us; the launch traced here: 108 us
  starting transfers between devices  40.6 us (37%)
  waiting for transfers between devices  37.6 us (34%)
  Pallas kernels  28.5 us (26%)
    ppermute x7, waiting for transfers between devices, on_device(): lax.ppermute(packed[d], 'azi', [(i, (i + d) % azi_count) for i in range(a...  28.2 us
    ppermute x6, starting transfers between devices, sum_azi(): other = lax.ppermute(values, 'azi', [(i, i ^ step) for i in range(count)])  15 us
    ppermute x7, starting transfers between devices, on_device(): lax.ppermute(packed[d], 'azi', [(i, (i + d) % azi_count) for i in range(a...  10.6 us
    ppermute x2, waiting for transfers between devices, exchange(): lax.ppermute(rad_head, 'rad', [(i + 1, i) for i in range(rad - 1)])  9.3 us
    ppermute x2, starting transfers between devices, exchange(): lax.ppermute(rad_tail, 'rad', [(i, i + 1) for i in range(rad - 1)])  8.03 us
    pallas_call x2, Pallas kernels, outer_stage(): pl.pallas_call(outer_kernel, out_shape=[pltpu.VMEM(field.shape, F32)] * 3...  7.32 us
    pallas_call x2, Pallas kernels, inner_stage(): pl.pallas_call(inner_kernel, out_shape=[pltpu.VMEM(field.shape, F32)] * 3...  6.74 us
    pallas_call x1, Pallas kernels, unpack(): pl.pallas_call(functools.partial(unpack_kernel, azi_count, block_shape[0]...  6.72 us
  transfers between devices with their start and end apart: 21, of which 6 were waited for; matrix products, arithmetic and copies ran while one was open for 0% of the time, Pallas kernels for 13%

profile of v5, /device:TPU:0, one launch (start us, length us, event | category | flops | bytes accessed | tf_op | source)
XLA Modules:
  0.0 108.4 jit_solution(8208293377420058311)
XLA Ops:
  1.3 3.1 %pack.1 = (f32[2,8,4096]{2,1,0:T(8,128)S(1)}, f32[2,8,4096]{2,1,0:T(8,128)S(1)}, f32[2,8,4096]{2,1,0:T(8,128)S(1)}, f32[2,8,4096]{2,1,0:T(8,128)S(1)}, f32[2,8,4...) custom-call(s32[512]{0:T(512)S(1)} %copy-done.1, ...), custom_call_target="tpu_custom_call" | custom-call | tf_op jit(solution)/shard_map/pack/pallas_call | solution.py:105
  4.4 4.1 %collective-permute-start = (f32[2,8,4096]{2,1,0:T(8,128)S(1)}, f32[2,8,4096]{2,1,0:T(8,128)S(1)}, u32[]{:S(2)}, u32[]{:S(2)}) collective-permute-start(f32[2,8,4096]{2,1,0:T(8,128)S(1)} %get-tuple-element.49), channel_id=1, source_target_pairs={{0,4},{1,5},{2,6},{3,7},{4,0},{5,1},{6,2},{7,3},{8,12},{9,13},{10,... | collective-permute-start | bytes 786440 | tf_op jit(solution)/shard_map/ppermute | solution.py:539
  9.2 1.9 %collective-permute-start.2 = (f32[2,8,4096]{2,1,0:T(8,128)S(1)}, f32[2,8,4096]{2,1,0:T(8,128)S(1)}, u32[]{:S(2)}, u32[]{:S(2)}) collective-permute-start(f32[2,8,4096]{2,1,0:T(8,128)S(1)} %get-tuple-element.51), channel_id=1, source_target_pairs={{0,5},{1,6},{2,7},{3,0},{4,1},{5,2},{6,3},{7,4},{8,13},{9,14},{10,... | collective-permute-start | bytes 786440 | tf_op jit(solution)/shard_map/ppermute | solution.py:539
  11.1 1.6 %collective-permute-start.3 = (f32[2,8,4096]{2,1,0:T(8,128)S(1)}, f32[2,8,4096]{2,1,0:T(8,128)S(1)}, u32[]{:S(2)}, u32[]{:S(2)}) collective-permute-start(f32[2,8,4096]{2,1,0:T(8,128)S(1)} %get-tuple-element.52), channel_id=1, source_target_pairs={{0,2},{1,3},{2,4},{3,5},{4,6},{5,7},{6,0},{7,1},{8,10},{9,11},{10,... | collective-permute-start | bytes 786440 | tf_op jit(solution)/shard_map/ppermute | solution.py:539
  12.7 2.2 %collective-permute-start.4 = (f32[2,8,4096]{2,1,0:T(8,128)S(1)}, f32[2,8,4096]{2,1,0:T(8,128)S(1)}, u32[]{:S(2)}, u32[]{:S(2)}) collective-permute-start(f32[2,8,4096]{2,1,0:T(8,128)S(1)} %get-tuple-element.53), channel_id=1, source_target_pairs={{0,6},{1,7},{2,0},{3,1},{4,2},{5,3},{6,4},{7,5},{8,14},{9,15},{10,... | collective-permute-start | bytes 786440 | tf_op jit(solution)/shard_map/ppermute | solution.py:539
  15.0 20.4 %collective-permute-done.refs_1_ = f32[2,8,4096]{2,1,0:T(8,128)S(1)} collective-permute-done((f32[2,8,4096]{2,1,0:T(8,128)S(1)}, f32[2,8,4096]{2,1,0:T(8,128)S(1)}, u32[]{:S(2)}, u32[]{:S(2)}) %collective-permute-start) | collective-permute-done | bytes 262176 | tf_op jit(solution)/shard_map/ppermute | solution.py:539
  35.3 4.0 %collective-permute-done.1.refs_2_ = f32[2,8,4096]{2,1,0:T(8,128)S(1)} collective-permute-done((f32[2,8,4096]{2,1,0:T(8,128)S(1)}, f32[2,8,4096]{2,1,0:T(8,128)S(1)}, u32[]{:S(2)}, u32[]{:S(2)}) %collective-permute-start.1) | collective-permute-done | bytes 262176 | tf_op jit(solution)/shard_map/ppermute | solution.py:539
  39.3 3.8 %collective-permute-done.5.refs_6_ = f32[2,8,4096]{2,1,0:T(8,128)S(1)} collective-permute-done((f32[2,8,4096]{2,1,0:T(8,128)S(1)}, f32[2,8,4096]{2,1,0:T(8,128)S(1)}, u32[]{:S(2)}, u32[]{:S(2)}) %collective-permute-start.5) | collective-permute-done | bytes 262176 | tf_op jit(solution)/shard_map/ppermute | solution.py:539
  43.2 6.7 %unpack.1 = (f32[16,16,8,256]{3,2,1,0:T(8,128)S(1)}, f32[2,16,8,256]{3,2,1,0:T(8,128)S(1)}, f32[2,16,8,256]{3,2,1,0:T(8,128)S(1)}, f32[16,2,8,256]{3,2,1,0:T(8,1...) custom-call(s32[17]{0:T(128)S(1)} %get-tuple-element.47.table, ...), custom_call_target="tpu_custom_call" | custom-call | tf_op jit(solution)/shard_map/unpack/pallas_call | solution.py:205
  50.0 2.9 %collective-permute-start.11 = (f32[16,8,256]{2,1,0:T(8,128)S(1)}, f32[16,8,256]{2,1,0:T(8,128)S(1)}, u32[]{:S(2)}, u32[]{:S(2)}) collective-permute-start(f32[16,8,256]{2,1,0:T(8,128)S(1)} %get-tuple-element.65), channel_id=1, source_target_pairs={{0,1},{1,0},{2,3},{3,2},{4,5},{5,4},{6,7},{7,6},{8,9},{9,8},{10,11... | collective-permute-start | bytes 393224 | tf_op jit(solution)/shard_map/ppermute | solution.py:517
  52.9 3.7 %collective-permute-start.8 = (f32[2,16,8,256]{3,2,1,0:T(8,128)S(1)}, f32[2,16,8,256]{3,2,1,0:T(8,128)S(1)}, u32[]{:S(2)}, u32[]{:S(2)}) collective-permute-start(f32[2,16,8,256]{3,2,1,0:T(8,128)S(1)} %get-tuple-element.59), channel_id=1, source_target_pairs={{0,8},{8,16},{16,24},{1,9},{9,17},{17,25},{2,10},{10,18},{18,26},{... | collective-permute-start | bytes 786440 | tf_op jit(solution)/shard_map/ppermute | solution.py:529
  56.7 9.0 %collective-permute-start.12 = (f32[16,8,256]{2,1,0:T(8,128)S(1)}, f32[16,8,256]{2,1,0:T(8,128)S(1)}, u32[]{:S(2)}, u32[]{:S(2)}) collective-permute-start(f32[16,8,256]{2,1,0:T(8,128)S(1)} %add.18), channel_id=1, source_target_pairs={{0,2},{1,3},{2,0},{3,1},{4,6},{5,7},{6,4},{7,5},{8,10},{9,11},{10,... | collective-permute-start | bytes 393224 | tf_op jit(solution)/shard_map/ppermute | solution.py:517
  65.7 2.4 %collective-permute-start.9 = (f32[16,2,8,256]{3,2,1,0:T(8,128)S(1)}, f32[16,2,8,256]{3,2,1,0:T(8,128)S(1)}, u32[]{:S(2)}, u32[]{:S(2)}) collective-permute-start(f32[16,2,8,256]{3,2,1,0:T(8,128)S(1)} %get-tuple-element.60), channel_id=1, source_target_pairs={{1,0},{2,1},{3,2},{4,3},{5,4},{6,5},{7,6},{0,7},{9,8},{10,9},{11,1... | collective-permute-start | bytes 786440 | tf_op jit(solution)/shard_map/ppermute | solution.py:530
  68.1 1.3 %collective-permute-start.10 = (f32[2,16,8,256]{3,2,1,0:T(8,128)S(1)}, f32[2,16,8,256]{3,2,1,0:T(8,128)S(1)}, u32[]{:S(2)}, u32[]{:S(2)}) collective-permute-start(f32[2,16,8,256]{3,2,1,0:T(8,128)S(1)} %get-tuple-element.61), channel_id=1, source_target_pairs={{8,0},{16,8},{24,16},{9,1},{17,9},{25,17},{10,2},{18,10},{26,18},{... | collective-permute-start | bytes 786440 | tf_op jit(solution)/shard_map/ppermute | solution.py:531
  69.4 3.4 %inner_stage.2 = (f32[16,16,8,256]{3,2,1,0:T(8,128)S(1)}, f32[16,16,8,256]{3,2,1,0:T(8,128)S(1)}, f32[16,16,8,256]{3,2,1,0:T(8,128)S(1)}) custom-call(f32[16,16,8,256]{3,2,1,0:T(8,128)S(1)} %get-tuple-element.57.field, f32[8,24]{1,0:T(8,128)S(1)} %get-tuple-element.62.weights, f32[8,256]{1,0:T(8,128)S(1)} %get-tuple-element.63.ratio, ...), custom_call_target="tpu_custom_call" | custom-call | tf_op jit(solution)/shard_map/inner_stage/pallas_call | solution.py:326
  73.5 3.9 %collective-permute-done.10.high_rad = f32[2,16,8,256]{3,2,1,0:T(8,128)S(1)} collective-permute-done((f32[2,16,8,256]{3,2,1,0:T(8,128)S(1)}, f32[2,16,8,256]{3,2,1,0:T(8,128)S(1)}, u32[]{:S(2)}, u32[]{:S(2)}) %collective-permute-start.10) | collective-permute-done | bytes 262176 | tf_op jit(solution)/shard_map/ppermute | solution.py:531
  77.4 3.7 %outer_stage.2 = (f32[16,16,8,256]{3,2,1,0:T(8,128)S(1)}, f32[16,16,8,256]{3,2,1,0:T(8,128)S(1)}, f32[16,16,8,256]{3,2,1,0:T(8,128)S(1)}) custom-call(f32[16,16,8,256]{3,2,1,0:T(8,128)S(1)} %get-tuple-element.57.field, f32[16,2,8,256]{3,2,1,0:T(8,128)S(1)} %collective-permute-done.7.low_azi, ...), custom_call_target="tpu_custom_call", output_to_operand_aliasing={{0}: (8, {}), {1}: (9, {}), {2}: (10, {})} | custom-call | tf_op jit(solution)/shard_map/outer_stage/pallas_call | solution.py:357
  82.4 4.3 %collective-permute-start.15 = (f32[2,16,8,256]{3,2,1,0:T(8,128)S(1)}, f32[2,16,8,256]{3,2,1,0:T(8,128)S(1)}, u32[]{:S(2)}, u32[]{:S(2)}) collective-permute-start(f32[2,16,8,256]{3,2,1,0:T(8,128)S(1)} %get-tuple-element.78), channel_id=1, source_target_pairs={{0,8},{8,16},{16,24},{1,9},{9,17},{17,25},{2,10},{10,18},{18,26},{... | collective-permute-start | bytes 786440 | tf_op jit(solution)/shard_map/ppermute | solution.py:529
  86.7 1.6 %collective-permute-start.19 = (f32[16,8,256]{2,1,0:T(8,128)S(1)}, f32[16,8,256]{2,1,0:T(8,128)S(1)}, u32[]{:S(2)}, u32[]{:S(2)}) collective-permute-start(f32[16,8,256]{2,1,0:T(8,128)S(1)} %add.21), channel_id=1, source_target_pairs={{0,2},{1,3},{2,0},{3,1},{4,6},{5,7},{6,4},{7,5},{8,10},{9,11},{10,... | collective-permute-start | bytes 393224 | tf_op jit(solution)/shard_map/ppermute | solution.py:517
  88.3 1.5 %collective-permute-start.16 = (f32[16,2,8,256]{3,2,1,0:T(8,128)S(1)}, f32[16,2,8,256]{3,2,1,0:T(8,128)S(1)}, u32[]{:S(2)}, u32[]{:S(2)}) collective-permute-start(f32[16,2,8,256]{3,2,1,0:T(8,128)S(1)} %get-tuple-element.79), channel_id=1, source_target_pairs={{1,0},{2,1},{3,2},{4,3},{5,4},{6,5},{7,6},{0,7},{9,8},{10,9},{11,1... | collective-permute-start | bytes 786440 | tf_op jit(solution)/shard_map/ppermute | solution.py:530
  91.1 3.4 %inner_stage.3 = (f32[16,16,8,256]{3,2,1,0:T(8,128)S(1)}, f32[16,16,8,256]{3,2,1,0:T(8,128)S(1)}, f32[16,16,8,256]{3,2,1,0:T(8,128)S(1)}) custom-call(f32[16,16,8,256]{3,2,1,0:T(8,128)S(1)} %get-tuple-element.76.field, f32[8,24]{1,0:T(8,128)S(1)} %get-tuple-element.62.weights, f32[8,256]{1,0:T(8,128)S(1)} %get-tuple-element.63.ratio, ...), custom_call_target="tpu_custom_call" | custom-call | tf_op jit(solution)/shard_map/inner_stage/pallas_call | solution.py:326
  95.3 5.4 %collective-permute-done.17.high_rad = f32[2,16,8,256]{3,2,1,0:T(8,128)S(1)} collective-permute-done((f32[2,16,8,256]{3,2,1,0:T(8,128)S(1)}, f32[2,16,8,256]{3,2,1,0:T(8,128)S(1)}, u32[]{:S(2)}, u32[]{:S(2)}) %collective-permute-start.17) | collective-permute-done | bytes 262176 | tf_op jit(solution)/shard_map/ppermute | solution.py:531
  100.7 3.7 %outer_stage.3 = (f32[16,16,8,256]{3,2,1,0:T(8,128)S(1)}, f32[16,16,8,256]{3,2,1,0:T(8,128)S(1)}, f32[16,16,8,256]{3,2,1,0:T(8,128)S(1)}) custom-call(f32[16,16,8,256]{3,2,1,0:T(8,128)S(1)} %get-tuple-element.76.field, f32[16,2,8,256]{3,2,1,0:T(8,128)S(1)} %collective-permute-done.14.low_azi, ...), custom_call_target="tpu_custom_call", output_to_operand_aliasing={{0}: (8, {}), {1}: (9, {}), {2}: (10, {})} | custom-call | tf_op jit(solution)/shard_map/outer_stage/pallas_call | solution.py:357
  104.4 3.9 %final_stage.1 = (f32[16,8,4096]{2,1,0:T(8,128)}, f32[16,8,4096]{2,1,0:T(8,128)}) custom-call(f32[16,8,4096]{2,1,0:T(8,128)S(1)} %get-tuple-element.56.held, f32[16,16,8,256]{3,2,1,0:T(8,128)S(1)} %get-tuple-element.88.settled, f32[16,16,8,256]{3,2,1,0:T(8,128)S(1)} %get-tuple-element.89.sums_azi, f32[16,16,8,256]{3,2,1,0:T(8,128)S(1)} %get-tuple-element.90.jumps_azi, ...), custom_call_target="tpu_custom_call" | custom-call | tf_op jit(solution)/shard_map/final_stage/pallas_call | solution.py:496
  (40 shorter events, 5.8 us)
Async XLA Ops:
  0.6 42.6 %copy-start = (f32[3,8,8]{2,1,0:T(8,128)S(1)}, f32[3,8,8]{2,1,0:T(8,128)}, u32[]{:S(2)}) copy-start(f32[3,8,8]{2,1,0:T(8,128)} %coupling.1) | copy-start | bytes 2308
  1.3 41.9 %copy-start.2 = (s32[16]{0:T(128)S(1)}, s32[16]{0:T(128)}, u32[]{:S(2)}) copy-start(s32[16]{0:T(128)} %levels.1) | copy-start | bytes 196
  1.3 41.9 %copy-start.3 = (f32[8]{0:T(128)S(1)}, f32[8]{0:T(128)}, u32[]{:S(2)}) copy-start(f32[8]{0:T(128)} %damping.1) | copy-start | bytes 100
  4.4 30.9 %collective-permute-start = (f32[2,8,4096]{2,1,0:T(8,128)S(1)}, f32[2,8,4096]{2,1,0:T(8,128)S(1)}, u32[]{:S(2)}, u32[]{:S(2)}) collective-permute-start(f32[2,8,4096]{2,1,0:T(8,128)S(1)} %get-tuple-element.49), channel_id=1, source_target_pairs={{0,4},{1,5},{2,6},{3,7},{4,0},{5,1},{6,2},{7,3},{8,12},{9,13},{10,... | collective-permute-start | bytes 786440 | tf_op jit(solution)/shard_map/ppermute | solution.py:539
  8.5 30.8 %collective-permute-start.1 = (f32[2,8,4096]{2,1,0:T(8,128)S(1)}, f32[2,8,4096]{2,1,0:T(8,128)S(1)}, u32[]{:S(2)}, u32[]{:S(2)}) collective-permute-start(f32[2,8,4096]{2,1,0:T(8,128)S(1)} %get-tuple-element.50), channel_id=1, source_target_pairs={{0,3},{1,4},{2,5},{3,6},{4,7},{5,0},{6,1},{7,2},{8,11},{9,12},{10,... | collective-permute-start | bytes 786440 | tf_op jit(solution)/shard_map/ppermute | solution.py:539
  9.2 30.1 %collective-permute-start.2 = (f32[2,8,4096]{2,1,0:T(8,128)S(1)}, f32[2,8,4096]{2,1,0:T(8,128)S(1)}, u32[]{:S(2)}, u32[]{:S(2)}) collective-permute-start(f32[2,8,4096]{2,1,0:T(8,128)S(1)} %get-tuple-element.51), channel_id=1, source_target_pairs={{0,5},{1,6},{2,7},{3,0},{4,1},{5,2},{6,3},{7,4},{8,13},{9,14},{10,... | collective-permute-start | bytes 786440 | tf_op jit(solution)/shard_map/ppermute | solution.py:539
  11.1 28.2 %collective-permute-start.3 = (f32[2,8,4096]{2,1,0:T(8,128)S(1)}, f32[2,8,4096]{2,1,0:T(8,128)S(1)}, u32[]{:S(2)}, u32[]{:S(2)}) collective-permute-start(f32[2,8,4096]{2,1,0:T(8,128)S(1)} %get-tuple-element.52), channel_id=1, source_target_pairs={{0,2},{1,3},{2,4},{3,5},{4,6},{5,7},{6,0},{7,1},{8,10},{9,11},{10,... | collective-permute-start | bytes 786440 | tf_op jit(solution)/shard_map/ppermute | solution.py:539
  12.7 26.6 %collective-permute-start.4 = (f32[2,8,4096]{2,1,0:T(8,128)S(1)}, f32[2,8,4096]{2,1,0:T(8,128)S(1)}, u32[]{:S(2)}, u32[]{:S(2)}) collective-permute-start(f32[2,8,4096]{2,1,0:T(8,128)S(1)} %get-tuple-element.53), channel_id=1, source_target_pairs={{0,6},{1,7},{2,0},{3,1},{4,2},{5,3},{6,4},{7,5},{8,14},{9,15},{10,... | collective-permute-start | bytes 786440 | tf_op jit(solution)/shard_map/ppermute | solution.py:539
  35.3 7.8 %collective-permute-start.5 = (f32[2,8,4096]{2,1,0:T(8,128)S(1)}, f32[2,8,4096]{2,1,0:T(8,128)S(1)}, u32[]{:S(2)}, u32[]{:S(2)}) collective-permute-start(f32[2,8,4096]{2,1,0:T(8,128)S(1)} %get-tuple-element.54), channel_id=1, source_target_pairs={{0,1},{1,2},{2,3},{3,4},{4,5},{5,6},{6,7},{7,0},{8,9},{9,10},{10,1... | collective-permute-start | bytes 786440 | tf_op jit(solution)/shard_map/ppermute | solution.py:539
  39.3 3.9 %collective-permute-start.6 = (f32[2,8,4096]{2,1,0:T(8,128)S(1)}, f32[2,8,4096]{2,1,0:T(8,128)S(1)}, u32[]{:S(2)}, u32[]{:S(2)}) collective-permute-start(f32[2,8,4096]{2,1,0:T(8,128)S(1)} %get-tuple-element.55), channel_id=1, source_target_pairs={{0,7},{1,0},{2,1},{3,2},{4,3},{5,4},{6,5},{7,6},{8,15},{9,8},{10,9... | collective-permute-start | bytes 786440 | tf_op jit(solution)/shard_map/ppermute | solution.py:539
  50.0 6.7 %collective-permute-start.11 = (f32[16,8,256]{2,1,0:T(8,128)S(1)}, f32[16,8,256]{2,1,0:T(8,128)S(1)}, u32[]{:S(2)}, u32[]{:S(2)}) collective-permute-start(f32[16,8,256]{2,1,0:T(8,128)S(1)} %get-tuple-element.65), channel_id=1, source_target_pairs={{0,1},{1,0},{2,3},{3,2},{4,5},{5,4},{6,7},{7,6},{8,9},{9,8},{10,11... | collective-permute-start | bytes 393224 | tf_op jit(solution)/shard_map/ppermute | solution.py:517
  52.9 20.6 %collective-permute-start.7 = (f32[16,2,8,256]{3,2,1,0:T(8,128)S(1)}, f32[16,2,8,256]{3,2,1,0:T(8,128)S(1)}, u32[]{:S(2)}, u32[]{:S(2)}) collective-permute-start(f32[16,2,8,256]{3,2,1,0:T(8,128)S(1)} %get-tuple-element.58), channel_id=1, source_target_pairs={{0,1},{1,2},{2,3},{3,4},{4,5},{5,6},{6,7},{7,0},{8,9},{9,10},{10,1... | collective-permute-start | bytes 786440 | tf_op jit(solution)/shard_map/ppermute | solution.py:528
  52.9 20.6 %collective-permute-start.8 = (f32[2,16,8,256]{3,2,1,0:T(8,128)S(1)}, f32[2,16,8,256]{3,2,1,0:T(8,128)S(1)}, u32[]{:S(2)}, u32[]{:S(2)}) collective-permute-start(f32[2,16,8,256]{3,2,1,0:T(8,128)S(1)} %get-tuple-element.59), channel_id=1, source_target_pairs={{0,8},{8,16},{16,24},{1,9},{9,17},{17,25},{2,10},{10,18},{18,26},{... | collective-permute-start | bytes 786440 | tf_op jit(solution)/shard_map/ppermute | solution.py:529
  56.7 16.1 %collective-permute-start.12 = (f32[16,8,256]{2,1,0:T(8,128)S(1)}, f32[16,8,256]{2,1,0:T(8,128)S(1)}, u32[]{:S(2)}, u32[]{:S(2)}) collective-permute-start(f32[16,8,256]{2,1,0:T(8,128)S(1)} %add.18), channel_id=1, source_target_pairs={{0,2},{1,3},{2,0},{3,1},{4,6},{5,7},{6,4},{7,5},{8,10},{9,11},{10,... | collective-permute-start | bytes 393224 | tf_op jit(solution)/shard_map/ppermute | solution.py:517
  65.7 7.8 %collective-permute-start.9 = (f32[16,2,8,256]{3,2,1,0:T(8,128)S(1)}, f32[16,2,8,256]{3,2,1,0:T(8,128)S(1)}, u32[]{:S(2)}, u32[]{:S(2)}) collective-permute-start(f32[16,2,8,256]{3,2,1,0:T(8,128)S(1)} %get-tuple-element.60), channel_id=1, source_target_pairs={{1,0},{2,1},{3,2},{4,3},{5,4},{6,5},{7,6},{0,7},{9,8},{10,9},{11,1... | collective-permute-start | bytes 786440 | tf_op jit(solution)/shard_map/ppermute | solution.py:530
  68.1 9.3 %collective-permute-start.10 = (f32[2,16,8,256]{3,2,1,0:T(8,128)S(1)}, f32[2,16,8,256]{3,2,1,0:T(8,128)S(1)}, u32[]{:S(2)}, u32[]{:S(2)}) collective-permute-start(f32[2,16,8,256]{3,2,1,0:T(8,128)S(1)} %get-tuple-element.61), channel_id=1, source_target_pairs={{8,0},{16,8},{24,16},{9,1},{17,9},{25,17},{10,2},{18,10},{26,18},{... | collective-permute-start | bytes 786440 | tf_op jit(solution)/shard_map/ppermute | solution.py:531
  72.8 8.2 %collective-permute-start.13 = (f32[16,8,256]{2,1,0:T(8,128)S(1)}, f32[16,8,256]{2,1,0:T(8,128)S(1)}, u32[]{:S(2)}, u32[]{:S(2)}) collective-permute-start(f32[16,8,256]{2,1,0:T(8,128)S(1)} %add.19), channel_id=1, source_target_pairs={{0,4},{1,5},{2,6},{3,7},{4,0},{5,1},{6,2},{7,3},{8,12},{9,13},{10,... | collective-permute-start | bytes 393224 | tf_op jit(solution)/shard_map/ppermute | solution.py:517
  81.8 4.9 %collective-permute-start.18 = (f32[16,8,256]{2,1,0:T(8,128)S(1)}, f32[16,8,256]{2,1,0:T(8,128)S(1)}, u32[]{:S(2)}, u32[]{:S(2)}) collective-permute-start(f32[16,8,256]{2,1,0:T(8,128)S(1)} %get-tuple-element.81), channel_id=1, source_target_pairs={{0,1},{1,0},{2,3},{3,2},{4,5},{5,4},{6,7},{7,6},{8,9},{9,8},{10,11... | collective-permute-start | bytes 393224 | tf_op jit(solution)/shard_map/ppermute | solution.py:517
  81.9 13.4 %collective-permute-start.14 = (f32[16,2,8,256]{3,2,1,0:T(8,128)S(1)}, f32[16,2,8,256]{3,2,1,0:T(8,128)S(1)}, u32[]{:S(2)}, u32[]{:S(2)}) collective-permute-start(f32[16,2,8,256]{3,2,1,0:T(8,128)S(1)} %get-tuple-element.77), channel_id=1, source_target_pairs={{0,1},{1,2},{2,3},{3,4},{4,5},{5,6},{6,7},{7,0},{8,9},{9,10},{10,1... | collective-permute-start | bytes 786440 | tf_op jit(solution)/shard_map/ppermute | solution.py:528
  82.4 12.9 %collective-permute-start.15 = (f32[2,16,8,256]{3,2,1,0:T(8,128)S(1)}, f32[2,16,8,256]{3,2,1,0:T(8,128)S(1)}, u32[]{:S(2)}, u32[]{:S(2)}) collective-permute-start(f32[2,16,8,256]{3,2,1,0:T(8,128)S(1)} %get-tuple-element.78), channel_id=1, source_target_pairs={{0,8},{8,16},{16,24},{1,9},{9,17},{17,25},{2,10},{10,18},{18,26},{... | collective-permute-start | bytes 786440 | tf_op jit(solution)/shard_map/ppermute | solution.py:529
  86.7 7.8 %collective-permute-start.19 = (f32[16,8,256]{2,1,0:T(8,128)S(1)}, f32[16,8,256]{2,1,0:T(8,128)S(1)}, u32[]{:S(2)}, u32[]{:S(2)}) collective-permute-start(f32[16,8,256]{2,1,0:T(8,128)S(1)} %add.21), channel_id=1, source_target_pairs={{0,2},{1,3},{2,0},{3,1},{4,6},{5,7},{6,4},{7,5},{8,10},{9,11},{10,... | collective-permute-start | bytes 393224 | tf_op jit(solution)/shard_map/ppermute | solution.py:517
  88.3 7.0 %collective-permute-start.16 = (f32[16,2,8,256]{3,2,1,0:T(8,128)S(1)}, f32[16,2,8,256]{3,2,1,0:T(8,128)S(1)}, u32[]{:S(2)}, u32[]{:S(2)}) collective-permute-start(f32[16,2,8,256]{3,2,1,0:T(8,128)S(1)} %get-tuple-element.79), channel_id=1, source_target_pairs={{1,0},{2,1},{3,2},{4,3},{5,4},{6,5},{7,6},{0,7},{9,8},{10,9},{11,1... | collective-permute-start | bytes 786440 | tf_op jit(solution)/shard_map/ppermute | solution.py:530
  89.8 10.9 %collective-permute-start.17 = (f32[2,16,8,256]{3,2,1,0:T(8,128)S(1)}, f32[2,16,8,256]{3,2,1,0:T(8,128)S(1)}, u32[]{:S(2)}, u32[]{:S(2)}) collective-permute-start(f32[2,16,8,256]{3,2,1,0:T(8,128)S(1)} %get-tuple-element.80), channel_id=1, source_target_pairs={{8,0},{16,8},{24,16},{9,1},{17,9},{25,17},{10,2},{18,10},{26,18},{... | collective-permute-start | bytes 786440 | tf_op jit(solution)/shard_map/ppermute | solution.py:531
  94.5 9.9 %collective-permute-start.20 = (f32[16,8,256]{2,1,0:T(8,128)S(1)}, f32[16,8,256]{2,1,0:T(8,128)S(1)}, u32[]{:S(2)}, u32[]{:S(2)}) collective-permute-start(f32[16,8,256]{2,1,0:T(8,128)S(1)} %add.22), channel_id=1, source_target_pairs={{0,4},{1,5},{2,6},{3,7},{4,0},{5,1},{6,2},{7,3},{8,12},{9,13},{10,... | collective-permute-start | bytes 393224 | tf_op jit(solution)/shard_map/ppermute | solution.py:517
  (1 other events, 0.7 us)
